TPU v7x, 32 devices: a whole 2x2x4 slice. The times are simulated.
32 devices in a mesh: vid: 2 (over core), txt: 4 (over y, x), head: 4 (over z).
Axes of the slice: x: 2, y: 2, z: 4, core: 2. Of those that a mesh axis runs over, the one named last changes fastest.
Arguments:
- latents: bfloat16 [32, 128, 768], P('txt', 'vid'), may hold values from -6 to 6
- video_tokens: bfloat16 [32, 1024, 768], P('txt', 'vid'), may hold values from -6 to 6
- caption_tokens: bfloat16 [32, 64, 768], P('vid', 'txt'), may hold values from -6 to 6
- caption_len: int32 [32], P('vid'), may hold values from 5 to 60
- key_mask: int32 [32, 64], P('vid', 'txt'), may hold values 0 or 1
- drop_flags: int32 [32], P('txt'), may hold values 0 or 1
- gain_latent: float32 [768], replicated, may hold values from 0.5 to 1.5
- gain_tokens: float32 [768], replicated, may hold values from 0.5 to 1.5
- gain_mlp: float32 [768], replicated, may hold values from 0.5 to 1.5
- query_weight: bfloat16 [768, 768], P(None, 'head'), may hold values from -0.21875 to 0.21875
- key_matrix: bfloat16 [768, 768], P(None, 'head'), may hold values from -0.21875 to 0.21875
- value_matrix: bfloat16 [768, 768], P(None, 'head'), may hold values from -0.21875 to 0.21875
- out_weight: bfloat16 [768, 768], P('head'), may hold values from -6 to 6
- up_weight: bfloat16 [768, 3072], P(None, 'head'), may hold values from -0.21875 to 0.21875
- down_weight: bfloat16 [3072, 768], P('head'), may hold values from -0.109375 to 0.109375
- cotangent: bfloat16 [32, 128, 768], P('txt', 'vid'), may hold values from -6 to 6
Outputs:
- latents_out: bfloat16 [32, 128, 768], P('txt', 'vid')
- latent_grad: float32 [32, 128, 768], P('txt', 'vid')
- video_grad: float32 [32, 1024, 768], P('txt', 'vid')
- caption_grad: float32 [32, 64, 768], P('vid', 'txt')
- grad_query: float32 [768, 768], P(None, 'head')
- grad_key: float32 [768, 768], P(None, 'head')
- grad_value: float32 [768, 768], P(None, 'head')
- grad_out: float32 [768, 768], P('head')
- grad_up: float32 [768, 3072], P(None, 'head')
- grad_down: float32 [3072, 768], P('head')
- grad_gain_latent: float32 [768], replicated
- grad_gain_tokens: float32 [768], replicated
- grad_gain_mlp: float32 [768], replicated
- kept_count: int32 [], replicated
All inputs are finite; a program needn't handle non-finite values. No bound on the sum of `key_mask` or of `drop_flags` on one device may be relied on, other than what follows from the above.
Results may differ from a plain program's by a relative error of at most 0.012.
Values may be sent and summed in bfloat16 or wider, within the bound.
No kernel may reach another device: no remote copies, remote signals or barrier semaphores. Data moves between devices by JAX's collectives and lax.ppermute only.
A program may use at most 128 MiB of HBM per device.

v0:
```python
import functools
import math

import jax
import jax.numpy as jnp
from jax import lax
from jax.experimental import pallas as pl
from jax.experimental.pallas import tpu as pltpu
from jax.sharding import PartitionSpec as P

D = 768
HEADS = 12


def combined_all(part, axis, combine):
    gathered = jax.tree.map(lambda a: lax.all_gather(a, axis), part)

    def take(source):
        return jax.tree.map(lambda a: lax.dynamic_index_in_dim(a, source, 0, False), gathered)

    return lax.fori_loop(
        1, lax.axis_size(axis), lambda source, state: combine(state, take(source)), take(0)
    )


def layer_norm(values, gain):
    center = values - jnp.mean(values, axis=-1, keepdims=True)
    spread = jnp.mean(center * center, axis=-1, keepdims=True)
    return center * lax.rsqrt(spread + 1e-05) * gain


def norm_back(values, gain, upstream):
    result, pullback = jax.vjp(layer_norm, values, gain)
    return pullback(upstream)


def gelu_exact(values):
    return jax.nn.gelu(values, approximate=False)


def combine_stats(first, second):
    peak = jnp.maximum(first[0], second[0])
    total = first[1] * jnp.exp(first[0] - peak) + second[1] * jnp.exp(second[0] - peak)
    return (peak, total)


def to_blocks(whole, vid_count, txt_count):
    items, rows, width = whole.shape
    split = whole.reshape(txt_count, items // txt_count, vid_count, rows // vid_count, width)
    return split.transpose(2, 0, 1, 3, 4).reshape(
        vid_count * txt_count, items // txt_count, rows // vid_count, width
    )


def from_blocks(blocked, vid_count, txt_count):
    count, items_here, rows_here, width = blocked.shape
    split = blocked.reshape(vid_count, txt_count, items_here, rows_here, width)
    return split.transpose(1, 2, 0, 3, 4).reshape(
        txt_count * items_here, vid_count * rows_here, width
    )


def place_sum(whole, part, start):
    current = lax.dynamic_slice_in_dim(whole, start, part.shape[0], 0)
    return lax.dynamic_update_slice_in_dim(whole, current + part, start, 0)


def place_stats(peak_all, total_all, peak, total, start):
    old_peak = lax.dynamic_slice_in_dim(peak_all, start, peak.shape[0], 0)
    old_total = lax.dynamic_slice_in_dim(total_all, start, peak.shape[0], 0)
    new_peak, new_total = combine_stats((old_peak, old_total), (peak, total))
    peak_all = lax.dynamic_update_slice_in_dim(peak_all, new_peak, start, 0)
    total_all = lax.dynamic_update_slice_in_dim(total_all, new_total, start, 0)
    return (peak_all, total_all)


def take_rows(whole, start, count):
    return lax.dynamic_slice_in_dim(whole, start, count, 0)


def local_general(
    latents,
    video_tokens,
    caption_tokens,
    caption_len,
    key_mask,
    drop_flags,
    gain_latent,
    gain_tokens,
    gain_mlp,
    query_weight,
    key_matrix,
    value_matrix,
    out_weight,
    up_weight,
    down_weight,
    cotangent,
):
    vid_count = lax.axis_size("vid")
    txt_count = lax.axis_size("txt")
    vid_index = lax.axis_index("vid")
    txt_index = lax.axis_index("txt")
    items_here = latents.shape[0]
    cap_items = caption_tokens.shape[0]
    items_total = items_here * txt_count
    head_width = query_weight.shape[1]
    head_size = D // HEADS
    heads_here = head_width // head_size
    scale = 1.0 / math.sqrt(head_size)
    video_here = video_tokens.shape[1]
    cap_here = caption_tokens.shape[1]
    video_start = txt_index * items_here
    cap_start = vid_index * cap_items
    keep = (1 - drop_flags).astype(jnp.float32)
    slots = txt_index * cap_here + jnp.arange(cap_here, dtype=jnp.int32)
    cap_valid = (slots[None, :] < caption_len[:, None]) & (key_mask == 1)
    cap_mask = cap_valid[:, None, None, :]

    def split_heads(values):
        return values.reshape(values.shape[0], values.shape[1], heads_here, head_size)

    lat_float = latents.astype(jnp.float32)
    lat_norm = layer_norm(lat_float, gain_latent).astype(jnp.bfloat16)
    queries = jnp.einsum(
        "bld,de->ble", lat_norm, query_weight, preferred_element_type=jnp.float32
    ).astype(jnp.bfloat16)
    all_queries = from_blocks(
        lax.all_gather(queries[None], ("vid", "txt"), axis=0, tiled=True), vid_count, txt_count
    )
    lat_total = all_queries.shape[1]
    video_queries = take_rows(all_queries, video_start, items_here)
    cap_queries = take_rows(all_queries, cap_start, cap_items)
    video_float = video_tokens.astype(jnp.float32)
    cap_float = caption_tokens.astype(jnp.float32)
    video_normed = layer_norm(video_float, gain_tokens).astype(jnp.bfloat16)
    caption_normed = layer_norm(cap_float, gain_tokens).astype(jnp.bfloat16)
    video_keys = jnp.einsum(
        "flc,co->flo", video_normed, key_matrix, preferred_element_type=jnp.float32
    ).astype(jnp.bfloat16)
    video_values = jnp.einsum(
        "flc,co->flo", video_normed, value_matrix, preferred_element_type=jnp.float32
    ).astype(jnp.bfloat16)
    cap_keys = jnp.einsum(
        "flc,co->flo", caption_normed, key_matrix, preferred_element_type=jnp.float32
    ).astype(jnp.bfloat16)
    cap_values = jnp.einsum(
        "flc,co->flo", caption_normed, value_matrix, preferred_element_type=jnp.float32
    ).astype(jnp.bfloat16)
    video_scores = (
        jnp.einsum(
            "blhe,bkhe->bhlk",
            split_heads(video_queries),
            split_heads(video_keys),
            preferred_element_type=jnp.float32,
        )
        * scale
    )
    cap_scores = (
        jnp.einsum(
            "blhe,bkhe->bhlk",
            split_heads(cap_queries),
            split_heads(cap_keys),
            preferred_element_type=jnp.float32,
        )
        * scale
    )
    cap_scores = jnp.where(cap_mask, cap_scores, -1e30)
    video_peak = jnp.max(video_scores, axis=-1)
    video_total = jnp.sum(jnp.exp(video_scores - video_peak[..., None]), axis=-1)
    cap_peak = jnp.max(cap_scores, axis=-1)
    cap_total = jnp.sum(
        jnp.where(cap_mask, jnp.exp(cap_scores - cap_peak[..., None]), 0.0), axis=-1
    )
    peak_all = jnp.full((items_total, heads_here, lat_total), -1e30, jnp.float32)
    total_all = jnp.zeros((items_total, heads_here, lat_total), jnp.float32)
    peak_all, total_all = place_stats(peak_all, total_all, video_peak, video_total, video_start)
    peak_all, total_all = place_stats(peak_all, total_all, cap_peak, cap_total, cap_start)
    peak, total = combined_all((peak_all, total_all), ("vid", "txt"), combine_stats)
    video_probs = (
        jnp.exp(video_scores - take_rows(peak, video_start, items_here)[..., None])
        / take_rows(total, video_start, items_here)[..., None]
    )
    cap_probs = jnp.where(
        cap_mask,
        jnp.exp(cap_scores - take_rows(peak, cap_start, cap_items)[..., None])
        / take_rows(total, cap_start, cap_items)[..., None],
        0.0,
    )
    video_low = video_probs.astype(jnp.bfloat16)
    cap_low = cap_probs.astype(jnp.bfloat16)
    video_part = jnp.einsum(
        "bhlk,bkhe->blhe", video_low, split_heads(video_values), preferred_element_type=jnp.float32
    ).reshape(items_here, lat_total, head_width)
    cap_part = jnp.einsum(
        "bhlk,bkhe->blhe", cap_low, split_heads(cap_values), preferred_element_type=jnp.float32
    ).reshape(cap_items, lat_total, head_width)
    value_all = jnp.zeros((items_total, lat_total, head_width), jnp.float32)
    value_all = place_sum(place_sum(value_all, video_part, video_start), cap_part, cap_start)
    attended = lax.psum_scatter(
        to_blocks(value_all, vid_count, txt_count), ("vid", "txt"), scatter_dimension=0, tiled=True
    )[0]
    mixed_in = (attended * keep[:, None, None]).astype(jnp.bfloat16)
    branch = lax.psum(
        jnp.einsum("ble,ed->bld", mixed_in, out_weight, preferred_element_type=jnp.float32), "head"
    )
    after_attn = lat_float + branch
    mlp_norm = layer_norm(after_attn, gain_mlp).astype(jnp.bfloat16)
    pre_act = jnp.einsum("bld,df->blf", mlp_norm, up_weight, preferred_element_type=jnp.float32)
    activ = gelu_exact(pre_act).astype(jnp.bfloat16)
    growth = lax.psum(
        jnp.einsum("blf,fd->bld", activ, down_weight, preferred_element_type=jnp.float32).astype(
            jnp.bfloat16
        ),
        "head",
    ).astype(jnp.float32)
    latents_out = (after_attn + growth).astype(jnp.bfloat16)
    grad_down = jnp.einsum("blf,bld->fd", activ, cotangent, preferred_element_type=jnp.float32)
    d_activ = jnp.einsum("bld,fd->blf", cotangent, down_weight, preferred_element_type=jnp.float32)
    d_pre = jax.vjp(gelu_exact, pre_act)[1](d_activ)[0].astype(jnp.bfloat16)
    grad_up = jnp.einsum("bld,blf->df", mlp_norm, d_pre, preferred_element_type=jnp.float32)
    d_mlp_norm = lax.psum(
        jnp.einsum("blf,df->bld", d_pre, up_weight, preferred_element_type=jnp.float32), "head"
    )
    d_after_norm, grad_gain_mlp = norm_back(after_attn, gain_mlp, d_mlp_norm)
    d_after = cotangent.astype(jnp.float32) + d_after_norm
    d_branch = d_after.astype(jnp.bfloat16)
    grad_out = jnp.einsum("ble,bld->ed", mixed_in, d_branch, preferred_element_type=jnp.float32)
    d_att = (
        jnp.einsum("bld,ed->ble", d_branch, out_weight, preferred_element_type=jnp.float32)
        * keep[:, None, None]
    ).astype(jnp.bfloat16)
    all_d_att = from_blocks(
        lax.all_gather(d_att[None], ("vid", "txt"), axis=0, tiled=True), vid_count, txt_count
    )
    video_d_att = split_heads(take_rows(all_d_att, video_start, items_here))
    cap_d_att = split_heads(take_rows(all_d_att, cap_start, cap_items))
    video_dprobs = jnp.einsum(
        "blhe,bkhe->bhlk",
        video_d_att,
        split_heads(video_values),
        preferred_element_type=jnp.float32,
    )
    cap_dprobs = jnp.einsum(
        "blhe,bkhe->bhlk", cap_d_att, split_heads(cap_values), preferred_element_type=jnp.float32
    )
    delta_all = jnp.zeros((items_total, heads_here, lat_total), jnp.float32)
    delta_all = place_sum(delta_all, jnp.sum(video_probs * video_dprobs, axis=-1), video_start)
    delta_all = place_sum(delta_all, jnp.sum(cap_probs * cap_dprobs, axis=-1), cap_start)
    delta = lax.psum(delta_all, ("vid", "txt"))
    video_dscores = (
        video_probs * (video_dprobs - take_rows(delta, video_start, items_here)[..., None])
    ).astype(jnp.bfloat16)
    cap_dscores = (
        cap_probs * (cap_dprobs - take_rows(delta, cap_start, cap_items)[..., None])
    ).astype(jnp.bfloat16)
    video_dq = (
        jnp.einsum(
            "bhlk,bkhe->blhe",
            video_dscores,
            split_heads(video_keys),
            preferred_element_type=jnp.float32,
        )
        * scale
    ).reshape(items_here, lat_total, head_width)
    cap_dq = (
        jnp.einsum(
            "bhlk,bkhe->blhe",
            cap_dscores,
            split_heads(cap_keys),
            preferred_element_type=jnp.float32,
        )
        * scale
    ).reshape(cap_items, lat_total, head_width)
    query_all = jnp.zeros((items_total, lat_total, head_width), jnp.float32)
    query_all = place_sum(place_sum(query_all, video_dq, video_start), cap_dq, cap_start)
    d_queries = lax.psum_scatter(
        to_blocks(query_all, vid_count, txt_count), ("vid", "txt"), scatter_dimension=0, tiled=True
    )[0].astype(jnp.bfloat16)
    video_key_grad = (
        (
            jnp.einsum(
                "bhlk,blhe->bkhe",
                video_dscores,
                split_heads(video_queries),
                preferred_element_type=jnp.float32,
            )
            * scale
        )
        .reshape(items_here, video_here, head_width)
        .astype(jnp.bfloat16)
    )
    video_value_grad = (
        jnp.einsum("bhlk,blhe->bkhe", video_low, video_d_att, preferred_element_type=jnp.float32)
        .reshape(items_here, video_here, head_width)
        .astype(jnp.bfloat16)
    )
    caption_key_grad = (
        (
            jnp.einsum(
                "bhlk,blhe->bkhe",
                cap_dscores,
                split_heads(cap_queries),
                preferred_element_type=jnp.float32,
            )
            * scale
        )
        .reshape(cap_items, cap_here, head_width)
        .astype(jnp.bfloat16)
    )
    caption_value_grad = (
        jnp.einsum("bhlk,blhe->bkhe", cap_low, cap_d_att, preferred_element_type=jnp.float32)
        .reshape(cap_items, cap_here, head_width)
        .astype(jnp.bfloat16)
    )
    grad_query = jnp.einsum("bld,ble->de", lat_norm, d_queries, preferred_element_type=jnp.float32)
    d_lat_norm = lax.psum(
        jnp.einsum("ble,de->bld", d_queries, query_weight, preferred_element_type=jnp.float32),
        "head",
    )
    d_lat_back, grad_gain_latent = norm_back(lat_float, gain_latent, d_lat_norm)
    latent_grad = d_after + d_lat_back
    grad_key = jnp.einsum(
        "zsg,zsv->gv", video_normed, video_key_grad, preferred_element_type=jnp.float32
    ) + jnp.einsum(
        "zsg,zsv->gv", caption_normed, caption_key_grad, preferred_element_type=jnp.float32
    )
    grad_value = jnp.einsum(
        "zsg,zsv->gv", video_normed, video_value_grad, preferred_element_type=jnp.float32
    ) + jnp.einsum(
        "zsg,zsv->gv", caption_normed, caption_value_grad, preferred_element_type=jnp.float32
    )
    video_term = jnp.einsum(
        "ayt,ot->ayo", video_key_grad, key_matrix, preferred_element_type=jnp.float32
    ) + jnp.einsum(
        "ayt,ot->ayo", video_value_grad, value_matrix, preferred_element_type=jnp.float32
    )
    cap_term = jnp.einsum(
        "ayt,ot->ayo", caption_key_grad, key_matrix, preferred_element_type=jnp.float32
    ) + jnp.einsum(
        "ayt,ot->ayo", caption_value_grad, value_matrix, preferred_element_type=jnp.float32
    )
    d_video_norm, d_cap_norm = lax.psum((video_term, cap_term), "head")
    video_grad, video_gain_part = norm_back(video_float, gain_tokens, d_video_norm)
    caption_grad, cap_gain_part = norm_back(cap_float, gain_tokens, d_cap_norm)
    grad_gain_tokens = video_gain_part + cap_gain_part
    kept_here = jnp.sum(keep)
    (
        grad_query,
        grad_key,
        grad_value,
        grad_out,
        grad_up,
        grad_down,
        grad_gain_latent,
        grad_gain_tokens,
        grad_gain_mlp,
        kept_total,
    ) = lax.psum(
        (
            grad_query,
            grad_key,
            grad_value,
            grad_out,
            grad_up,
            grad_down,
            grad_gain_latent,
            grad_gain_tokens,
            grad_gain_mlp,
            kept_here,
        ),
        ("vid", "txt"),
    )
    kept_count = (kept_total / vid_count).astype(jnp.int32)
    return (
        latents_out,
        latent_grad,
        video_grad,
        caption_grad,
        grad_query,
        grad_key,
        grad_value,
        grad_out,
        grad_up,
        grad_down,
        grad_gain_latent,
        grad_gain_tokens,
        grad_gain_mlp,
        kept_count,
    )


def swap_cores(values):
    return lax.ppermute(values, "vid", [(0, 1), (1, 0)])


def head_shift(values, shift, count):
    return lax.ppermute(values, "head", [(i, (i - shift) % count) for i in range(count)])


def take_block(values, index, size, axis=0):
    return lax.dynamic_slice_in_dim(values, index * size, size, axis)


def sum_over_head(part, place, count):
    low = part.astype(jnp.bfloat16)
    total = lax.dynamic_index_in_dim(part, place, 0, False)
    for shift in range(1, count):
        chunk = lax.dynamic_index_in_dim(low, (place - shift) % count, 0, False)
        total = total + head_shift(chunk, shift, count).astype(jnp.float32)
    total = total.astype(jnp.bfloat16)
    result = lax.dynamic_update_index_in_dim(jnp.zeros_like(low), total, place, 0)
    for shift in range(1, count):
        result = lax.dynamic_update_index_in_dim(
            result, head_shift(total, shift, count), (place + shift) % count, 0
        )
    return result


def group_steps(count):
    return [(step, [(i, (i - step) % count) for i in range(count)]) for step in range(1, count)]


def reduce_over_cores(rows, core):
    half = rows.shape[0] // 2
    other = swap_cores(take_block(rows, 1 - core, half))
    return take_block(rows, core, half).astype(F32) + other.astype(F32), other


def reduce_over_group(half, place, count):
    part = half.shape[0] // count
    low = half.astype(BF16)
    total = take_block(half, place, part)
    for step, perm in group_steps(count):
        chunk = take_block(low, (place - step) % count, part)
        total = total + lax.ppermute(chunk, "txt", perm).astype(F32)
    return total.astype(BF16)


def gather_group(total, core, place, count):
    part = total.shape[0]
    half = part * count
    mine = jnp.zeros((half, total.shape[1]), BF16)
    mine = lax.dynamic_update_slice_in_dim(mine, total, place * part, 0)
    for step, perm in group_steps(count):
        mine = lax.dynamic_update_slice_in_dim(
            mine, lax.ppermute(total, "txt", perm), (place + step) % count * part, 0
        )
    whole = jnp.zeros((2 * half, total.shape[1]), BF16)
    whole = lax.dynamic_update_slice_in_dim(whole, mine, core * half, 0)
    return lax.dynamic_update_slice_in_dim(whole, swap_cores(mine), (1 - core) * half, 0)


def caption_perm(step, vid_count, txt_count, cores):
    pairs = []
    for v in range(vid_count):
        for t in range(txt_count):
            block = (t + step) % txt_count
            dest_txt = v * (txt_count // vid_count) + block // cores
            dest_vid = block % cores
            pairs.append((v * txt_count + t, dest_vid * txt_count + dest_txt))
    return pairs


PAIR = 128
F32 = jnp.float32
BF16 = jnp.bfloat16


def dot_nt(a, b):
    return lax.dot_general(a, b, (((1,), (1,)), ((), ())), preferred_element_type=F32)


def dot_nn(a, b):
    return lax.dot_general(a, b, (((1,), (0,)), ((), ())), preferred_element_type=F32)


def dot_tn(a, b):
    return lax.dot_general(a, b, (((0,), (0,)), ((), ())), preferred_element_type=F32)


def square(ref):
    return ref[...].reshape(D, D)


def two_heads(values):
    low = lax.broadcasted_iota(jnp.int32, values.shape, 1) < PAIR // 2
    zero = jnp.zeros_like(values)
    return jnp.concatenate([jnp.where(low, values, zero), jnp.where(low, zero, values)], axis=0)


def from_two_heads(both):
    n = both.shape[1] // 2
    first = lax.broadcasted_iota(jnp.int32, (PAIR, n), 0) < PAIR // 2
    return jnp.where(first, both[:, :n], both[:, n:]).T


def chunk_list(video, cap, size):
    return [(start, size) for start in range(0, video, size)] + [(video, cap)]


def norm_kernel(s_ref, tok_ref, gain_ref, *refs):
    gain = gain_ref[...]
    out_ref = refs[-1]
    for at in range(0, tok_ref.shape[0], 64):
        rows = pl.ds(at, 64)
        out_ref[rows, :] = layer_norm(tok_ref[rows, :].astype(F32), gain).astype(BF16)


def cap_mask(cap_ref):
    mask = cap_ref[:, pl.ds(D, PAIR)]
    return jnp.concatenate([mask, mask], axis=1).astype(F32) > 0.5


def forward_kernel(
    s_ref, tok_ref, cap_ref, gain_ref, lat_ref, gain_lat_ref, wq_ref, wk_ref, wv_ref, *refs
):
    q_ref, k_ref, v_ref, lse_ref, o_ref, s_scr = refs[-6:]
    keys, width = k_ref.shape
    cap = cap_ref.shape[0]
    step = (keys - cap) // 4

    def matrix(ref):
        return ref[...].reshape(width, D)

    latn = layer_norm(lat_ref[...].astype(F32), gain_lat_ref[...]).astype(BF16)
    q_ref[...] = (dot_nt(latn, matrix(wq_ref)).astype(BF16).astype(F32) * 0.125).astype(BF16)

    def project(c, carry):
        rows = pl.ds(pl.multiple_of(c * step, 16), step)
        k_ref[rows, :] = dot_nt(tok_ref[rows, :], matrix(wk_ref)).astype(BF16)
        v_ref[rows, :] = dot_nt(tok_ref[rows, :], matrix(wv_ref)).astype(BF16)
        return carry

    lax.fori_loop(0, 4, project, 0)
    cap_rows = pl.ds(keys - cap, cap)
    cap_norm = layer_norm(cap_ref[:, pl.ds(0, D)].astype(F32), gain_ref[...]).astype(BF16)
    k_ref[cap_rows, :] = dot_nt(cap_norm, matrix(wk_ref)).astype(BF16)
    v_ref[cap_rows, :] = dot_nt(cap_norm, matrix(wv_ref)).astype(BF16)
    chunks = chunk_list(keys - cap, cap, 256)

    def pair(p, carry):
        cols = pl.ds(pl.multiple_of(p * PAIR, PAIR), PAIR)
        q2 = two_heads(q_ref[:, cols])
        peak = None
        for start, size in chunks:
            rows = pl.ds(start, size)
            s = dot_nt(k_ref[rows, cols], q2)
            if start == keys - cap:
                s = jnp.where(cap_mask(cap_ref), s, -1e30)
            s_scr[rows, :] = s
            top = jnp.max(s, axis=0, keepdims=True)
            peak = top if peak is None else jnp.maximum(peak, top)
        total = jnp.zeros_like(peak)
        out = jnp.zeros((PAIR, q2.shape[0]), F32)
        for start, size in chunks:
            rows = pl.ds(start, size)
            e = jnp.exp(s_scr[rows, :] - peak)
            total = total + jnp.sum(e, axis=0, keepdims=True)
            out = out + dot_tn(v_ref[rows, cols], e.astype(BF16))
        o_ref[:, cols] = from_two_heads(out / total)
        lse_ref[pl.ds(p, 1), :] = peak + jnp.log(total)
        return carry

    lax.fori_loop(0, width // PAIR, pair, 0)


def backward_kernel(
    first, s_ref, q_ref, k_ref, v_ref, lse_ref, o_ref, datt_ref, own_ref, other_ref, cap_ref,
    wk_ref, wv_ref, gain_ref, tok_ref, wq_ref, lat_ref, after_ref, gain_lat_ref, *refs
):
    if first:
        own_out, other_out, cap_out, lat_out, sums_ref, gain_out = refs[:6]
    else:
        sums_in, gain_in, ready_ref = refs[:3]
        own_out, other_out, cap_out, lat_out, late_ref = refs[5:10]
        sums_ref, gain_out = refs[-2:]
    dq_ref, dk_ref, dv_ref = refs[6:9] if first else refs[10:13]
    item = pl.program_id(0)
    keys = k_ref.shape[0]
    cap = cap_ref.shape[0]
    chunks = chunk_list(keys - cap, cap, 256)

    def pair(p, carry):
        cols = pl.ds(pl.multiple_of(p * PAIR, PAIR), PAIR)
        q2 = two_heads(q_ref[:, cols])
        d_att = datt_ref[:, cols]
        d2 = two_heads(d_att)
        prod = (d_att.astype(F32) * o_ref[:, cols]).T
        delta = jnp.concatenate(
            [
                jnp.sum(prod[: PAIR // 2], axis=0, keepdims=True),
                jnp.sum(prod[PAIR // 2 :], axis=0, keepdims=True),
            ],
            axis=1,
        )
        pairs_here = D // PAIR // lse_ref.shape[0]
        lse = lse_ref[p // pairs_here, pl.ds(p % pairs_here, 1), :]
        dq = jnp.zeros((PAIR, q2.shape[0]), F32)
        for start, size in chunks:
            rows = pl.ds(start, size)
            k = k_ref[rows, cols]
            s = dot_nt(k, q2)
            d_probs = dot_nt(v_ref[rows, cols], d2)
            if start == keys - cap:
                s = jnp.where(cap_mask(cap_ref), s, -1e30)
            probs = jnp.exp(s - lse)
            d_scores = (probs * (d_probs - delta)).astype(BF16)
            dv_ref[rows, cols] = dot_nn(probs.astype(BF16), d2).astype(BF16)
            dk_ref[rows, cols] = dot_nn(d_scores, q2).astype(BF16)
            dq = dq + dot_tn(k, d_scores)
        dq_ref[:, cols] = (from_two_heads(dq) * 0.125).astype(BF16)
        return carry

    lax.fori_loop(0, D // PAIR, pair, 0)
    gain = gain_ref[...]

    @pl.when(item == 0)
    def _():
        gain_out[...] = jnp.zeros_like(gain_out) if first else gain_in[...]
        sums_ref[...] = jnp.zeros_like(sums_ref) if first else sums_in[...]

    window = pl.ds(pl.multiple_of(s_ref[2], PAIR), sums_ref.shape[1])
    video_rows = pl.ds(0, keys - cap)
    cap_rows = pl.ds(keys - cap, cap)
    cap_norm = layer_norm(cap_ref[:, pl.ds(0, D)].astype(F32), gain).astype(BF16)
    latn = layer_norm(lat_ref[...].astype(F32), gain_lat_ref[...]).astype(BF16)
    sums_ref[0] += dot_tn(dq_ref[:, window], latn)
    for n, ref in ((1, dk_ref), (2, dv_ref)):
        sums_ref[n] += dot_tn(ref[video_rows, window], tok_ref[...]) + dot_tn(
            ref[cap_rows, window], cap_norm
        )

    def norm_back(x, up, gain, row):
        center = x - jnp.mean(x, axis=-1, keepdims=True)
        rate = lax.rsqrt(jnp.mean(center * center, axis=-1, keepdims=True) + 1e-05)
        hat = center * rate
        gain_out[pl.ds(row, 1), :] += jnp.sum(up * hat, axis=0, keepdims=True)
        scaled = up * gain
        first = jnp.mean(scaled, axis=-1, keepdims=True)
        second = jnp.mean(scaled * hat, axis=-1, keepdims=True)
        return rate * (scaled - first - hat * second)

    half = lat_out.shape[0]
    lat_grad = after_ref[...] + norm_back(
        lat_ref[...].astype(F32), dot_nn(dq_ref[...], square(wq_ref)), gain_lat_ref[...], 1
    )
    lat_out[...] = lat_grad[:half]
    other_out[pl.ds(other_ref.shape[0], half), :] = lat_grad[half:].astype(BF16)

    start = 0
    for ref, out, size in ((own_ref, own_out, 256), (other_ref, other_out, 256), (cap_ref, cap_out, cap)):
        def chunk(c, carry, ref=ref, out=out, size=size, start=start):
            rows = pl.ds(pl.multiple_of(c * size, 16), size)
            key_rows = pl.ds(pl.multiple_of(start + c * size, 16), size)
            up = dot_nn(dk_ref[key_rows, :], square(wk_ref)) + dot_nn(
                dv_ref[key_rows, :], square(wv_ref)
            )
            back = norm_back(ref[rows, pl.ds(0, D)].astype(F32), up, gain, 0)
            out[rows, :] = back.astype(out.dtype)
            return carry

        lax.fori_loop(0, ref.shape[0] // size, chunk, 0)
        start += ref.shape[0]

    if first:
        return

    @pl.when(item == pl.num_programs(0) - 1)
    def _():
        width = D // 4
        mine = pl.ds(pl.multiple_of(s_ref[3], PAIR // 2), width)
        for n in range(3):
            late_ref[pl.ds(n * width, width), :] = sums_ref[n, mine, :].astype(BF16)
        ready = ready_ref.shape[0]
        late_ref[pl.ds(3 * width, ready), :] = ready_ref[...]
        gains = jnp.concatenate([gain_out[...], jnp.zeros((8, D), F32)], axis=0)
        late_ref[pl.ds(3 * width + ready, 16), :] = gains.astype(BF16)
        spare = late_ref.shape[0] - 3 * width - ready - 16
        late_ref[pl.ds(3 * width + ready + 16, spare), :] = jnp.zeros((spare, D), BF16)


def place_kernel(s_ref, video_in, lat_in, video_part, lat_part, video_ref, lat_ref):
    video_ref[...] = video_part[...].astype(F32)

    @pl.when(pl.program_id(1) == 0)
    def _():
        lat_ref[...] = lat_part[...].astype(F32)


def local(
    latents,
    video_tokens,
    caption_tokens,
    caption_len,
    key_mask,
    drop_flags,
    gain_latent,
    gain_tokens,
    gain_mlp,
    query_weight,
    key_matrix,
    value_matrix,
    out_weight,
    up_weight,
    down_weight,
    cotangent,
):
    txt_count = lax.axis_size("txt")
    head_count = lax.axis_size("head")
    core = lax.axis_index("vid")
    place_index = lax.axis_index("txt")
    z = lax.axis_index("head")
    items_here = latents.shape[0]
    own = items_here // 2
    lat_half = latents.shape[1]
    lat_rows = 2 * lat_half
    video_here = video_tokens.shape[1]
    cap_here = caption_tokens.shape[1]
    cap_rows = cap_here * txt_count
    keys_here = 2 * video_here + cap_rows
    head_width = query_weight.shape[1]

    def dot(spec, a, b):
        return jnp.einsum(spec, a, b, preferred_element_type=F32)

    packed = jnp.stack([query_weight.T, key_matrix.T, value_matrix.T, out_weight])
    half = take_block(packed, core, 2)
    up1 = lax.ppermute(half, "head", [(0, 1), (1, 2), (2, 3)])
    down1 = lax.ppermute(half, "head", [(1, 0), (2, 1), (3, 2)])
    near_at = z // 2
    zero = jnp.int32(0)
    own_at = z % 2
    part_shape = (2, 2, 2, head_width, D)

    def place_chunk(whole, chunk, at_core, at_chunk):
        chunk = chunk.reshape((-1, 1) + chunk.shape[-3:])
        return lax.dynamic_update_slice(whole, chunk, (at_core, at_chunk, zero, zero, zero))

    video_other = swap_cores(take_block(video_tokens, 1 - core, own))
    both = jnp.concatenate([latents, cotangent], axis=1)
    both_own = take_block(both, core, own)
    both_other = swap_cores(take_block(both, 1 - core, own))
    lat = jnp.concatenate([both_own[:, :lat_half], both_other[:, :lat_half]], axis=1)
    cot = jnp.concatenate([both_own[:, lat_half:], both_other[:, lat_half:]], axis=1)
    drop_own = take_block(drop_flags, core, own)
    keep = (1 - drop_own).astype(F32)
    window = z * head_width // PAIR * PAIR
    inside = z * head_width - window
    scalars = jnp.stack([core, near_at, window, inside])
    scalars_far = jnp.stack([core, 1 - near_at, window, inside])

    place_slots = place_index * cap_here + jnp.arange(cap_here, dtype=jnp.int32)
    cap_valid = (place_slots[None, :] < caption_len[:, None]) & (key_mask == 1)
    flags = jnp.broadcast_to(cap_valid.astype(BF16)[:, :, None], cap_valid.shape + (PAIR,))
    cap_message = jnp.concatenate([caption_tokens, flags], axis=2)
    cap_parts = []
    for step in range(txt_count):
        block = take_block(cap_message, (place_index + step) % txt_count, own)
        cap_parts.append(
            lax.ppermute(block, ("vid", "txt"), caption_perm(step, 2, txt_count, 2))
        )
    def item_spec(rows, width=D, first=0):
        return pl.BlockSpec((None, rows, width), lambda i, s: (first + i, 0, 0))

    def own_spec(rows, first=0):
        return pl.BlockSpec((None, rows, D), lambda i, s: (s[0] * own + first + i, 0, 0))

    def whole_spec(*shape):
        return pl.BlockSpec(shape, lambda i, s: (0,) * len(shape))

    def weight_spec(m):
        return pl.BlockSpec(
            (2, None, 2, None, head_width, D),
            lambda i, s: (0, m // 2, 0, m % 2, 0, 0),
            pipeline_mode=pl.Buffered(1),
        )

    def part_spec(m):
        return pl.BlockSpec(
            (None, 2, None, head_width, D),
            lambda i, s: (m // 2, 0, m % 2, 0, 0),
            pipeline_mode=pl.Buffered(1),
        )

    def half_spec(rows):
        return pl.BlockSpec((None, rows, 2 * head_width), lambda i, s: (i, 0, s[1]))

    row_spec = pl.BlockSpec((1, D), lambda i, s: (0, 0))

    def call(kernel, name, ins, outs, operands, micros, scratch=(), aliases={}, scalars=scalars, grid=own):
        return pl.pallas_call(
            kernel,
            name=name,
            grid_spec=pltpu.PrefetchScalarGridSpec(
                num_scalar_prefetch=1,
                grid=(grid,),
                in_specs=ins,
                out_specs=[spec for spec, _, _ in outs],
                scratch_shapes=list(scratch),
            ),
            out_shape=[jax.ShapeDtypeStruct(shape, dtype) for _, shape, dtype in outs],
            input_output_aliases=aliases,
            cost_estimate=pl.CostEstimate(
                flops=micros * 1100 * 10**6, transcendentals=0, bytes_accessed=micros * 10**6
            ),
            compiler_params=pltpu.CompilerParams(vmem_limit_bytes=56 << 20),
        )(scalars, *operands)

    def item_out(rows, dtype, width=D):
        return (item_spec(rows, width), (own, rows, width), dtype)

    gain_lat_row = gain_latent[None]
    gain_tok_row = gain_tokens[None]
    gain_mlp_row = gain_mlp[None]
    def token_norm(part, spec, tokens, before=()):
        return call(
            norm_kernel,
            "token_norm",
            [spec, row_spec] + [pl.BlockSpec(memory_space=pl.ANY)] * len(before),
            [
                (
                    pl.BlockSpec((None, video_here, D), lambda i, s: (i, part, 0)),
                    (own, 2 * video_here, D),
                    BF16,
                )
            ],
            (tokens, gain_tok_row) + tuple(before),
            5,
            aliases={3: 0} if before else {},
        )

    tok_norm = token_norm(0, own_spec(video_here), video_tokens)
    (tok_norm,) = token_norm(1, item_spec(video_here), video_other, tok_norm)
    tok_norm, up1, down1, cap_parts = lax.optimization_barrier((tok_norm, up1, down1, cap_parts))
    cap = jnp.concatenate(cap_parts, axis=1)
    partner = jnp.where(z % 2 == 1, up1, down1)
    near = jnp.zeros(part_shape, BF16)
    near = place_chunk(near, packed.reshape((2, 2) + packed.shape[1:]), zero, own_at)
    near = place_chunk(near, partner, core, 1 - own_at)
    near = place_chunk(near, swap_cores(partner), 1 - core, 1 - own_at)

    half_then, _ = lax.optimization_barrier((half, up1))
    up2 = lax.ppermute(up1, "head", [(1, 2), (2, 3)])
    down2 = lax.ppermute(down1, "head", [(1, 0), (2, 1)])
    up3 = lax.ppermute(half_then, "head", [(0, 3)])
    down3 = lax.ppermute(half_then, "head", [(3, 0)])

    def forward(part, scalars, before=()):
        return call(
            forward_kernel,
            "attention_forward",
            [item_spec(2 * video_here), item_spec(cap_rows, D + PAIR), row_spec]
            + [item_spec(lat_rows), row_spec]
            + [part_spec(m) for m in range(3)]
            + [pl.BlockSpec(memory_space=pl.ANY)] * len(before),
            [
                (half_spec(lat_rows), (own, lat_rows, D), BF16),
                (half_spec(keys_here), (own, keys_here, D), BF16),
                (half_spec(keys_here), (own, keys_here, D), BF16),
                (
                    pl.BlockSpec((None, None, 8, 2 * lat_rows), lambda i, s: (i, s[1], 0, 0)),
                    (own, 2, 8, 2 * lat_rows),
                    F32,
                ),
                (half_spec(lat_rows), (own, lat_rows, D), F32),
            ],
            (tok_norm, cap, gain_tok_row, lat, gain_lat_row, part, part, part) + tuple(before),
            23,
            [pltpu.VMEM((keys_here, 2 * lat_rows), F32)],
            {9 + n: n for n in range(len(before))},
            scalars,
        )

    before = forward(near, scalars)
    before, up2, down2, up3, down3 = lax.optimization_barrier((before, up2, down2, up3, down3))

    def by_place(*choices):
        low = jnp.where(z == 0, choices[0], choices[1])
        return jnp.where(z < 2, low, jnp.where(z == 2, choices[2], choices[3]))

    far_mine = jnp.stack([by_place(down2, down1, up2, up3), by_place(down3, down2, up1, up2)])
    far = jnp.zeros(part_shape, BF16)
    far = lax.dynamic_update_index_in_dim(far, far_mine, core, 0)
    far = lax.dynamic_update_index_in_dim(far, swap_cores(far_mine), 1 - core, 0)
    def both_halves(near, far):
        whole = jnp.zeros((2,) + near.shape, BF16)
        whole = lax.dynamic_update_index_in_dim(whole, near, near_at, 0)
        return lax.dynamic_update_index_in_dim(whole, far, 1 - near_at, 0)

    queries, keys, values, lse, attended = forward(far, scalars_far, before)
    w_out = both_halves(near[1, :, 1], far[1, :, 1]).reshape(D, D)
    lat_float = lat.astype(F32)
    mixed_in = (attended * keep[:, None, None]).astype(BF16)
    after_attn = lat_float + dot("ble,ed->bld", mixed_in, w_out)
    mlp_norm = layer_norm(after_attn, gain_mlp).astype(BF16)

    pre_act = dot("bld,df->blf", mlp_norm, up_weight)
    activ, gelu_pull = jax.vjp(gelu_exact, pre_act)
    activ = activ.astype(BF16)
    d_pre = gelu_pull(dot("bld,fd->blf", cot, down_weight))[0].astype(BF16)
    d_mlp_part = dot("blf,df->bld", d_pre, up_weight)
    d_mlp_part, activ, d_pre = lax.optimization_barrier((d_mlp_part, activ, d_pre))
    d_mlp_norm = sum_over_head(d_mlp_part, z, head_count)
    grad_down = dot("blf,bld->fd", activ, cot).astype(BF16)
    grad_up = dot("bld,blf->df", mlp_norm, d_pre).astype(BF16)
    near, far, _ = lax.optimization_barrier((near, far, d_mlp_part))
    weights = both_halves(near, far)
    early = jnp.where(core == 0, grad_up, grad_down).astype(F32)
    early = early + swap_cores(jnp.where(core == 0, grad_down, grad_up)).astype(F32)
    activ, d_mlp_norm, early, weights = lax.optimization_barrier(
        (activ, d_mlp_norm, early.astype(BF16), weights)
    )
    early = lax.psum(early, "txt")
    growth = lax.psum(dot("blf,fd->bld", activ, down_weight).astype(BF16), "head")

    d_after_norm, gain_mlp_part = norm_back_rows(after_attn, gain_mlp, d_mlp_norm.astype(F32))
    d_after = cot.astype(F32) + d_after_norm
    d_branch = d_after.astype(BF16)
    d_att = (dot("bld,ed->ble", d_branch, w_out) * keep[:, None, None]).astype(BF16)
    mixed_mine = lax.dynamic_slice_in_dim(mixed_in, z * head_width, head_width, 2)
    grad_out = dot("ble,bld->ed", mixed_mine, d_branch)
    ready = jnp.concatenate(
        [
            grad_out,
            jnp.sum(gain_mlp_part, axis=0)[None],
            jnp.full((1, D), jnp.sum(keep)),
            jnp.zeros((14, D), F32),
        ]
    ).astype(BF16)
    late_size = 4 * head_width + 32
    late_size = late_size + -late_size % (32 * txt_count)
    some = own // 2

    def backward(at, before=(), operands=()):
        first = at == 0
        sums_shape = (3, 2 * PAIR, D)
        outs = [
            (own_spec(video_here, at), video_tokens.shape, F32),
            (item_spec(video_here + lat_half), (some, video_here + lat_half, D), BF16),
            (item_spec(cap_rows), (some, cap_rows, D), BF16),
            (own_spec(lat_half, at), latents.shape, F32),
        ]
        scratch = [
            pltpu.VMEM((lat_rows, D), BF16),
            pltpu.VMEM((keys_here, D), BF16),
            pltpu.VMEM((keys_here, D), BF16),
        ]
        if first:
            ins = []
            outs = outs + [(whole_spec(*sums_shape), sums_shape, F32), (whole_spec(8, D), (8, D), F32)]
        else:
            ins = [whole_spec(*sums_shape), whole_spec(8, D), whole_spec(*ready.shape)]
            ins = ins + [pl.BlockSpec(memory_space=pl.ANY)] * len(before)
            outs = outs + [(whole_spec(late_size, D), (late_size, D), BF16)]
            scratch = scratch + [pltpu.VMEM(sums_shape, F32), pltpu.VMEM((8, D), F32)]
        return call(
            functools.partial(backward_kernel, first),
            "attention_backward",
            [
                item_spec(lat_rows, D, at),
                item_spec(keys_here, D, at),
                item_spec(keys_here, D, at),
                pl.BlockSpec((None, 2, 8, 2 * lat_rows), lambda i, s: (at + i, 0, 0, 0)),
                item_spec(lat_rows, D, at),
                item_spec(lat_rows, D, at),
                own_spec(video_here, at),
                item_spec(video_here, D, at),
                item_spec(cap_rows, D + PAIR, at),
                weight_spec(1),
                weight_spec(2),
                row_spec,
                item_spec(2 * video_here, D, at),
                weight_spec(0),
                item_spec(lat_rows, D, at),
                item_spec(lat_rows, D, at),
                row_spec,
            ]
            + ins,
            outs,
            (
                queries, keys, values, lse, attended, d_att, video_tokens, video_other, cap,
                weights, weights, gain_tok_row, tok_norm, weights, lat, d_after,
                gain_lat_row,
            )
            + tuple(operands)
            + tuple(before),
            3,
            scratch,
            {} if first else {21: 0, 22: 3},
            grid=some,
        )

    def place(at, video_grad, latent_grad, part):
        piece = video_here // 2
        return pl.pallas_call(
            place_kernel,
            name="place_rows",
            grid_spec=pltpu.PrefetchScalarGridSpec(
                num_scalar_prefetch=1,
                grid=(some, 2),
                in_specs=[
                    pl.BlockSpec(memory_space=pl.ANY),
                    pl.BlockSpec(memory_space=pl.ANY),
                    pl.BlockSpec((None, piece, D), lambda i, r, s: (i, r, 0)),
                    pl.BlockSpec((None, lat_half, D), lambda i, r, s: (i, video_here // lat_half, 0)),
                ],
                out_specs=[
                    pl.BlockSpec((None, piece, D), lambda i, r, s: ((1 - s[0]) * own + at + i, r, 0)),
                    pl.BlockSpec(
                        (None, lat_half, D), lambda i, r, s: ((1 - s[0]) * own + at + i, 0, 0)
                    ),
                ],
            ),
            out_shape=[
                jax.ShapeDtypeStruct(video_tokens.shape, F32),
                jax.ShapeDtypeStruct(latents.shape, F32),
            ],
            input_output_aliases={1: 0, 2: 1},
            cost_estimate=pl.CostEstimate(
                flops=3 * 10**9, transcendentals=0, bytes_accessed=5 * 10**6
            ),
        )(scalars, video_grad, latent_grad, part, part)

    d_att, ready = lax.optimization_barrier((d_att, ready))
    video_grad, back_a, cap_a, latent_grad, sums, gain_sums = backward(0)
    here_a = swap_cores(back_a)
    early, sums = lax.optimization_barrier((early, sums))
    video_grad, back_b, cap_b, latent_grad, late = backward(
        some, (video_grad, latent_grad), (sums, gain_sums, ready)
    )
    growth, _ = lax.optimization_barrier((growth, late))
    late_half, late_swapped = reduce_over_cores(late, core)
    here_b = swap_cores(back_b)
    cap_back = jnp.concatenate([cap_a, cap_b])
    cap_back, _ = lax.optimization_barrier((cap_back, late_swapped))
    late_total = reduce_over_group(late_half, place_index, txt_count)
    here_a, _ = lax.optimization_barrier((here_a, late_half))
    early_other = swap_cores(early)
    video_grad, latent_grad = place(0, video_grad, latent_grad, here_a)
    here_b, early, early_other, _ = lax.optimization_barrier((here_b, early, early_other, late_total))
    late = gather_group(late_total, core, place_index, txt_count).astype(F32)
    video_grad, latent_grad = place(some, video_grad, latent_grad, here_b)
    out_mine = (after_attn + growth.astype(F32)).astype(BF16)
    caption_grad = jnp.zeros((txt_count, own, cap_here, D), F32)
    for step in range(txt_count):
        perm = [(b, a) for a, b in caption_perm(step, 2, txt_count, 2)]
        part = lax.ppermute(
            cap_back[:, step * cap_here : (step + 1) * cap_here], ("vid", "txt"), perm
        )
        caption_grad = lax.dynamic_update_index_in_dim(
            caption_grad, part.astype(F32), (place_index + step) % txt_count, 0
        )
    caption_grad = caption_grad.reshape(caption_tokens.shape)

    gains = late[4 * head_width :]

    def give_back(values):
        other = swap_cores(values[:, lat_half:].astype(BF16)).astype(values.dtype)
        whole = jnp.zeros((items_here, lat_half, D), values.dtype)
        whole = lax.dynamic_update_slice_in_dim(whole, values[:, :lat_half], core * own, 0)
        return lax.dynamic_update_slice_in_dim(whole, other, (1 - core) * own, 0)

    latents_out = give_back(out_mine)
    kept_count = gains[1, 0].astype(jnp.int32)
    return (
        latents_out,
        latent_grad,
        video_grad,
        caption_grad,
        late[:head_width].T,
        late[head_width : 2 * head_width].T,
        late[2 * head_width : 3 * head_width].T,
        late[3 * head_width : 4 * head_width],
        jnp.where(core == 0, early, early_other).astype(F32),
        jnp.where(core == 0, early_other, early).astype(F32),
        gains[17],
        gains[16],
        gains[0],
        kept_count,
    )


def norm_back_rows(values, gain, upstream):
    mean = jnp.mean(values, axis=-1, keepdims=True)
    center = values - mean
    rate = lax.rsqrt(jnp.mean(center * center, axis=-1, keepdims=True) + 1e-05)
    hat = center * rate
    scaled = upstream * gain
    first = jnp.mean(scaled, axis=-1, keepdims=True)
    second = jnp.mean(scaled * hat, axis=-1, keepdims=True)
    return rate * (scaled - first - hat * second), jnp.sum(upstream * hat, axis=-2)


def fits(mesh):
    shape = mesh.shape
    return shape["vid"] == 2 and shape["txt"] == 4 and shape["head"] == 4


def solution(mesh):
    in_specs = (
        P("txt", "vid", None),
        P("txt", "vid", None),
        P("vid", "txt", None),
        P("vid"),
        P("vid", "txt"),
        P("txt"),
        P(),
        P(),
        P(),
        P(None, "head"),
        P(None, "head"),
        P(None, "head"),
        P("head", None),
        P(None, "head"),
        P("head", None),
        P("txt", "vid", None),
    )
    out_specs = (
        P("txt", "vid", None),
        P("txt", "vid", None),
        P("txt", "vid", None),
        P("vid", "txt", None),
        P(None, "head"),
        P(None, "head"),
        P(None, "head"),
        P("head", None),
        P(None, "head"),
        P("head", None),
        P(),
        P(),
        P(),
        P(),
    )
    return jax.shard_map(local if fits(mesh) else local_general, mesh=mesh, in_specs=in_specs, out_specs=out_specs, check_vma=False)
```

profile of v0, /device:TPU:0, one launch (start us, length us, event | category | flops | bytes accessed | tf_op | source)
XLA Modules:
  0.0 357.1 jit_solution(3185376928082786068)
XLA Ops:
  7.3 3.9 %constant_dynamic-slice_fusion.6 = bf16[4,512,768]{2,1,0:T(8,128)(2,1)} fusion(bf16[8,512,768]{2,1,0:T(8,128)(2,1)} %own_ref.3, s32[]{:T(128)S(6)} %select_n.263), kind=kLoop, calls=%fused_computation.125 | loop fusion | bytes 6291460 | tf_op jit(solution)/shard_map/dynamic_slice | solution.py:401
  12.8 4.6 %collective-permute-start.2 = (bf16[2,192,768]{2,1,0:T(8,128)(2,1)}, bf16[2,192,768]{2,1,0:T(8,128)(2,1)S(1)}, u32[]{:S(2)}, u32[]{:S(2)}) collective-permute-start(bf16[2,192,768]{2,1,0:T(8,128)(2,1)} %constant_dynamic-slice_fusion.5), channel_id=1, source_target_pairs={{0,1},{1,2},{2,3},{4,5},{5,6},{6,7},{8,9},{9,10},{10,11},{12,13},{... | collective-permute-start | bytes 1769480 | tf_op jit(solution)/shard_map/ppermute | solution.py:728
  28.3 5.9 %token_norm.2.refs_0_ = bf16[4,1024,768]{2,1,0:T(8,128)(2,1)} custom-call(s32[4]{0:T(128)} %add_add_fusion.1.s_ref, bf16[8,512,768]{2,1,0:T(8,128)(2,1)} %own_ref.3, f32[1,768]{1,0:T(1,128)} %broadcast_in_dim.115.gain_ref), custom_call_target="tpu_custom_call" | custom-call | flops 5500000256 | bytes 5000000 | tf_op jit(solution)/shard_map/token_norm/pallas_call | solution.py:791
  34.2 3.5 collective-permute-start.5
  39.7 4.7 %collective-permute-start.7 = (bf16[4,16,896]{2,1,0:T(8,128)(2,1)S(1)}, bf16[4,16,896]{2,1,0:T(8,128)(2,1)S(1)}, u32[]{:S(2)}, u32[]{:S(2)}) collective-permute-start(bf16[4,16,896]{2,1,0:T(8,128)(2,1)S(1)} %get-tuple-element.175), channel_id=1, source_target_pairs={{0,20},{4,0},{8,16},{12,4},{16,28},{20,8},{24,24},{28,12},{1,21},{... | collective-permute-start | bytes 344072 | tf_op jit(solution)/shard_map/ppermute | solution.py:760
  44.4 5.8 %token_norm.3.tok_ref = bf16[4,1024,768]{2,1,0:T(8,128)(2,1)} custom-call(s32[4]{0:T(128)} %add_add_fusion.1.s_ref, bf16[4,512,768]{2,1,0:T(8,128)(2,1)} %collective-permute-done.1.tok_ref.other_ref, f32[1,768]{1,0:T(1,128)} %broadcast_in_dim.115.gain_ref, bf16[4,1024,768]{2,1,0:T(8,128)(2,1)} %token_norm.2.refs_0_), custom_call_target="tpu_custom_call", output_to_operand_aliasing={{}: (3, {})} | custom-call | flops 5500000256 | bytes 5000000 | tf_op jit(solution)/shard_map/token_norm/pallas_call | solution.py:791
  54.5 6.1 %collective-permute-start.11 = (bf16[2,192,768]{2,1,0:T(8,128)(2,1)}, bf16[2,192,768]{2,1,0:T(8,128)(2,1)S(1)}, u32[]{:S(2)}, u32[]{:S(2)}) collective-permute-start(bf16[2,192,768]{2,1,0:T(8,128)(2,1)} %constant_dynamic-slice_fusion.5), channel_id=1, source_target_pairs={{0,3},{4,7},{8,11},{12,15},{16,19},{20,23},{24,27},{28,31}} | collective-permute-start | bytes 1769480 | tf_op jit(solution)/shard_map/ppermute | solution.py:845
  65.2 29.1 %attention_forward.2 = (bf16[4,128,768]{2,1,0:T(8,128)(2,1)}, bf16[4,1088,768]{2,1,0:T(8,128)(2,1)}, bf16[4,1088,768]{2,1,0:T(8,128)(2,1)}, f32[4,2,8,256]{3,2,1,0:T(8,128)}, f32[4,128,768]{2,1,0:T(8,128)}) custom-call(s32[4]{0:T(128)} %add_add_fusion.1.s_ref, bf16[4,1024,768]{2,1,0:T(8,128)(2,1)} %token_norm.3.tok_ref, bf16[4,64,896]{2,1,0:T(8,128)(2,1)} %copy-done.10, ...), custom_call_target="tpu_custom_call" | custom-call | flops 25300000768 | bytes 23000000 | tf_op jit(solution)/shard_map/attention_forward/pallas_call | solution.py:791
  105.9 29.1 %attention_forward.3 = (bf16[4,128,768]{2,1,0:T(8,128)(2,1)}, bf16[4,1088,768]{2,1,0:T(8,128)(2,1)}, bf16[4,1088,768]{2,1,0:T(8,128)(2,1)}, f32[4,2,8,256]{3,2,1,0:T(8,128)}, f32[4,128,768]{2,1,0:T(8,128)}) custom-call(s32[4]{0:T(128)} %add_add_fusion.s_ref, ...), custom_call_target="tpu_custom_call", output_to_operand_aliasing={{0}: (9, {}), {1}: (10, {}), {2}: (11, {}), {3}: (12, {}), ... | custom-call | flops 25300000768 | bytes 23000000 | tf_op jit(solution)/shard_map/attention_forward/pallas_call | solution.py:791
  141.1 3.9 %multiply_convert_fusion.1 = (bf16[4,128,768]{2,1,0:T(8,128)(2,1)S(1)}, f32[4,128,768]{2,1,0:T(8,128)S(1)}, f32[4,128,768]{2,1,0:T(8,128)S(1)}) fusion(bf16[768,768]{1,0:T(8,128)(2,1)S(1)} %copy-done, f32[4,128,768]{2,1,0:T(8,128)S(1)} %get-tuple-element.153, f32[768]{0:T(1024)S(1)} %copy-done.34, f32[4,128]{1,0:T(4,128)S(1)} %add_rsqrt_fusion, ...), kind=kOutput, calls=%fused_computation.19 | convolution fusion | flops 631111680 | bytes 6691840 | tf_op jit(solution)/shard_map/bld,df->blf/dot_general | solution.py:724
  147.2 4.8 %collective-permute-start.15 = (bf16[128,768]{1,0:T(8,128)(2,1)S(1)}, bf16[128,768]{1,0:T(8,128)(2,1)S(1)}, u32[]{:S(2)}, u32[]{:S(2)}) collective-permute-start(bf16[128,768]{1,0:T(8,128)(2,1)S(1)} %get-tuple-element.169), channel_id=1, source_target_pairs={{0,2},{1,3},{2,0},{3,1},{4,6},{5,7},{6,4},{7,5},{8,10},{9,11},{10,... | collective-permute-start | bytes 589832 | tf_op jit(solution)/shard_map/ppermute | solution.py:397
  158.3 7.2 %collective-permute-done.15 = bf16[128,768]{1,0:T(8,128)(2,1)S(1)} collective-permute-done((bf16[128,768]{1,0:T(8,128)(2,1)S(1)}, bf16[128,768]{1,0:T(8,128)(2,1)S(1)}, u32[]{:S(2)}, u32[]{:S(2)}) %collective-permute-start.15) | collective-permute-done | bytes 196640 | tf_op jit(solution)/shard_map/ppermute | solution.py:397
  165.7 3.5 collective-permute-start.17
  175.6 13.8 %collective-permute-done.18 = bf16[128,768]{1,0:T(8,128)(2,1)S(1)} collective-permute-done((bf16[128,768]{1,0:T(8,128)(2,1)S(1)}, bf16[128,768]{1,0:T(8,128)(2,1)S(1)}, u32[]{:S(2)}, u32[]{:S(2)}) %collective-permute-start.18) | collective-permute-done | bytes 196640 | tf_op jit(solution)/shard_map/ppermute | solution.py:397
  197.3 3.5 multiply_convert_fusion.datt_ref
  201.7 36.4 %attention_backward.2 = (f32[8,512,768]{2,1,0:T(8,128)}, bf16[2,576,768]{2,1,0:T(8,128)(2,1)}, bf16[2,64,768]{2,1,0:T(8,128)(2,1)}, f32[8,64,768]{2,1,0:T(8,128)...) custom-call(s32[4]{0:T(128)} %add_add_fusion.1.s_ref, bf16[4,128,768]{2,1,0:T(8,128)(2,1)} %get-tuple-element.104.q_ref, ...), custom_call_target="tpu_custom_call" | custom-call | flops 3300000000 | bytes 3000000 | tf_op jit(solution)/shard_map/attention_backward/pallas_call | solution.py:791
  238.1 5.5 %all-reduce.5.cloned.1.call-done = bf16[768,768]{1,0:T(8,128)(2,1)} async-done(((bf16[768,768]{1,0:T(8,128)(2,1)}), bf16[768,768]{1,0:T(8,128)(2,1)}) %all-reduce.5.cloned.1.call-update) | async-done | bytes 1179664 | tf_op jit(solution)/shard_map/psum | solution.py:913
  243.6 37.5 %attention_backward.3 = (f32[8,512,768]{2,1,0:T(8,128)}, bf16[2,576,768]{2,1,0:T(8,128)(2,1)}, bf16[2,64,768]{2,1,0:T(8,128)(2,1)}, f32[8,64,768]{2,1,0:T(8,128)}, bf16[896,768]{1,0:T(8,128)(2,1)}) custom-call(s32[4]{0:T(128)} %add_add_fusion.1.s_ref, bf16[4,128,768]{2,1,0:T(8,128)(2,1)} %get-tuple-element.104.q_ref, ...), custom_call_target="tpu_custom_call", output_to_operand_aliasing={{0}: (21, {}), {3}: (22, {})} | custom-call | flops 3300000000 | bytes 3000000 | tf_op jit(solution)/shard_map/attention_backward/pallas_call | solution.py:791
  281.1 8.7 %all-reduce.3.cloned.1.call-done = bf16[4,128,768]{2,1,0:T(8,128)(2,1)} async-done(((bf16[4,128,768]{2,1,0:T(8,128)(2,1)}), bf16[4,128,768]{2,1,0:T(8,128)(2,1)}) %all-reduce.3.cloned.1.call-update) | async-done | bytes 786448 | tf_op jit(solution)/shard_map/psum | solution.py:914
  303.5 4.9 %place_rows.2 = (f32[8,512,768]{2,1,0:T(8,128)}, f32[8,64,768]{2,1,0:T(8,128)}) custom-call(s32[4]{0:T(128)} %add_add_fusion.1.s_ref, f32[8,512,768]{2,1,0:T(8,128)} %get-tuple-element.120.video_in, f32[8,64,768]{2,1,0:T(8,128)} %get-tuple-element.121.lat_in, ...), custom_call_target="tpu_custom_call", output_to_operand_aliasing={{0}: (1, {}), {1}: (2, {})} | custom-call | flops 3000000000 | bytes 5000000 | tf_op jit(solution)/shard_map/place_rows/pallas_call | solution.py:995
  318.1 3.2 collective-permute-done.33
  324.3 3.6 %collective-permute-done.35 = bf16[112,768]{1,0:T(8,128)(2,1)S(1)} collective-permute-done((bf16[112,768]{1,0:T(8,128)(2,1)S(1)}, bf16[112,768]{1,0:T(8,128)(2,1)S(1)}, u32[]{:S(2)}, u32[]{:S(2)}) %collective-permute-start.35) | collective-permute-done | bytes 172064 | tf_op jit(solution)/shard_map/ppermute | solution.py:446
  339.5 4.4 %select_convert_fusion = (f32[768,768]{1,0:T(8,128)}, f32[768,768]{1,0:T(8,128)}) fusion(bf16[768,768]{1,0:T(8,128)(2,1)} %collective-permute-done.25, bf16[768,768]{1,0:T(8,128)(2,1)S(1)} %copy-done.18, pred[]{:T(512)S(6)} %eq.51), kind=kLoop, calls=%fused_computation.53 | loop fusion | flops 2359296 | bytes 7077889 | tf_op jit(solution)/shard_map/convert_element_type | solution.py:1075
  343.9 4.8 %place_rows.3 = (f32[8,512,768]{2,1,0:T(8,128)}, f32[8,64,768]{2,1,0:T(8,128)}) custom-call(s32[4]{0:T(128)} %add_add_fusion.1.s_ref, f32[8,512,768]{2,1,0:T(8,128)} %get-tuple-element.124.video_in, f32[8,64,768]{2,1,0:T(8,128)} %get-tuple-element.125.lat_in, bf16[2,576,768]{2,1,0:T(8,128)(2,1)} %copy-done.9, ...), custom_call_target="tpu_custom_call", output_to_operand_aliasing={{0}: (1, {}), {1}: (2, {})} | custom-call | flops 3000000000 | bytes 5000000 | tf_op jit(solution)/shard_map/place_rows/pallas_call | solution.py:995
  (250 shorter events, 101.4 us)
Async XLA Ops:
  7.2 236.4 %all-reduce.5.cloned.1.call-start = ((), (), s32[]{:S(2)}) async-start(), calls=%async_computation.1 | async-start | bytes 2359296 | tf_op jit(solution)/shard_map/psum | solution.py:913
  11.2 28.5 %collective-permute-start.1 = (bf16[4,512,768]{2,1,0:T(8,128)(2,1)}, bf16[4,512,768]{2,1,0:T(8,128)(2,1)}, u32[]{:S(2)}, u32[]{:S(2)}) collective-permute-start(bf16[4,512,768]{2,1,0:T(8,128)(2,1)} %constant_dynamic-slice_fusion.6), channel_id=1, source_target_pairs={{0,16},{16,0},{1,17},{17,1},{2,18},{18,2},{3,19},{19,3},{4,20},{20... | collective-permute-start | bytes 9437192 | tf_op jit(solution)/shard_map/ppermute | solution.py:393
  12.8 37.4 %collective-permute-start.2 = (bf16[2,192,768]{2,1,0:T(8,128)(2,1)}, bf16[2,192,768]{2,1,0:T(8,128)(2,1)S(1)}, u32[]{:S(2)}, u32[]{:S(2)}) collective-permute-start(bf16[2,192,768]{2,1,0:T(8,128)(2,1)} %constant_dynamic-slice_fusion.5), channel_id=1, source_target_pairs={{0,1},{1,2},{2,3},{4,5},{5,6},{6,7},{8,9},{9,10},{10,11},{12,13},{... | collective-permute-start | bytes 1769480 | tf_op jit(solution)/shard_map/ppermute | solution.py:728
  17.4 32.8 %collective-permute-start.3 = (bf16[2,192,768]{2,1,0:T(8,128)(2,1)}, bf16[2,192,768]{2,1,0:T(8,128)(2,1)}, u32[]{:S(2)}, u32[]{:S(2)}) collective-permute-start(bf16[2,192,768]{2,1,0:T(8,128)(2,1)} %constant_dynamic-slice_fusion.5), channel_id=1, source_target_pairs={{1,0},{2,1},{3,2},{5,4},{6,5},{7,6},{9,8},{10,9},{11,10},{13,12},{... | collective-permute-start | bytes 1769480 | tf_op jit(solution)/shard_map/ppermute | solution.py:729
  19.9 14.3 %collective-permute-start = (bf16[4,128,768]{2,1,0:T(8,128)(2,1)}, bf16[4,128,768]{2,1,0:T(8,128)(2,1)}, u32[]{:S(2)}, u32[]{:S(2)}) collective-permute-start(bf16[4,128,768]{2,1,0:T(8,128)(2,1)} %constant_dynamic-slice_fusion.7), channel_id=1, source_target_pairs={{0,16},{16,0},{1,17},{17,1},{2,18},{18,2},{3,19},{19,3},{4,20},{20... | collective-permute-start | bytes 2359304 | tf_op jit(solution)/shard_map/ppermute | solution.py:393
  22.0 17.6 %collective-permute-start.4 = (bf16[4,16,896]{2,1,0:T(8,128)(2,1)}, bf16[4,16,896]{2,1,0:T(8,128)(2,1)}, u32[]{:S(2)}, u32[]{:S(2)}) collective-permute-start(bf16[4,16,896]{2,1,0:T(8,128)(2,1)} %get-tuple-element.176), channel_id=1, source_target_pairs={{0,0},{4,16},{8,4},{12,20},{16,8},{20,24},{24,12},{28,28},{1,1},{5... | collective-permute-start | bytes 344072 | tf_op jit(solution)/shard_map/ppermute | solution.py:760
  34.2 16.0 %collective-permute-start.5 = (bf16[4,16,896]{2,1,0:T(8,128)(2,1)S(1)}, bf16[4,16,896]{2,1,0:T(8,128)(2,1)S(1)}, u32[]{:S(2)}, u32[]{:S(2)}) collective-permute-start(bf16[4,16,896]{2,1,0:T(8,128)(2,1)S(1)} %copy-done.33), channel_id=1, source_target_pairs={{0,16},{4,4},{8,20},{12,0},{16,24},{20,12},{24,28},{28,8},{1,17},{... | collective-permute-start | bytes 344072 | tf_op jit(solution)/shard_map/ppermute | solution.py:760
  51.4 11.6 %collective-permute-start.8 = (bf16[2,192,768]{2,1,0:T(8,128)(2,1)S(1)}, bf16[2,192,768]{2,1,0:T(8,128)(2,1)S(1)}, u32[]{:S(2)}, u32[]{:S(2)}) collective-permute-start(bf16[2,192,768]{2,1,0:T(8,128)(2,1)S(1)} %get-tuple-element.155), channel_id=1, source_target_pairs={{0,16},{16,0},{1,17},{17,1},{2,18},{18,2},{3,19},{19,3},{4,20},{20... | collective-permute-start | bytes 1769480 | tf_op jit(solution)/shard_map/ppermute | solution.py:393
  52.5 41.8 %collective-permute-start.9 = (bf16[2,192,768]{2,1,0:T(8,128)(2,1)S(1)}, bf16[2,192,768]{2,1,0:T(8,128)(2,1)S(1)}, u32[]{:S(2)}, u32[]{:S(2)}) collective-permute-start(bf16[2,192,768]{2,1,0:T(8,128)(2,1)S(1)} %collective-permute-done.2), channel_id=1, source_target_pairs={{1,2},{2,3},{5,6},{6,7},{9,10},{10,11},{13,14},{14,15},{17,18},{18... | collective-permute-start | bytes 1769480 | tf_op jit(solution)/shard_map/ppermute | solution.py:843
  53.2 41.2 %collective-permute-start.10 = (bf16[2,192,768]{2,1,0:T(8,128)(2,1)}, bf16[2,192,768]{2,1,0:T(8,128)(2,1)S(1)}, u32[]{:S(2)}, u32[]{:S(2)}) collective-permute-start(bf16[2,192,768]{2,1,0:T(8,128)(2,1)} %collective-permute-done.3), channel_id=1, source_target_pairs={{1,0},{2,1},{5,4},{6,5},{9,8},{10,9},{13,12},{14,13},{17,16},{18,1... | collective-permute-start | bytes 1769480 | tf_op jit(solution)/shard_map/ppermute | solution.py:844
  54.5 39.9 %collective-permute-start.11 = (bf16[2,192,768]{2,1,0:T(8,128)(2,1)}, bf16[2,192,768]{2,1,0:T(8,128)(2,1)S(1)}, u32[]{:S(2)}, u32[]{:S(2)}) collective-permute-start(bf16[2,192,768]{2,1,0:T(8,128)(2,1)} %constant_dynamic-slice_fusion.5), channel_id=1, source_target_pairs={{0,3},{4,7},{8,11},{12,15},{16,19},{20,23},{24,27},{28,31}} | collective-permute-start | bytes 1769480 | tf_op jit(solution)/shard_map/ppermute | solution.py:845
  60.6 33.8 %collective-permute-start.12 = (bf16[2,192,768]{2,1,0:T(8,128)(2,1)}, bf16[2,192,768]{2,1,0:T(8,128)(2,1)S(1)}, u32[]{:S(2)}, u32[]{:S(2)}) collective-permute-start(bf16[2,192,768]{2,1,0:T(8,128)(2,1)} %constant_dynamic-slice_fusion.5), channel_id=1, source_target_pairs={{3,0},{7,4},{11,8},{15,12},{19,16},{23,20},{27,24},{31,28}} | collective-permute-start | bytes 1769480 | tf_op jit(solution)/shard_map/ppermute | solution.py:846
  147.1 11.2 %collective-permute-start.16 = (bf16[128,768]{1,0:T(8,128)(2,1)S(1)}, bf16[128,768]{1,0:T(8,128)(2,1)S(1)}, u32[]{:S(2)}, u32[]{:S(2)}) collective-permute-start(bf16[128,768]{1,0:T(8,128)(2,1)S(1)} %get-tuple-element.168), channel_id=1, source_target_pairs={{0,1},{1,2},{2,3},{3,0},{4,5},{5,6},{6,7},{7,4},{8,9},{9,10},{10,1... | collective-permute-start | bytes 589832 | tf_op jit(solution)/shard_map/ppermute | solution.py:397
  147.2 18.3 %collective-permute-start.15 = (bf16[128,768]{1,0:T(8,128)(2,1)S(1)}, bf16[128,768]{1,0:T(8,128)(2,1)S(1)}, u32[]{:S(2)}, u32[]{:S(2)}) collective-permute-start(bf16[128,768]{1,0:T(8,128)(2,1)S(1)} %get-tuple-element.169), channel_id=1, source_target_pairs={{0,2},{1,3},{2,0},{3,1},{4,6},{5,7},{6,4},{7,5},{8,10},{9,11},{10,... | collective-permute-start | bytes 589832 | tf_op jit(solution)/shard_map/ppermute | solution.py:397
  152.0 13.5 %collective-permute-start.14 = (bf16[128,768]{1,0:T(8,128)(2,1)S(1)}, bf16[128,768]{1,0:T(8,128)(2,1)S(1)}, u32[]{:S(2)}, u32[]{:S(2)}) collective-permute-start(bf16[128,768]{1,0:T(8,128)(2,1)S(1)} %get-tuple-element.167), channel_id=1, source_target_pairs={{0,3},{1,0},{2,1},{3,2},{4,7},{5,4},{6,5},{7,6},{8,11},{9,8},{10,9... | collective-permute-start | bytes 589832 | tf_op jit(solution)/shard_map/ppermute | solution.py:397
  154.0 35.5 %collective-permute-start.20 = (bf16[768,768]{1,0:T(8,128)(2,1)S(1)}, bf16[768,768]{1,0:T(8,128)(2,1)S(1)}, u32[]{:S(2)}, u32[]{:S(2)}) collective-permute-start(bf16[768,768]{1,0:T(8,128)(2,1)S(1)} %get-tuple-element.184), channel_id=1, source_target_pairs={{0,16},{16,0},{1,17},{17,1},{2,18},{18,2},{3,19},{19,3},{4,20},{20... | collective-permute-start | bytes 3538952 | tf_op jit(solution)/shard_map/ppermute | solution.py:393
  170.8 18.6 %collective-permute-start.18 = (bf16[128,768]{1,0:T(8,128)(2,1)S(1)}, bf16[128,768]{1,0:T(8,128)(2,1)S(1)}, u32[]{:S(2)}, u32[]{:S(2)}) collective-permute-start(bf16[128,768]{1,0:T(8,128)(2,1)S(1)} %get-tuple-element.149), channel_id=1, source_target_pairs={{0,2},{1,3},{2,0},{3,1},{4,6},{5,7},{6,4},{7,5},{8,10},{9,11},{10,... | collective-permute-start | bytes 589832 | tf_op jit(solution)/shard_map/ppermute | solution.py:397
  173.5 15.9 %collective-permute-start.19 = (bf16[128,768]{1,0:T(8,128)(2,1)S(1)}, bf16[128,768]{1,0:T(8,128)(2,1)S(1)}, u32[]{:S(2)}, u32[]{:S(2)}) collective-permute-start(bf16[128,768]{1,0:T(8,128)(2,1)S(1)} %get-tuple-element.149), channel_id=1, source_target_pairs={{0,1},{1,2},{2,3},{3,0},{4,5},{5,6},{6,7},{7,4},{8,9},{9,10},{10,1... | collective-permute-start | bytes 589832 | tf_op jit(solution)/shard_map/ppermute | solution.py:397
  191.8 98.1 %all-reduce.3.cloned.1.call-start = ((), (), s32[]{:S(2)}) async-start(), calls=%async_computation | async-start | bytes 1572864 | tf_op jit(solution)/shard_map/psum | solution.py:914
  238.0 60.3 %collective-permute-start.22 = (bf16[2,576,768]{2,1,0:T(8,128)(2,1)}, bf16[2,576,768]{2,1,0:T(8,128)(2,1)}, u32[]{:S(2)}, u32[]{:S(2)}) collective-permute-start(bf16[2,576,768]{2,1,0:T(8,128)(2,1)} %get-tuple-element.122), channel_id=1, source_target_pairs={{0,16},{16,0},{1,17},{17,1},{2,18},{18,2},{3,19},{19,3},{4,20},{20... | collective-permute-start | bytes 5308424 | tf_op jit(solution)/shard_map/ppermute | solution.py:393
  293.7 45.1 %collective-permute-start.24 = (bf16[2,576,768]{2,1,0:T(8,128)(2,1)}, bf16[2,576,768]{2,1,0:T(8,128)(2,1)S(1)}, u32[]{:S(2)}, u32[]{:S(2)}) collective-permute-start(bf16[2,576,768]{2,1,0:T(8,128)(2,1)} %get-tuple-element.126), channel_id=1, source_target_pairs={{0,16},{16,0},{1,17},{17,1},{2,18},{18,2},{3,19},{19,3},{4,20},{20... | collective-permute-start | bytes 5308424 | tf_op jit(solution)/shard_map/ppermute | solution.py:393
  293.7 45.1 %collective-permute-start.25 = (bf16[768,768]{1,0:T(8,128)(2,1)}, bf16[768,768]{1,0:T(8,128)(2,1)}, u32[]{:S(2)}, u32[]{:S(2)}) collective-permute-start(bf16[768,768]{1,0:T(8,128)(2,1)} %all-reduce.5.cloned.1.call-done), channel_id=1, source_target_pairs={{0,16},{16,0},{1,17},{17,1},{2,18},{18,2},{3,19},{19,3},{4,20},{20... | collective-permute-start | bytes 3538952 | tf_op jit(solution)/shard_map/ppermute | solution.py:393
  302.0 11.4 %collective-permute-start.26 = (bf16[112,768]{1,0:T(8,128)(2,1)S(1)}, bf16[112,768]{1,0:T(8,128)(2,1)S(1)}, u32[]{:S(2)}, u32[]{:S(2)}) collective-permute-start(bf16[112,768]{1,0:T(8,128)(2,1)S(1)} %get-tuple-element.172), channel_id=1, source_target_pairs={{0,12},{4,0},{8,4},{12,8},{1,13},{5,1},{9,5},{13,9},{2,14},{6,2},{... | collective-permute-start | bytes 516104 | tf_op jit(solution)/shard_map/ppermute | solution.py:435
  310.5 19.8 %collective-permute-start.30 = (bf16[4,16,768]{2,1,0:T(8,128)(2,1)S(1)}, bf16[4,16,768]{2,1,0:T(8,128)(2,1)S(1)}, u32[]{:S(2)}, u32[]{:S(2)}) collective-permute-start(bf16[4,16,768]{2,1,0:T(8,128)(2,1)S(1)} %get-tuple-element.181), channel_id=1, source_target_pairs={{16,0},{4,4},{20,8},{0,12},{24,16},{12,20},{28,24},{8,28},{17,1},{... | collective-permute-start | bytes 294920 | tf_op jit(solution)/shard_map/ppermute | solution.py:1047
  (61 other events, 416.9 us)
Sparse Core Ops, SparseCore 0:
  191.9 51.6 all-reduce.4
  246.0 43.8 all-reduce.2
where the time goes:
time: 364 us; the launch traced here: 357 us
  Pallas kernels  154 us (42%)
  starting transfers between devices  54.7 us (15%)
  waiting for transfers between devices  48.3 us (13%)
  local copies, waits for them, and re-layouts  40.9 us (11%)
  other arithmetic  25.8 us (7%)
  between operations  17.3 us (5%)
  matrix products  16.6 us (5%)
    pallas_call x6, Pallas kernels, call(): pl.pallas_call(kernel, name=name, grid_spec=pltpu.PrefetchScalarGridSpec(...  144 us
    ppermute x6, waiting for transfers between devices, head_shift(): lax.ppermute(values, 'head', [(i, (i - shift) % count) for i in range(cou...  23.1 us
    dot_general x9, matrix products, dot(): return jnp.einsum(spec, a, b, preferred_element_type=F32)  16.6 us
    unnamed x96, local copies, waits for them, and re-layouts  13.1 us
    ppermute x6, starting transfers between devices, head_shift(): lax.ppermute(values, 'head', [(i, (i - shift) % count) for i in range(cou...  11.3 us
    ppermute x4, starting transfers between devices, local(): lax.ppermute(block, ('vid', 'txt'), caption_perm(step, 2, txt_count, 2))  10.4 us
    pallas_call x2, Pallas kernels, place(): pl.pallas_call(place_kernel, name='place_rows', grid_spec=pltpu.PrefetchS...  9.76 us
    psum x1, waiting for transfers between devices, local(): lax.psum(dot('blf,fd->bld', activ, down_weight).astype(BF16), 'head')  8.73 us
  transfers between devices with their start and end apart: 39, of which 11 were waited for; matrix products, arithmetic and copies ran while one was open for 13% of the time, Pallas kernels for 34%

commit v1 on v0

--- a/solution.py
+++ b/solution.py
@@ -401,14 +401,18 @@
     return lax.dynamic_slice_in_dim(values, index * size, size, axis)
 
 
-def sum_over_head(part, place, count):
-    low = part.astype(jnp.bfloat16)
+def reduce_over_head(part, place, count):
+    low = part.astype(BF16)
     total = lax.dynamic_index_in_dim(part, place, 0, False)
     for shift in range(1, count):
         chunk = lax.dynamic_index_in_dim(low, (place - shift) % count, 0, False)
-        total = total + head_shift(chunk, shift, count).astype(jnp.float32)
-    total = total.astype(jnp.bfloat16)
-    result = lax.dynamic_update_index_in_dim(jnp.zeros_like(low), total, place, 0)
+        total = total + head_shift(chunk, shift, count).astype(F32)
+    return total.astype(BF16)
+
+
+def gather_head(total, place, count):
+    result = jnp.zeros((count,) + total.shape, BF16)
+    result = lax.dynamic_update_index_in_dim(result, total, place, 0)
     for shift in range(1, count):
         result = lax.dynamic_update_index_in_dim(
             result, head_shift(total, shift, count), (place + shift) % count, 0
@@ -462,6 +466,7 @@
 
 
 PAIR = 128
+BACK_COST = 3
 F32 = jnp.float32
 BF16 = jnp.bfloat16
 
@@ -511,52 +516,50 @@
     return jnp.concatenate([mask, mask], axis=1).astype(F32) > 0.5
 
 
-def forward_kernel(
-    s_ref, tok_ref, cap_ref, gain_ref, lat_ref, gain_lat_ref, wq_ref, wk_ref, wv_ref, *refs
-):
-    q_ref, k_ref, v_ref, lse_ref, o_ref, s_scr = refs[-6:]
+def forward_kernel(s_ref, tok_ref, cap_ref, gain_ref, lat_ref, gain_lat_ref, wq_ref, wkv_ref, *refs):
+    q_ref, k_ref, v_ref, lse_ref, o_ref, s_scr, e_scr, wkv_scr = refs[-8:]
     keys, width = k_ref.shape
     cap = cap_ref.shape[0]
     step = (keys - cap) // 4
-
-    def matrix(ref):
-        return ref[...].reshape(width, D)
-
     latn = layer_norm(lat_ref[...].astype(F32), gain_lat_ref[...]).astype(BF16)
-    q_ref[...] = (dot_nt(latn, matrix(wq_ref)).astype(BF16).astype(F32) * 0.125).astype(BF16)
-
-    def project(c, carry):
+    queries = dot_nt(latn, wq_ref[...].reshape(width, D)).astype(BF16).astype(F32)
+    q_ref[...] = (queries * 0.125).astype(BF16)
+
+    @pl.when(pl.program_id(0) == 0)
+    def _():
+        wkv_scr[...] = wkv_ref[...].reshape(2 * width, D).T
+
+    def project(rows, tokens):
+        both = dot_nn(tokens, wkv_scr[...]).astype(BF16)
+        k_ref[rows, :] = both[:, :width]
+        v_ref[rows, :] = both[:, width:]
+
+    def project_video(c, carry):
         rows = pl.ds(pl.multiple_of(c * step, 16), step)
-        k_ref[rows, :] = dot_nt(tok_ref[rows, :], matrix(wk_ref)).astype(BF16)
-        v_ref[rows, :] = dot_nt(tok_ref[rows, :], matrix(wv_ref)).astype(BF16)
+        project(rows, tok_ref[rows, :])
         return carry
 
-    lax.fori_loop(0, 4, project, 0)
+    lax.fori_loop(0, 4, project_video, 0)
     cap_rows = pl.ds(keys - cap, cap)
-    cap_norm = layer_norm(cap_ref[:, pl.ds(0, D)].astype(F32), gain_ref[...]).astype(BF16)
-    k_ref[cap_rows, :] = dot_nt(cap_norm, matrix(wk_ref)).astype(BF16)
-    v_ref[cap_rows, :] = dot_nt(cap_norm, matrix(wv_ref)).astype(BF16)
-    chunks = chunk_list(keys - cap, cap, 256)
+    project(cap_rows, layer_norm(cap_ref[:, pl.ds(0, D)].astype(F32), gain_ref[...]).astype(BF16))
+    pieces = [pl.ds(start, 64) for start in range(0, keys, 64)]
 
     def pair(p, carry):
         cols = pl.ds(pl.multiple_of(p * PAIR, PAIR), PAIR)
         q2 = two_heads(q_ref[:, cols])
-        peak = None
-        for start, size in chunks:
-            rows = pl.ds(start, size)
-            s = dot_nt(k_ref[rows, cols], q2)
-            if start == keys - cap:
-                s = jnp.where(cap_mask(cap_ref), s, -1e30)
-            s_scr[rows, :] = s
-            top = jnp.max(s, axis=0, keepdims=True)
-            peak = top if peak is None else jnp.maximum(peak, top)
-        total = jnp.zeros_like(peak)
-        out = jnp.zeros((PAIR, q2.shape[0]), F32)
-        for start, size in chunks:
-            rows = pl.ds(start, size)
+        s_scr[...] = dot_nt(k_ref[:, cols], q2)
+        s_scr[cap_rows, :] = jnp.where(cap_mask(cap_ref), s_scr[cap_rows, :], -1e30)
+        peak = s_scr[pieces[0], :]
+        for rows in pieces[1:]:
+            peak = jnp.maximum(peak, s_scr[rows, :])
+        peak = jnp.max(peak, axis=0, keepdims=True)
+        total = jnp.zeros((8, q2.shape[0]), F32)
+        for rows in pieces:
             e = jnp.exp(s_scr[rows, :] - peak)
-            total = total + jnp.sum(e, axis=0, keepdims=True)
-            out = out + dot_tn(v_ref[rows, cols], e.astype(BF16))
+            e_scr[rows, :] = e.astype(BF16)
+            total = total + jnp.sum(e.reshape(-1, 8, q2.shape[0]), axis=0)
+        total = jnp.sum(total, axis=0, keepdims=True)
+        out = dot_tn(v_ref[:, cols], e_scr[...])
         o_ref[:, cols] = from_two_heads(out / total)
         lse_ref[pl.ds(p, 1), :] = peak + jnp.log(total)
         return carry
@@ -565,20 +568,16 @@
 
 
 def backward_kernel(
-    first, s_ref, q_ref, k_ref, v_ref, lse_ref, o_ref, datt_ref, own_ref, other_ref, cap_ref,
-    wk_ref, wv_ref, gain_ref, tok_ref, wq_ref, lat_ref, after_ref, gain_lat_ref, *refs
+    s_ref, q_ref, k_ref, v_ref, lse_ref, o_ref, datt_ref, own_ref, other_ref, cap_ref,
+    wk_ref, wv_ref, gain_ref, tok_ref, wq_ref, lat_ref, after_ref, gain_lat_ref, ready_ref,
+    own_out, other_out, cap_out, lat_out, late_ref,
+    dq_ref, dk_ref, dv_ref, s_scr, dp_scr, p_scr, ds_scr, up_scr, sums_ref, gain_out,
 ):
-    if first:
-        own_out, other_out, cap_out, lat_out, sums_ref, gain_out = refs[:6]
-    else:
-        sums_in, gain_in, ready_ref = refs[:3]
-        own_out, other_out, cap_out, lat_out, late_ref = refs[5:10]
-        sums_ref, gain_out = refs[-2:]
-    dq_ref, dk_ref, dv_ref = refs[6:9] if first else refs[10:13]
     item = pl.program_id(0)
     keys = k_ref.shape[0]
     cap = cap_ref.shape[0]
-    chunks = chunk_list(keys - cap, cap, 256)
+    cap_rows = pl.ds(keys - cap, cap)
+    pieces = [pl.ds(start, 64) for start in range(0, keys, 64)]
 
     def pair(p, carry):
         cols = pl.ds(pl.multiple_of(p * PAIR, PAIR), PAIR)
@@ -595,19 +594,16 @@
         )
         pairs_here = D // PAIR // lse_ref.shape[0]
         lse = lse_ref[p // pairs_here, pl.ds(p % pairs_here, 1), :]
-        dq = jnp.zeros((PAIR, q2.shape[0]), F32)
-        for start, size in chunks:
-            rows = pl.ds(start, size)
-            k = k_ref[rows, cols]
-            s = dot_nt(k, q2)
-            d_probs = dot_nt(v_ref[rows, cols], d2)
-            if start == keys - cap:
-                s = jnp.where(cap_mask(cap_ref), s, -1e30)
-            probs = jnp.exp(s - lse)
-            d_scores = (probs * (d_probs - delta)).astype(BF16)
-            dv_ref[rows, cols] = dot_nn(probs.astype(BF16), d2).astype(BF16)
-            dk_ref[rows, cols] = dot_nn(d_scores, q2).astype(BF16)
-            dq = dq + dot_tn(k, d_scores)
+        s_scr[...] = dot_nt(k_ref[:, cols], q2)
+        dp_scr[...] = dot_nt(v_ref[:, cols], d2)
+        s_scr[cap_rows, :] = jnp.where(cap_mask(cap_ref), s_scr[cap_rows, :], -1e30)
+        for rows in pieces:
+            probs = jnp.exp(s_scr[rows, :] - lse)
+            p_scr[rows, :] = probs.astype(BF16)
+            ds_scr[rows, :] = (probs * (dp_scr[rows, :] - delta)).astype(BF16)
+        dv_ref[:, cols] = dot_nn(p_scr[...], d2).astype(BF16)
+        dk_ref[:, cols] = dot_nn(ds_scr[...], q2).astype(BF16)
+        dq = dot_tn(k_ref[:, cols], ds_scr[...])
         dq_ref[:, cols] = (from_two_heads(dq) * 0.125).astype(BF16)
         return carry
 
@@ -616,25 +612,28 @@
 
     @pl.when(item == 0)
     def _():
-        gain_out[...] = jnp.zeros_like(gain_out) if first else gain_in[...]
-        sums_ref[...] = jnp.zeros_like(sums_ref) if first else sums_in[...]
-
-    window = pl.ds(pl.multiple_of(s_ref[2], PAIR), sums_ref.shape[1])
+        gain_out[...] = jnp.zeros_like(gain_out)
+        sums_ref[...] = jnp.zeros_like(sums_ref)
+
+    wide = sums_ref.shape[0] // 3
+    window = pl.ds(pl.multiple_of(s_ref[2], PAIR), wide)
     video_rows = pl.ds(0, keys - cap)
-    cap_rows = pl.ds(keys - cap, cap)
     cap_norm = layer_norm(cap_ref[:, pl.ds(0, D)].astype(F32), gain).astype(BF16)
     latn = layer_norm(lat_ref[...].astype(F32), gain_lat_ref[...]).astype(BF16)
-    sums_ref[0] += dot_tn(dq_ref[:, window], latn)
-    for n, ref in ((1, dk_ref), (2, dv_ref)):
-        sums_ref[n] += dot_tn(ref[video_rows, window], tok_ref[...]) + dot_tn(
-            ref[cap_rows, window], cap_norm
-        )
+    sums_ref[pl.ds(0, wide), :] += dot_tn(dq_ref[:, window], latn)
+
+    def both(rows):
+        return jnp.concatenate([dk_ref[rows, window], dv_ref[rows, window]], axis=1)
+
+    sums_ref[pl.ds(wide, 2 * wide), :] += dot_tn(both(video_rows), tok_ref[...]) + dot_tn(
+        both(cap_rows), cap_norm
+    )
 
     def norm_back(x, up, gain, row):
         center = x - jnp.mean(x, axis=-1, keepdims=True)
         rate = lax.rsqrt(jnp.mean(center * center, axis=-1, keepdims=True) + 1e-05)
         hat = center * rate
-        gain_out[pl.ds(row, 1), :] += jnp.sum(up * hat, axis=0, keepdims=True)
+        gain_out[pl.ds(8 * row, 8), :] += jnp.sum((up * hat).reshape(-1, 8, D), axis=0)
         scaled = up * gain
         first = jnp.mean(scaled, axis=-1, keepdims=True)
         second = jnp.mean(scaled * hat, axis=-1, keepdims=True)
@@ -652,28 +651,30 @@
         def chunk(c, carry, ref=ref, out=out, size=size, start=start):
             rows = pl.ds(pl.multiple_of(c * size, 16), size)
             key_rows = pl.ds(pl.multiple_of(start + c * size, 16), size)
-            up = dot_nn(dk_ref[key_rows, :], square(wk_ref)) + dot_nn(
+            up_scr[pl.ds(0, size), :] = dot_nn(dk_ref[key_rows, :], square(wk_ref)) + dot_nn(
                 dv_ref[key_rows, :], square(wv_ref)
             )
-            back = norm_back(ref[rows, pl.ds(0, D)].astype(F32), up, gain, 0)
-            out[rows, :] = back.astype(out.dtype)
+            for at in range(0, size, 32):
+                piece = pl.ds(pl.multiple_of(c * size, 16) + at, 32)
+                back = norm_back(
+                    ref[piece, pl.ds(0, D)].astype(F32), up_scr[pl.ds(at, 32), :], gain, 0
+                )
+                out[piece, :] = back.astype(out.dtype)
             return carry
 
         lax.fori_loop(0, ref.shape[0] // size, chunk, 0)
         start += ref.shape[0]
-
-    if first:
-        return
 
     @pl.when(item == pl.num_programs(0) - 1)
     def _():
         width = D // 4
-        mine = pl.ds(pl.multiple_of(s_ref[3], PAIR // 2), width)
         for n in range(3):
-            late_ref[pl.ds(n * width, width), :] = sums_ref[n, mine, :].astype(BF16)
+            mine = pl.ds(pl.multiple_of(s_ref[3] + n * wide, PAIR // 2), width)
+            late_ref[pl.ds(n * width, width), :] = sums_ref[mine, :].astype(BF16)
         ready = ready_ref.shape[0]
         late_ref[pl.ds(3 * width, ready), :] = ready_ref[...]
-        gains = jnp.concatenate([gain_out[...], jnp.zeros((8, D), F32)], axis=0)
+        gains = [jnp.sum(gain_out[pl.ds(8 * row, 8), :], axis=0, keepdims=True) for row in (0, 1)]
+        gains = jnp.concatenate(gains + [jnp.zeros((14, D), F32)], axis=0)
         late_ref[pl.ds(3 * width + ready, 16), :] = gains.astype(BF16)
         spare = late_ref.shape[0] - 3 * width - ready - 16
         late_ref[pl.ds(3 * width + ready + 16, spare), :] = jnp.zeros((spare, D), BF16)
@@ -723,7 +724,7 @@
     def dot(spec, a, b):
         return jnp.einsum(spec, a, b, preferred_element_type=F32)
 
-    packed = jnp.stack([query_weight.T, key_matrix.T, value_matrix.T, out_weight])
+    packed = jnp.stack([key_matrix.T, value_matrix.T, query_weight.T, out_weight])
     half = take_block(packed, core, 2)
     up1 = lax.ppermute(half, "head", [(0, 1), (1, 2), (2, 3)])
     down1 = lax.ppermute(half, "head", [(1, 0), (2, 1), (3, 2)])
@@ -733,8 +734,8 @@
     part_shape = (2, 2, 2, head_width, D)
 
     def place_chunk(whole, chunk, at_core, at_chunk):
-        chunk = chunk.reshape((-1, 1) + chunk.shape[-3:])
-        return lax.dynamic_update_slice(whole, chunk, (at_core, at_chunk, zero, zero, zero))
+        chunk = chunk.reshape((-1, 2, 1) + chunk.shape[-2:])
+        return lax.dynamic_update_slice(whole, chunk, (at_core, zero, at_chunk, zero, zero))
 
     video_other = swap_cores(take_block(video_tokens, 1 - core, own))
     both = jnp.concatenate([latents, cotangent], axis=1)
@@ -770,15 +771,15 @@
 
     def weight_spec(m):
         return pl.BlockSpec(
-            (2, None, 2, None, head_width, D),
-            lambda i, s: (0, m // 2, 0, m % 2, 0, 0),
+            (2, None, None, 2, head_width, D),
+            lambda i, s: (0, m // 2, m % 2, 0, 0, 0),
             pipeline_mode=pl.Buffered(1),
         )
 
-    def part_spec(m):
+    def part_spec(at_core, first, count):
         return pl.BlockSpec(
-            (None, 2, None, head_width, D),
-            lambda i, s: (m // 2, 0, m % 2, 0, 0),
+            (None, count, 2, head_width, D),
+            lambda i, s: (at_core, first, 0, 0, 0),
             pipeline_mode=pl.Buffered(1),
         )
 
@@ -851,7 +852,7 @@
             "attention_forward",
             [item_spec(2 * video_here), item_spec(cap_rows, D + PAIR), row_spec]
             + [item_spec(lat_rows), row_spec]
-            + [part_spec(m) for m in range(3)]
+            + [part_spec(1, 0, 1), part_spec(0, 0, 2)]
             + [pl.BlockSpec(memory_space=pl.ANY)] * len(before),
             [
                 (half_spec(lat_rows), (own, lat_rows, D), BF16),
@@ -864,10 +865,14 @@
                 ),
                 (half_spec(lat_rows), (own, lat_rows, D), F32),
             ],
-            (tok_norm, cap, gain_tok_row, lat, gain_lat_row, part, part, part) + tuple(before),
+            (tok_norm, cap, gain_tok_row, lat, gain_lat_row, part, part) + tuple(before),
             23,
-            [pltpu.VMEM((keys_here, 2 * lat_rows), F32)],
-            {9 + n: n for n in range(len(before))},
+            [
+                pltpu.VMEM((keys_here, 2 * lat_rows), F32),
+                pltpu.VMEM((keys_here, 2 * lat_rows), BF16),
+                pltpu.VMEM((D, 4 * head_width), BF16),
+            ],
+            {8 + n: n for n in range(len(before))},
             scalars,
         )
 
@@ -878,7 +883,9 @@
         low = jnp.where(z == 0, choices[0], choices[1])
         return jnp.where(z < 2, low, jnp.where(z == 2, choices[2], choices[3]))
 
-    far_mine = jnp.stack([by_place(down2, down1, up2, up3), by_place(down3, down2, up1, up2)])
+    far_mine = jnp.stack(
+        [by_place(down2, down1, up2, up3), by_place(down3, down2, up1, up2)], axis=1
+    )
     far = jnp.zeros(part_shape, BF16)
     far = lax.dynamic_update_index_in_dim(far, far_mine, core, 0)
     far = lax.dynamic_update_index_in_dim(far, swap_cores(far_mine), 1 - core, 0)
@@ -888,7 +895,7 @@
         return lax.dynamic_update_index_in_dim(whole, far, 1 - near_at, 0)
 
     queries, keys, values, lse, attended = forward(far, scalars_far, before)
-    w_out = both_halves(near[1, :, 1], far[1, :, 1]).reshape(D, D)
+    w_out = both_halves(near[1, 1], far[1, 1]).reshape(D, D)
     lat_float = lat.astype(F32)
     mixed_in = (attended * keep[:, None, None]).astype(BF16)
     after_attn = lat_float + dot("ble,ed->bld", mixed_in, w_out)
@@ -900,7 +907,7 @@
     d_pre = gelu_pull(dot("bld,fd->blf", cot, down_weight))[0].astype(BF16)
     d_mlp_part = dot("blf,df->bld", d_pre, up_weight)
     d_mlp_part, activ, d_pre = lax.optimization_barrier((d_mlp_part, activ, d_pre))
-    d_mlp_norm = sum_over_head(d_mlp_part, z, head_count)
+    d_mlp_norm = gather_head(reduce_over_head(d_mlp_part, z, head_count), z, head_count)
     grad_down = dot("blf,bld->fd", activ, cot).astype(BF16)
     grad_up = dot("bld,blf->df", mlp_norm, d_pre).astype(BF16)
     near, far, _ = lax.optimization_barrier((near, far, d_mlp_part))
@@ -911,7 +918,7 @@
         (activ, d_mlp_norm, early.astype(BF16), weights)
     )
     early = lax.psum(early, "txt")
-    growth = lax.psum(dot("blf,fd->bld", activ, down_weight).astype(BF16), "head")
+    growth = reduce_over_head(dot("blf,fd->bld", activ, down_weight), z, head_count)
 
     d_after_norm, gain_mlp_part = norm_back_rows(after_attn, gain_mlp, d_mlp_norm.astype(F32))
     d_after = cot.astype(F32) + d_after_norm
@@ -929,75 +936,64 @@
     ).astype(BF16)
     late_size = 4 * head_width + 32
     late_size = late_size + -late_size % (32 * txt_count)
-    some = own // 2
-
-    def backward(at, before=(), operands=()):
-        first = at == 0
-        sums_shape = (3, 2 * PAIR, D)
-        outs = [
-            (own_spec(video_here, at), video_tokens.shape, F32),
-            (item_spec(video_here + lat_half), (some, video_here + lat_half, D), BF16),
-            (item_spec(cap_rows), (some, cap_rows, D), BF16),
-            (own_spec(lat_half, at), latents.shape, F32),
-        ]
-        scratch = [
+    pair_shape = (keys_here, 2 * lat_rows)
+    d_att, ready = lax.optimization_barrier((d_att, ready))
+    video_grad, other_back, cap_back, latent_grad, late = call(
+        backward_kernel,
+        "attention_backward",
+        [
+            item_spec(lat_rows),
+            item_spec(keys_here),
+            item_spec(keys_here),
+            pl.BlockSpec((None, 2, 8, 2 * lat_rows), lambda i, s: (i, 0, 0, 0)),
+            item_spec(lat_rows),
+            item_spec(lat_rows),
+            own_spec(video_here),
+            item_spec(video_here),
+            item_spec(cap_rows, D + PAIR),
+            weight_spec(0),
+            weight_spec(1),
+            row_spec,
+            item_spec(2 * video_here),
+            weight_spec(2),
+            item_spec(lat_rows),
+            item_spec(lat_rows),
+            row_spec,
+            whole_spec(*ready.shape),
+        ],
+        [
+            (own_spec(video_here), video_tokens.shape, F32),
+            item_out(video_here + lat_half, BF16),
+            item_out(cap_rows, BF16),
+            (own_spec(lat_half), latents.shape, F32),
+            (whole_spec(late_size, D), (late_size, D), BF16),
+        ],
+        (
+            queries, keys, values, lse, attended, d_att, video_tokens, video_other, cap,
+            weights, weights, gain_tok_row, tok_norm, weights, lat, d_after, gain_lat_row, ready,
+        ),
+        BACK_COST,
+        [
             pltpu.VMEM((lat_rows, D), BF16),
             pltpu.VMEM((keys_here, D), BF16),
             pltpu.VMEM((keys_here, D), BF16),
-        ]
-        if first:
-            ins = []
-            outs = outs + [(whole_spec(*sums_shape), sums_shape, F32), (whole_spec(8, D), (8, D), F32)]
-        else:
-            ins = [whole_spec(*sums_shape), whole_spec(8, D), whole_spec(*ready.shape)]
-            ins = ins + [pl.BlockSpec(memory_space=pl.ANY)] * len(before)
-            outs = outs + [(whole_spec(late_size, D), (late_size, D), BF16)]
-            scratch = scratch + [pltpu.VMEM(sums_shape, F32), pltpu.VMEM((8, D), F32)]
-        return call(
-            functools.partial(backward_kernel, first),
-            "attention_backward",
-            [
-                item_spec(lat_rows, D, at),
-                item_spec(keys_here, D, at),
-                item_spec(keys_here, D, at),
-                pl.BlockSpec((None, 2, 8, 2 * lat_rows), lambda i, s: (at + i, 0, 0, 0)),
-                item_spec(lat_rows, D, at),
-                item_spec(lat_rows, D, at),
-                own_spec(video_here, at),
-                item_spec(video_here, D, at),
-                item_spec(cap_rows, D + PAIR, at),
-                weight_spec(1),
-                weight_spec(2),
-                row_spec,
-                item_spec(2 * video_here, D, at),
-                weight_spec(0),
-                item_spec(lat_rows, D, at),
-                item_spec(lat_rows, D, at),
-                row_spec,
-            ]
-            + ins,
-            outs,
-            (
-                queries, keys, values, lse, attended, d_att, video_tokens, video_other, cap,
-                weights, weights, gain_tok_row, tok_norm, weights, lat, d_after,
-                gain_lat_row,
-            )
-            + tuple(operands)
-            + tuple(before),
-            3,
-            scratch,
-            {} if first else {21: 0, 22: 3},
-            grid=some,
-        )
-
-    def place(at, video_grad, latent_grad, part):
+            pltpu.VMEM(pair_shape, F32),
+            pltpu.VMEM(pair_shape, F32),
+            pltpu.VMEM(pair_shape, BF16),
+            pltpu.VMEM(pair_shape, BF16),
+            pltpu.VMEM((256, D), F32),
+            pltpu.VMEM((6 * PAIR, D), F32),
+            pltpu.VMEM((16, D), F32),
+        ],
+    )
+    def place(video_grad, latent_grad, part):
         piece = video_here // 2
         return pl.pallas_call(
             place_kernel,
             name="place_rows",
             grid_spec=pltpu.PrefetchScalarGridSpec(
                 num_scalar_prefetch=1,
-                grid=(some, 2),
+                grid=(own, 2),
                 in_specs=[
                     pl.BlockSpec(memory_space=pl.ANY),
                     pl.BlockSpec(memory_space=pl.ANY),
@@ -1005,10 +1001,8 @@
                     pl.BlockSpec((None, lat_half, D), lambda i, r, s: (i, video_here // lat_half, 0)),
                 ],
                 out_specs=[
-                    pl.BlockSpec((None, piece, D), lambda i, r, s: ((1 - s[0]) * own + at + i, r, 0)),
-                    pl.BlockSpec(
-                        (None, lat_half, D), lambda i, r, s: ((1 - s[0]) * own + at + i, 0, 0)
-                    ),
+                    pl.BlockSpec((None, piece, D), lambda i, r, s: ((1 - s[0]) * own + i, r, 0)),
+                    pl.BlockSpec((None, lat_half, D), lambda i, r, s: ((1 - s[0]) * own + i, 0, 0)),
                 ],
             ),
             out_shape=[
@@ -1017,29 +1011,24 @@
             ],
             input_output_aliases={1: 0, 2: 1},
             cost_estimate=pl.CostEstimate(
-                flops=3 * 10**9, transcendentals=0, bytes_accessed=5 * 10**6
+                flops=6 * 10**9, transcendentals=0, bytes_accessed=10**7
             ),
         )(scalars, video_grad, latent_grad, part, part)
 
-    d_att, ready = lax.optimization_barrier((d_att, ready))
-    video_grad, back_a, cap_a, latent_grad, sums, gain_sums = backward(0)
-    here_a = swap_cores(back_a)
-    early, sums = lax.optimization_barrier((early, sums))
-    video_grad, back_b, cap_b, latent_grad, late = backward(
-        some, (video_grad, latent_grad), (sums, gain_sums, ready)
-    )
-    growth, _ = lax.optimization_barrier((growth, late))
+    growth, early, late = lax.optimization_barrier((growth, early, late))
     late_half, late_swapped = reduce_over_cores(late, core)
-    here_b = swap_cores(back_b)
-    cap_back = jnp.concatenate([cap_a, cap_b])
+    other_here = swap_cores(other_back)
     cap_back, _ = lax.optimization_barrier((cap_back, late_swapped))
     late_total = reduce_over_group(late_half, place_index, txt_count)
-    here_a, _ = lax.optimization_barrier((here_a, late_half))
     early_other = swap_cores(early)
-    video_grad, latent_grad = place(0, video_grad, latent_grad, here_a)
-    here_b, early, early_other, _ = lax.optimization_barrier((here_b, early, early_other, late_total))
+    other_here, _ = lax.optimization_barrier((other_here, late_half))
+    growth, _ = lax.optimization_barrier((growth, late_swapped))
+    growth = gather_head(growth, z, head_count)
+    video_grad, latent_grad = place(video_grad, latent_grad, other_here)
+    video_grad, latent_grad, late_total = lax.optimization_barrier(
+        (video_grad, latent_grad, late_total)
+    )
     late = gather_group(late_total, core, place_index, txt_count).astype(F32)
-    video_grad, latent_grad = place(some, video_grad, latent_grad, here_b)
     out_mine = (after_attn + growth.astype(F32)).astype(BF16)
     caption_grad = jnp.zeros((txt_count, own, cap_here, D), F32)
     for step in range(txt_count):

time: 364 us -> 353 us (0.970); the launches traced: 357 us -> 352 us
  Pallas kernels: 154 us -> 130 us
  starting transfers between devices: 54.7 us -> 69.3 us
  waiting for transfers between devices: 48.3 us -> 60.2 us
    pallas_call x6 -> x5, Pallas kernels: 144 us -> 122 us  [call(): pl.pallas_call(kernel, name=name, grid_spec=pltpu.PrefetchScalarGridSpec(...]
    ppermute x6 -> x12, waiting for transfers between devices: 23.1 us -> 37.5 us  [head_shift(): lax.ppermute(values, 'head', [(i, (i - shift) % count) for i in range(cou...]
    psum x1 -> x0, waiting for transfers between devices: 8.73 us -> none  [local(): lax.psum(dot('blf,fd->bld', activ, down_weight).astype(BF16), 'head')]
    ppermute x4, starting transfers between devices: 7.82 us -> 15.3 us  [local(): lax.ppermute(cap_back[:, step * cap_here:(step + 1) * cap_here], ('vid',...]
    ppermute x4, waiting for transfers between devices: 0.86 us -> 7.63 us  [local(): lax.ppermute(cap_back[:, step * cap_here:(step + 1) * cap_here], ('vid',...]
    psum x1, waiting for transfers between devices: 5.5 us -> 0.01 us  [local(): early = lax.psum(early, 'txt')]
    ppermute x6 -> x12, starting transfers between devices: 11.3 us -> 16.1 us  [head_shift(): lax.ppermute(values, 'head', [(i, (i - shift) % count) for i in range(cou...]
    pallas_call x2 -> x1, Pallas kernels: 9.76 us -> 7.64 us  [place(): pl.pallas_call(place_kernel, name='place_rows', grid_spec=pltpu.PrefetchS...]
  transfers between devices with their start and end apart: 39 -> 43, of which waited for: 11 -> 12; matrix products, arithmetic and copies ran while one was open for 13% -> 11% of each run, Pallas kernels for 34% -> 29%
where the time goes in v1:
time: 353 us; the launch traced here: 352 us
  Pallas kernels  130 us (37%)
  starting transfers between devices  69.3 us (20%)
  waiting for transfers between devices  60.2 us (17%)
  local copies, waits for them, and re-layouts  38.1 us (11%)
  other arithmetic  23.5 us (7%)
  between operations  17 us (5%)
  matrix products  14 us (4%)
    pallas_call x5, Pallas kernels, call(): pl.pallas_call(kernel, name=name, grid_spec=pltpu.PrefetchScalarGridSpec(...  122 us
    ppermute x12, waiting for transfers between devices, head_shift(): lax.ppermute(values, 'head', [(i, (i - shift) % count) for i in range(cou...  37.5 us
    ppermute x12, starting transfers between devices, head_shift(): lax.ppermute(values, 'head', [(i, (i - shift) % count) for i in range(cou...  16.1 us
    ppermute x4, starting transfers between devices, local(): lax.ppermute(cap_back[:, step * cap_here:(step + 1) * cap_here], ('vid',...  15.3 us
    dot_general x9, matrix products, dot(): return jnp.einsum(spec, a, b, preferred_element_type=F32)  14 us
    unnamed x98, local copies, waits for them, and re-layouts  12.7 us
    ppermute x4, starting transfers between devices, local(): lax.ppermute(block, ('vid', 'txt'), caption_perm(step, 2, txt_count, 2))  9.08 us
    dynamic_slice x5, local copies, waits for them, and re-layouts, take_block(): return lax.dynamic_slice_in_dim(values, index * size, size, axis)  7.79 us
  transfers between devices with their start and end apart: 43, of which 12 were waited for; matrix products, arithmetic and copies ran while one was open for 11% of the time, Pallas kernels for 29%

profile of v1, /device:TPU:0, one launch (start us, length us, event | category | flops | bytes accessed | tf_op | source)
XLA Modules:
  0.0 351.6 jit_solution(713636746308041878)
XLA Ops:
  7.3 3.9 %constant_dynamic-slice_fusion.6 = bf16[4,512,768]{2,1,0:T(8,128)(2,1)} fusion(bf16[8,512,768]{2,1,0:T(8,128)(2,1)} %own_ref.1, s32[]{:T(128)S(6)} %select_n.283), kind=kLoop, calls=%fused_computation.129 | loop fusion | bytes 6291460 | tf_op jit(solution)/shard_map/dynamic_slice | solution.py:401
  12.8 4.5 %collective-permute-start.2 = (bf16[2,192,768]{2,1,0:T(8,128)(2,1)}, bf16[2,192,768]{2,1,0:T(8,128)(2,1)S(1)}, u32[]{:S(2)}, u32[]{:S(2)}) collective-permute-start(bf16[2,192,768]{2,1,0:T(8,128)(2,1)} %constant_dynamic-slice_fusion.5), channel_id=1, source_target_pairs={{0,1},{1,2},{2,3},{4,5},{5,6},{6,7},{8,9},{9,10},{10,11},{12,13},{... | collective-permute-start | bytes 1769480 | tf_op jit(solution)/shard_map/ppermute | solution.py:729
  32.9 5.9 %token_norm.2.refs_0_ = bf16[4,1024,768]{2,1,0:T(8,128)(2,1)} custom-call(s32[4]{0:T(128)} %add_add_fusion.1.s_ref, bf16[8,512,768]{2,1,0:T(8,128)(2,1)} %own_ref.1, f32[1,768]{1,0:T(1,128)} %broadcast_in_dim.124.gain_ref), custom_call_target="tpu_custom_call" | custom-call | flops 5500000256 | bytes 5000000 | tf_op jit(solution)/shard_map/token_norm/pallas_call | solution.py:792
  41.8 4.8 %collective-permute-start.7 = (bf16[4,16,896]{2,1,0:T(8,128)(2,1)S(1)}, bf16[4,16,896]{2,1,0:T(8,128)(2,1)S(1)}, u32[]{:S(2)}, u32[]{:S(2)}) collective-permute-start(bf16[4,16,896]{2,1,0:T(8,128)(2,1)S(1)} %copy-done.36), channel_id=1, source_target_pairs={{0,20},{4,0},{8,16},{12,4},{16,28},{20,8},{24,24},{28,12},{1,21},{... | collective-permute-start | bytes 344072 | tf_op jit(solution)/shard_map/ppermute | solution.py:761
  46.7 5.8 %token_norm.3.tok_ref = bf16[4,1024,768]{2,1,0:T(8,128)(2,1)} custom-call(s32[4]{0:T(128)} %add_add_fusion.1.s_ref, bf16[4,512,768]{2,1,0:T(8,128)(2,1)} %collective-permute-done.1.tok_ref.other_ref, f32[1,768]{1,0:T(1,128)} %broadcast_in_dim.124.gain_ref, bf16[4,1024,768]{2,1,0:T(8,128)(2,1)} %token_norm.2.refs_0_), custom_call_target="tpu_custom_call", output_to_operand_aliasing={{}: (3, {})} | custom-call | flops 5500000256 | bytes 5000000 | tf_op jit(solution)/shard_map/token_norm/pallas_call | solution.py:792
  53.7 6.6 %collective-permute-start.11 = (bf16[2,192,768]{2,1,0:T(8,128)(2,1)}, bf16[2,192,768]{2,1,0:T(8,128)(2,1)S(1)}, u32[]{:S(2)}, u32[]{:S(2)}) collective-permute-start(bf16[2,192,768]{2,1,0:T(8,128)(2,1)} %constant_dynamic-slice_fusion.5), channel_id=1, source_target_pairs={{0,3},{4,7},{8,11},{12,15},{16,19},{20,23},{24,27},{28,31}} | collective-permute-start | bytes 1769480 | tf_op jit(solution)/shard_map/ppermute | solution.py:846
  67.6 27.4 %attention_forward.2 = (bf16[4,128,768]{2,1,0:T(8,128)(2,1)}, bf16[4,1088,768]{2,1,0:T(8,128)(2,1)}, bf16[4,1088,768]{2,1,0:T(8,128)(2,1)}, f32[4,2,8,256]{3,2,1,0:T(8,128)}, f32[4,128,768]{2,1,0:T(8,128)}) custom-call(s32[4]{0:T(128)} %add_add_fusion.1.s_ref, bf16[4,1024,768]{2,1,0:T(8,128)(2,1)} %token_norm.3.tok_ref, bf16[4,64,896]{2,1,0:T(8,128)(2,1)} %copy-done.27, ...), custom_call_target="tpu_custom_call" | custom-call | flops 25300000768 | bytes 23000000 | tf_op jit(solution)/shard_map/attention_forward/pallas_call | solution.py:792
  105.3 27.4 %attention_forward.3 = (bf16[4,128,768]{2,1,0:T(8,128)(2,1)}, bf16[4,1088,768]{2,1,0:T(8,128)(2,1)}, bf16[4,1088,768]{2,1,0:T(8,128)(2,1)}, f32[4,2,8,256]{3,2,1,0:T(8,128)}, f32[4,128,768]{2,1,0:T(8,128)}) custom-call(s32[4]{0:T(128)} %add_add_fusion.s_ref, ...), custom_call_target="tpu_custom_call", output_to_operand_aliasing={{0}: (8, {}), {1}: (9, {}), {2}: (10, {}), {3}: (11, {}), {... | custom-call | flops 25300000768 | bytes 23000000 | tf_op jit(solution)/shard_map/attention_forward/pallas_call | solution.py:792
  136.3 3.9 %multiply_convert_fusion.1 = (bf16[4,128,768]{2,1,0:T(8,128)(2,1)S(1)}, f32[4,128,768]{2,1,0:T(8,128)S(1)}, f32[4,128,768]{2,1,0:T(8,128)S(1)}) fusion(bf16[768,768]{1,0:T(8,128)(2,1)S(1)} %copy-done, f32[4,128,768]{2,1,0:T(8,128)S(1)} %get-tuple-element.137, f32[768]{0:T(1024)S(1)} %copy-done.39, f32[4,128]{1,0:T(4,128)S(1)} %add_rsqrt_fusion, ...), kind=kOutput, calls=%fused_computation.19 | convolution fusion | flops 631111680 | bytes 6691840 | tf_op jit(solution)/shard_map/bld,df->blf/dot_general | solution.py:725
  144.5 3.6 %collective-permute-start.14 = (bf16[128,768]{1,0:T(8,128)(2,1)S(1)}, bf16[128,768]{1,0:T(8,128)(2,1)S(1)}, u32[]{:S(2)}, u32[]{:S(2)}) collective-permute-start(bf16[128,768]{1,0:T(8,128)(2,1)S(1)} %get-tuple-element.154), channel_id=1, source_target_pairs={{0,3},{1,0},{2,1},{3,2},{4,7},{5,4},{6,5},{7,6},{8,11},{9,8},{10,9... | collective-permute-start | bytes 589832 | tf_op jit(solution)/shard_map/ppermute | solution.py:397
  151.3 2.6 broadcast_in_dim.136
  155.5 11.5 %collective-permute-done.15 = bf16[128,768]{1,0:T(8,128)(2,1)S(1)} collective-permute-done((bf16[128,768]{1,0:T(8,128)(2,1)S(1)}, bf16[128,768]{1,0:T(8,128)(2,1)S(1)}, u32[]{:S(2)}, u32[]{:S(2)}) %collective-permute-start.15) | collective-permute-done | bytes 196640 | tf_op jit(solution)/shard_map/ppermute | solution.py:397
  173.9 12.6 %collective-permute-done.18 = bf16[128,768]{1,0:T(8,128)(2,1)S(1)} collective-permute-done((bf16[128,768]{1,0:T(8,128)(2,1)S(1)}, bf16[128,768]{1,0:T(8,128)(2,1)S(1)}, u32[]{:S(2)}, u32[]{:S(2)}) %collective-permute-start.18) | collective-permute-done | bytes 196640 | tf_op jit(solution)/shard_map/ppermute | solution.py:397
  199.8 55.6 %attention_backward.1 = (f32[8,512,768]{2,1,0:T(8,128)}, bf16[4,576,768]{2,1,0:T(8,128)(2,1)}, bf16[4,64,768]{2,1,0:T(8,128)(2,1)}, f32[8,64,768]{2,1,0:T(8,128)}, bf16[896,768]{1,0:T(8,128)(2,1)}) custom-call(s32[4]{0:T(128)} %add_add_fusion.1.s_ref, bf16[4,128,768]{2,1,0:T(8,128)(2,1)} %get-tuple-element.98.q_ref, ...), custom_call_target="tpu_custom_call" | custom-call | flops 3300000000 | bytes 3000000 | tf_op jit(solution)/shard_map/attention_backward/pallas_call | solution.py:792
  258.8 4.1 %collective-permute-done.24 = bf16[448,768]{1,0:T(8,128)(2,1)S(1)} collective-permute-done((bf16[448,768]{1,0:T(8,128)(2,1)}, bf16[448,768]{1,0:T(8,128)(2,1)S(1)}, u32[]{:S(2)}, u32[]{:S(2)}) %collective-permute-start.24) | collective-permute-done | bytes 688160 | tf_op jit(solution)/shard_map/ppermute | solution.py:393
  267.1 12.6 %collective-permute-start.34 = (bf16[4,16,768]{2,1,0:T(8,128)(2,1)S(1)}, bf16[4,16,768]{2,1,0:T(8,128)(2,1)S(1)}, u32[]{:S(2)}, u32[]{:S(2)}) collective-permute-start(bf16[4,16,768]{2,1,0:T(8,128)(2,1)S(1)} %get-tuple-element.168), channel_id=1, source_target_pairs={{16,0},{4,4},{20,8},{0,12},{24,16},{12,20},{28,24},{8,28},{17,1},{... | collective-permute-start | bytes 294920 | tf_op jit(solution)/shard_map/ppermute | solution.py:1036
  282.7 3.8 %collective-permute-done.35 = bf16[4,16,768]{2,1,0:T(8,128)(2,1)S(1)} collective-permute-done((bf16[4,16,768]{2,1,0:T(8,128)(2,1)S(1)}, bf16[4,16,768]{2,1,0:T(8,128)(2,1)S(1)}, u32[]{:S(2)}, u32[]{:S(2)}) %collective-permute-start.35) | collective-permute-done | bytes 98336 | tf_op jit(solution)/shard_map/ppermute | solution.py:1036
  289.1 3.3 collective-permute-done.36
  297.7 3.3 collective-permute-done.32
  302.7 11.7 %collective-permute-done.26 = bf16[128,768]{1,0:T(8,128)(2,1)S(1)} collective-permute-done((bf16[128,768]{1,0:T(8,128)(2,1)S(1)}, bf16[128,768]{1,0:T(8,128)(2,1)S(1)}, u32[]{:S(2)}, u32[]{:S(2)}) %collective-permute-start.26) | collective-permute-done | bytes 196640 | tf_op jit(solution)/shard_map/ppermute | solution.py:397
  314.5 7.6 %place_rows.1 = (f32[8,512,768]{2,1,0:T(8,128)}, f32[8,64,768]{2,1,0:T(8,128)}) custom-call(s32[4]{0:T(128)} %add_add_fusion.1.s_ref, f32[8,512,768]{2,1,0:T(8,128)} %get-tuple-element.110.video_in, f32[8,64,768]{2,1,0:T(8,128)} %get-tuple-element.111.lat_in, ...), custom_call_target="tpu_custom_call", output_to_operand_aliasing={{0}: (1, {}), {1}: (2, {})} | custom-call | flops 6000000000 | bytes 10000000 | tf_op jit(solution)/shard_map/place_rows/pallas_call | solution.py:991
  326.3 3.5 %collective-permute-done.37 = bf16[112,768]{1,0:T(8,128)(2,1)S(1)} collective-permute-done((bf16[112,768]{1,0:T(8,128)(2,1)}, bf16[112,768]{1,0:T(8,128)(2,1)S(1)}, u32[]{:S(2)}, u32[]{:S(2)}) %collective-permute-start.37) | collective-permute-done | bytes 172064 | tf_op jit(solution)/shard_map/ppermute | solution.py:450
  329.9 4.1 %collective-permute-done.38 = bf16[112,768]{1,0:T(8,128)(2,1)S(1)} collective-permute-done((bf16[112,768]{1,0:T(8,128)(2,1)S(1)}, bf16[112,768]{1,0:T(8,128)(2,1)S(1)}, u32[]{:S(2)}, u32[]{:S(2)}) %collective-permute-start.38) | collective-permute-done | bytes 172064 | tf_op jit(solution)/shard_map/ppermute | solution.py:450
  334.8 3.8 %select_convert_fusion = (f32[768,768]{1,0:T(8,128)}, f32[768,768]{1,0:T(8,128)}) fusion(bf16[768,768]{1,0:T(8,128)(2,1)} %collective-permute-done.41, bf16[768,768]{1,0:T(8,128)(2,1)S(1)} %copy-done.18, pred[]{:T(512)S(6)} %eq.57), kind=kLoop, calls=%fused_computation.53 | loop fusion | flops 2359296 | bytes 7077889 | tf_op jit(solution)/shard_map/convert_element_type | solution.py:1064
  (264 shorter events, 100.8 us)
Async XLA Ops:
  7.2 249.1 %all-reduce.2.cloned.1.call-start = ((), (), s32[]{:S(2)}) async-start(), calls=%async_computation | async-start | bytes 2359296 | tf_op jit(solution)/shard_map/psum | solution.py:920
  11.2 30.6 %collective-permute-start.1 = (bf16[4,512,768]{2,1,0:T(8,128)(2,1)}, bf16[4,512,768]{2,1,0:T(8,128)(2,1)}, u32[]{:S(2)}, u32[]{:S(2)}) collective-permute-start(bf16[4,512,768]{2,1,0:T(8,128)(2,1)} %constant_dynamic-slice_fusion.6), channel_id=1, source_target_pairs={{0,16},{16,0},{1,17},{17,1},{2,18},{18,2},{3,19},{19,3},{4,20},{20... | collective-permute-start | bytes 9437192 | tf_op jit(solution)/shard_map/ppermute | solution.py:393
  12.8 39.7 %collective-permute-start.2 = (bf16[2,192,768]{2,1,0:T(8,128)(2,1)}, bf16[2,192,768]{2,1,0:T(8,128)(2,1)S(1)}, u32[]{:S(2)}, u32[]{:S(2)}) collective-permute-start(bf16[2,192,768]{2,1,0:T(8,128)(2,1)} %constant_dynamic-slice_fusion.5), channel_id=1, source_target_pairs={{0,1},{1,2},{2,3},{4,5},{5,6},{6,7},{8,9},{9,10},{10,11},{12,13},{... | collective-permute-start | bytes 1769480 | tf_op jit(solution)/shard_map/ppermute | solution.py:729
  17.3 35.2 %collective-permute-start.3 = (bf16[2,192,768]{2,1,0:T(8,128)(2,1)}, bf16[2,192,768]{2,1,0:T(8,128)(2,1)S(1)}, u32[]{:S(2)}, u32[]{:S(2)}) collective-permute-start(bf16[2,192,768]{2,1,0:T(8,128)(2,1)} %constant_dynamic-slice_fusion.5), channel_id=1, source_target_pairs={{1,0},{2,1},{3,2},{5,4},{6,5},{7,6},{9,8},{10,9},{11,10},{13,12},{... | collective-permute-start | bytes 1769480 | tf_op jit(solution)/shard_map/ppermute | solution.py:730
  20.7 21.0 %collective-permute-start.4 = (bf16[4,16,896]{2,1,0:T(8,128)(2,1)}, bf16[4,16,896]{2,1,0:T(8,128)(2,1)}, u32[]{:S(2)}, u32[]{:S(2)}) collective-permute-start(bf16[4,16,896]{2,1,0:T(8,128)(2,1)} %get-tuple-element.163), channel_id=1, source_target_pairs={{0,0},{4,16},{8,4},{12,20},{16,8},{20,24},{24,12},{28,28},{1,1},{5... | collective-permute-start | bytes 344072 | tf_op jit(solution)/shard_map/ppermute | solution.py:761
  38.9 13.6 %collective-permute-start.5 = (bf16[4,16,896]{2,1,0:T(8,128)(2,1)S(1)}, bf16[4,16,896]{2,1,0:T(8,128)(2,1)S(1)}, u32[]{:S(2)}, u32[]{:S(2)}) collective-permute-start(bf16[4,16,896]{2,1,0:T(8,128)(2,1)S(1)} %copy-done.38), channel_id=1, source_target_pairs={{0,16},{4,4},{8,20},{12,0},{16,24},{20,12},{24,28},{28,8},{1,17},{... | collective-permute-start | bytes 344072 | tf_op jit(solution)/shard_map/ppermute | solution.py:761
  53.7 41.2 %collective-permute-start.11 = (bf16[2,192,768]{2,1,0:T(8,128)(2,1)}, bf16[2,192,768]{2,1,0:T(8,128)(2,1)S(1)}, u32[]{:S(2)}, u32[]{:S(2)}) collective-permute-start(bf16[2,192,768]{2,1,0:T(8,128)(2,1)} %constant_dynamic-slice_fusion.5), channel_id=1, source_target_pairs={{0,3},{4,7},{8,11},{12,15},{16,19},{20,23},{24,27},{28,31}} | collective-permute-start | bytes 1769480 | tf_op jit(solution)/shard_map/ppermute | solution.py:846
  60.3 34.6 %collective-permute-start.12 = (bf16[2,192,768]{2,1,0:T(8,128)(2,1)}, bf16[2,192,768]{2,1,0:T(8,128)(2,1)S(1)}, u32[]{:S(2)}, u32[]{:S(2)}) collective-permute-start(bf16[2,192,768]{2,1,0:T(8,128)(2,1)} %constant_dynamic-slice_fusion.5), channel_id=1, source_target_pairs={{3,0},{7,4},{11,8},{15,12},{19,16},{23,20},{27,24},{31,28}} | collective-permute-start | bytes 1769480 | tf_op jit(solution)/shard_map/ppermute | solution.py:847
  61.6 33.3 %collective-permute-start.10 = (bf16[2,192,768]{2,1,0:T(8,128)(2,1)S(1)}, bf16[2,192,768]{2,1,0:T(8,128)(2,1)S(1)}, u32[]{:S(2)}, u32[]{:S(2)}) collective-permute-start(bf16[2,192,768]{2,1,0:T(8,128)(2,1)S(1)} %collective-permute-done.3), channel_id=1, source_target_pairs={{1,0},{2,1},{5,4},{6,5},{9,8},{10,9},{13,12},{14,13},{17,16},{18,1... | collective-permute-start | bytes 1769480 | tf_op jit(solution)/shard_map/ppermute | solution.py:845
  62.9 32.0 %collective-permute-start.9 = (bf16[2,192,768]{2,1,0:T(8,128)(2,1)S(1)}, bf16[2,192,768]{2,1,0:T(8,128)(2,1)}, u32[]{:S(2)}, u32[]{:S(2)}) collective-permute-start(bf16[2,192,768]{2,1,0:T(8,128)(2,1)S(1)} %collective-permute-done.2), channel_id=1, source_target_pairs={{1,2},{2,3},{5,6},{6,7},{9,10},{10,11},{13,14},{14,15},{17,18},{18... | collective-permute-start | bytes 1769480 | tf_op jit(solution)/shard_map/ppermute | solution.py:844
  144.0 42.5 %collective-permute-start.20 = (bf16[768,768]{1,0:T(8,128)(2,1)S(1)}, bf16[768,768]{1,0:T(8,128)(2,1)S(1)}, u32[]{:S(2)}, u32[]{:S(2)}) collective-permute-start(bf16[768,768]{1,0:T(8,128)(2,1)S(1)} %get-tuple-element.171), channel_id=1, source_target_pairs={{0,16},{16,0},{1,17},{17,1},{2,18},{18,2},{3,19},{19,3},{4,20},{20... | collective-permute-start | bytes 3538952 | tf_op jit(solution)/shard_map/ppermute | solution.py:393
  148.1 18.9 %collective-permute-start.15 = (bf16[128,768]{1,0:T(8,128)(2,1)S(1)}, bf16[128,768]{1,0:T(8,128)(2,1)S(1)}, u32[]{:S(2)}, u32[]{:S(2)}) collective-permute-start(bf16[128,768]{1,0:T(8,128)(2,1)S(1)} %get-tuple-element.156), channel_id=1, source_target_pairs={{0,2},{1,3},{2,0},{3,1},{4,6},{5,7},{6,4},{7,5},{8,10},{9,11},{10,... | collective-permute-start | bytes 589832 | tf_op jit(solution)/shard_map/ppermute | solution.py:397
  149.4 17.7 %collective-permute-start.16 = (bf16[128,768]{1,0:T(8,128)(2,1)S(1)}, bf16[128,768]{1,0:T(8,128)(2,1)S(1)}, u32[]{:S(2)}, u32[]{:S(2)}) collective-permute-start(bf16[128,768]{1,0:T(8,128)(2,1)S(1)} %get-tuple-element.155), channel_id=1, source_target_pairs={{0,1},{1,2},{2,3},{3,0},{4,5},{5,6},{6,7},{7,4},{8,9},{9,10},{10,1... | collective-permute-start | bytes 589832 | tf_op jit(solution)/shard_map/ppermute | solution.py:397
  168.9 17.6 %collective-permute-start.18 = (bf16[128,768]{1,0:T(8,128)(2,1)S(1)}, bf16[128,768]{1,0:T(8,128)(2,1)S(1)}, u32[]{:S(2)}, u32[]{:S(2)}) collective-permute-start(bf16[128,768]{1,0:T(8,128)(2,1)S(1)} %get-tuple-element.133), channel_id=1, source_target_pairs={{0,2},{1,3},{2,0},{3,1},{4,6},{5,7},{6,4},{7,5},{8,10},{9,11},{10,... | collective-permute-start | bytes 589832 | tf_op jit(solution)/shard_map/ppermute | solution.py:397
  170.3 16.1 %collective-permute-start.19 = (bf16[128,768]{1,0:T(8,128)(2,1)S(1)}, bf16[128,768]{1,0:T(8,128)(2,1)S(1)}, u32[]{:S(2)}, u32[]{:S(2)}) collective-permute-start(bf16[128,768]{1,0:T(8,128)(2,1)S(1)} %get-tuple-element.133), channel_id=1, source_target_pairs={{0,1},{1,2},{2,3},{3,0},{4,5},{5,6},{6,7},{7,4},{8,9},{9,10},{10,1... | collective-permute-start | bytes 589832 | tf_op jit(solution)/shard_map/ppermute | solution.py:397
  196.9 58.5 %collective-permute-start.21 = (bf16[128,768]{1,0:T(8,128)(2,1)S(1)}, bf16[128,768]{1,0:T(8,128)(2,1)S(1)}, u32[]{:S(2)}, u32[]{:S(2)}) collective-permute-start(bf16[128,768]{1,0:T(8,128)(2,1)S(1)} %get-tuple-element.151), channel_id=1, source_target_pairs={{0,3},{1,0},{2,1},{3,2},{4,7},{5,4},{6,5},{7,6},{8,11},{9,8},{10,9... | collective-permute-start | bytes 589832 | tf_op jit(solution)/shard_map/ppermute | solution.py:397
  197.0 58.5 %collective-permute-start.22 = (bf16[128,768]{1,0:T(8,128)(2,1)S(1)}, bf16[128,768]{1,0:T(8,128)(2,1)S(1)}, u32[]{:S(2)}, u32[]{:S(2)}) collective-permute-start(bf16[128,768]{1,0:T(8,128)(2,1)S(1)} %get-tuple-element.153), channel_id=1, source_target_pairs={{0,2},{1,3},{2,0},{3,1},{4,6},{5,7},{6,4},{7,5},{8,10},{9,11},{10,... | collective-permute-start | bytes 589832 | tf_op jit(solution)/shard_map/ppermute | solution.py:397
  197.9 57.6 %collective-permute-start.23 = (bf16[128,768]{1,0:T(8,128)(2,1)S(1)}, bf16[128,768]{1,0:T(8,128)(2,1)S(1)}, u32[]{:S(2)}, u32[]{:S(2)}) collective-permute-start(bf16[128,768]{1,0:T(8,128)(2,1)S(1)} %get-tuple-element.152), channel_id=1, source_target_pairs={{0,1},{1,2},{2,3},{3,0},{4,5},{5,6},{6,7},{7,4},{8,9},{9,10},{10,1... | collective-permute-start | bytes 589832 | tf_op jit(solution)/shard_map/ppermute | solution.py:397
  255.4 59.1 %collective-permute-start.29 = (bf16[4,576,768]{2,1,0:T(8,128)(2,1)}, bf16[4,576,768]{2,1,0:T(8,128)(2,1)}, u32[]{:S(2)}, u32[]{:S(2)}) collective-permute-start(bf16[4,576,768]{2,1,0:T(8,128)(2,1)} %get-tuple-element.112), channel_id=1, source_target_pairs={{0,16},{16,0},{1,17},{17,1},{2,18},{18,2},{3,19},{19,3},{4,20},{20... | collective-permute-start | bytes 10616840 | tf_op jit(solution)/shard_map/ppermute | solution.py:393
  258.7 76.1 %collective-permute-start.41 = (bf16[768,768]{1,0:T(8,128)(2,1)}, bf16[768,768]{1,0:T(8,128)(2,1)}, u32[]{:S(2)}, u32[]{:S(2)}) collective-permute-start(bf16[768,768]{1,0:T(8,128)(2,1)} %all-reduce.2.cloned.1.call-done), channel_id=1, source_target_pairs={{0,16},{16,0},{1,17},{17,1},{2,18},{18,2},{3,19},{19,3},{4,20},{20... | collective-permute-start | bytes 3538952 | tf_op jit(solution)/shard_map/ppermute | solution.py:393
  264.2 31.3 %collective-permute-start.30 = (bf16[112,768]{1,0:T(8,128)(2,1)S(1)}, bf16[112,768]{1,0:T(8,128)(2,1)S(1)}, u32[]{:S(2)}, u32[]{:S(2)}) collective-permute-start(bf16[112,768]{1,0:T(8,128)(2,1)S(1)} %get-tuple-element.159), channel_id=1, source_target_pairs={{0,12},{4,0},{8,4},{12,8},{1,13},{5,1},{9,5},{13,9},{2,14},{6,2},{... | collective-permute-start | bytes 516104 | tf_op jit(solution)/shard_map/ppermute | solution.py:439
  265.8 31.6 %collective-permute-start.31 = (bf16[112,768]{1,0:T(8,128)(2,1)S(1)}, bf16[112,768]{1,0:T(8,128)(2,1)S(1)}, u32[]{:S(2)}, u32[]{:S(2)}) collective-permute-start(bf16[112,768]{1,0:T(8,128)(2,1)S(1)} %get-tuple-element.161), channel_id=1, source_target_pairs={{0,8},{4,12},{8,0},{12,4},{1,9},{5,13},{9,1},{13,5},{2,10},{6,14},... | collective-permute-start | bytes 516104 | tf_op jit(solution)/shard_map/ppermute | solution.py:439
  267.1 14.8 %collective-permute-start.34 = (bf16[4,16,768]{2,1,0:T(8,128)(2,1)S(1)}, bf16[4,16,768]{2,1,0:T(8,128)(2,1)S(1)}, u32[]{:S(2)}, u32[]{:S(2)}) collective-permute-start(bf16[4,16,768]{2,1,0:T(8,128)(2,1)S(1)} %get-tuple-element.168), channel_id=1, source_target_pairs={{16,0},{4,4},{20,8},{0,12},{24,16},{12,20},{28,24},{8,28},{17,1},{... | collective-permute-start | bytes 294920 | tf_op jit(solution)/shard_map/ppermute | solution.py:1036
  297.4 17.0 %collective-permute-start.26 = (bf16[128,768]{1,0:T(8,128)(2,1)S(1)}, bf16[128,768]{1,0:T(8,128)(2,1)S(1)}, u32[]{:S(2)}, u32[]{:S(2)}) collective-permute-start(bf16[128,768]{1,0:T(8,128)(2,1)S(1)} %copy-done.25), channel_id=1, source_target_pairs={{0,2},{1,3},{2,0},{3,1},{4,6},{5,7},{6,4},{7,5},{8,10},{9,11},{10,... | collective-permute-start | bytes 589832 | tf_op jit(solution)/shard_map/ppermute | solution.py:397
  (66 other events, 480.5 us)
Sparse Core Ops, SparseCore 0:
  193.8 51.9 all-reduce.1

commit v2 on v1

--- a/solution.py
+++ b/solution.py
@@ -440,16 +440,20 @@
     return total.astype(BF16)
 
 
-def gather_group(total, core, place, count):
+def gather_places(total, place, count):
     part = total.shape[0]
-    half = part * count
-    mine = jnp.zeros((half, total.shape[1]), BF16)
+    mine = jnp.zeros((part * count, total.shape[1]), BF16)
     mine = lax.dynamic_update_slice_in_dim(mine, total, place * part, 0)
     for step, perm in group_steps(count):
         mine = lax.dynamic_update_slice_in_dim(
             mine, lax.ppermute(total, "txt", perm), (place + step) % count * part, 0
         )
-    whole = jnp.zeros((2 * half, total.shape[1]), BF16)
+    return mine
+
+
+def gather_cores(mine, core):
+    half = mine.shape[0]
+    whole = jnp.zeros((2 * half, mine.shape[1]), BF16)
     whole = lax.dynamic_update_slice_in_dim(whole, mine, core * half, 0)
     return lax.dynamic_update_slice_in_dim(whole, swap_cores(mine), (1 - core) * half, 0)
 
@@ -503,12 +507,20 @@
     return [(start, size) for start in range(0, video, size)] + [(video, cap)]
 
 
-def norm_kernel(s_ref, tok_ref, gain_ref, *refs):
+def norm_kernel(s_ref, own_ref, other_ref, gain_ref, out_ref):
     gain = gain_ref[...]
-    out_ref = refs[-1]
-    for at in range(0, tok_ref.shape[0], 64):
-        rows = pl.ds(at, 64)
-        out_ref[rows, :] = layer_norm(tok_ref[rows, :].astype(F32), gain).astype(BF16)
+    start = 0
+    for ref in (own_ref, other_ref):
+        def chunk(c, carry, ref=ref, start=start):
+            for part in range(2):
+                at = pl.multiple_of(c * 128, 128) + 64 * part
+                out_ref[pl.ds(start + at, 64), :] = layer_norm(
+                    ref[pl.ds(at, 64), :].astype(F32), gain
+                ).astype(BF16)
+            return carry
+
+        lax.fori_loop(0, ref.shape[0] // 128, chunk, 0)
+        start += ref.shape[0]
 
 
 def cap_mask(cap_ref):
@@ -813,38 +825,25 @@
     gain_lat_row = gain_latent[None]
     gain_tok_row = gain_tokens[None]
     gain_mlp_row = gain_mlp[None]
-    def token_norm(part, spec, tokens, before=()):
-        return call(
-            norm_kernel,
-            "token_norm",
-            [spec, row_spec] + [pl.BlockSpec(memory_space=pl.ANY)] * len(before),
-            [
-                (
-                    pl.BlockSpec((None, video_here, D), lambda i, s: (i, part, 0)),
-                    (own, 2 * video_here, D),
-                    BF16,
-                )
-            ],
-            (tokens, gain_tok_row) + tuple(before),
-            5,
-            aliases={3: 0} if before else {},
-        )
-
-    tok_norm = token_norm(0, own_spec(video_here), video_tokens)
-    (tok_norm,) = token_norm(1, item_spec(video_here), video_other, tok_norm)
+    (tok_norm,) = call(
+        norm_kernel,
+        "token_norm",
+        [own_spec(video_here), item_spec(video_here), row_spec],
+        [item_out(2 * video_here, BF16)],
+        (video_tokens, video_other, gain_tok_row),
+        9,
+    )
     tok_norm, up1, down1, cap_parts = lax.optimization_barrier((tok_norm, up1, down1, cap_parts))
     cap = jnp.concatenate(cap_parts, axis=1)
     partner = jnp.where(z % 2 == 1, up1, down1)
     near = jnp.zeros(part_shape, BF16)
     near = place_chunk(near, packed.reshape((2, 2) + packed.shape[1:]), zero, own_at)
     near = place_chunk(near, partner, core, 1 - own_at)
-    near = place_chunk(near, swap_cores(partner), 1 - core, 1 - own_at)
-
-    half_then, _ = lax.optimization_barrier((half, up1))
-    up2 = lax.ppermute(up1, "head", [(1, 2), (2, 3)])
-    down2 = lax.ppermute(down1, "head", [(1, 0), (2, 1)])
-    up3 = lax.ppermute(half_then, "head", [(0, 3)])
-    down3 = lax.ppermute(half_then, "head", [(3, 0)])
+    partner_other = swap_cores(partner)
+    near = place_chunk(near, partner_other, 1 - core, 1 - own_at)
+    up1, down1, half_then, _ = lax.optimization_barrier((up1, down1, half, partner_other))
+    ring_up = lax.ppermute(jnp.where(z == 3, half_then, up1), "head", [(1, 2), (2, 3), (3, 0)])
+    ring_down = lax.ppermute(jnp.where(z == 0, half_then, down1), "head", [(1, 0), (2, 1), (0, 3)])
 
     def forward(part, scalars, before=()):
         return call(
@@ -877,15 +876,12 @@
         )
 
     before = forward(near, scalars)
-    before, up2, down2, up3, down3 = lax.optimization_barrier((before, up2, down2, up3, down3))
-
-    def by_place(*choices):
-        low = jnp.where(z == 0, choices[0], choices[1])
-        return jnp.where(z < 2, low, jnp.where(z == 2, choices[2], choices[3]))
-
-    far_mine = jnp.stack(
-        [by_place(down2, down1, up2, up3), by_place(down3, down2, up1, up2)], axis=1
-    )
+    before, up1, down1, ring_up, ring_down = lax.optimization_barrier(
+        (before, up1, down1, ring_up, ring_down)
+    )
+    far_low = jnp.where(z == 1, down1, jnp.where(z == 2, ring_up, ring_down))
+    far_high = jnp.where(z == 1, ring_down, jnp.where(z == 2, up1, ring_up))
+    far_mine = jnp.stack([far_low, far_high], axis=1)
     far = jnp.zeros(part_shape, BF16)
     far = lax.dynamic_update_index_in_dim(far, far_mine, core, 0)
     far = lax.dynamic_update_index_in_dim(far, swap_cores(far_mine), 1 - core, 0)
@@ -914,11 +910,12 @@
     weights = both_halves(near, far)
     early = jnp.where(core == 0, grad_up, grad_down).astype(F32)
     early = early + swap_cores(jnp.where(core == 0, grad_down, grad_up)).astype(F32)
-    activ, d_mlp_norm, early, weights = lax.optimization_barrier(
-        (activ, d_mlp_norm, early.astype(BF16), weights)
+    growth = dot("blf,fd->bld", activ, down_weight)
+    growth, d_mlp_norm, early, weights = lax.optimization_barrier(
+        (growth, d_mlp_norm, early.astype(BF16), weights)
     )
     early = lax.psum(early, "txt")
-    growth = reduce_over_head(dot("blf,fd->bld", activ, down_weight), z, head_count)
+    growth = reduce_over_head(growth, z, head_count)
 
     d_after_norm, gain_mlp_part = norm_back_rows(after_attn, gain_mlp, d_mlp_norm.astype(F32))
     d_after = cot.astype(F32) + d_after_norm
@@ -1017,30 +1014,33 @@
 
     growth, early, late = lax.optimization_barrier((growth, early, late))
     late_half, late_swapped = reduce_over_cores(late, core)
+    other_back, early, _ = lax.optimization_barrier((other_back, early, late_swapped))
     other_here = swap_cores(other_back)
-    cap_back, _ = lax.optimization_barrier((cap_back, late_swapped))
+    early_other = swap_cores(early)
     late_total = reduce_over_group(late_half, place_index, txt_count)
-    early_other = swap_cores(early)
-    other_here, _ = lax.optimization_barrier((other_here, late_half))
-    growth, _ = lax.optimization_barrier((growth, late_swapped))
+    late_total, growth, early_other, other_here, cap_back = lax.optimization_barrier(
+        (late_total, growth, early_other, other_here, cap_back)
+    )
     growth = gather_head(growth, z, head_count)
-    video_grad, latent_grad = place(video_grad, latent_grad, other_here)
-    video_grad, latent_grad, late_total = lax.optimization_barrier(
-        (video_grad, latent_grad, late_total)
-    )
-    late = gather_group(late_total, core, place_index, txt_count).astype(F32)
-    out_mine = (after_attn + growth.astype(F32)).astype(BF16)
-    caption_grad = jnp.zeros((txt_count, own, cap_here, D), F32)
+    cap_parts = []
     for step in range(txt_count):
         perm = [(b, a) for a, b in caption_perm(step, 2, txt_count, 2)]
-        part = lax.ppermute(
-            cap_back[:, step * cap_here : (step + 1) * cap_here], ("vid", "txt"), perm
-        )
+        cap_parts.append(
+            lax.ppermute(cap_back[:, step * cap_here : (step + 1) * cap_here], ("vid", "txt"), perm)
+        )
+    late = gather_places(late_total, place_index, txt_count)
+    video_grad, latent_grad = place(video_grad, latent_grad, other_here)
+    late, video_grad, latent_grad, cap_parts, growth = lax.optimization_barrier(
+        (late, video_grad, latent_grad, cap_parts, growth)
+    )
+    late = gather_cores(late, core).astype(F32)
+    caption_grad = jnp.zeros((txt_count, own, cap_here, D), F32)
+    for step, part in enumerate(cap_parts):
         caption_grad = lax.dynamic_update_index_in_dim(
             caption_grad, part.astype(F32), (place_index + step) % txt_count, 0
         )
     caption_grad = caption_grad.reshape(caption_tokens.shape)
-
+    out_mine = (after_attn + growth.reshape(after_attn.shape).astype(F32)).astype(BF16)
     gains = late[4 * head_width :]
 
     def give_back(values):

time: 353 us -> 323 us (0.915)
  waiting for transfers between devices: 60.2 us -> 37.4 us
  starting transfers between devices: 69.3 us -> 63.3 us
  local copies, waits for them, and re-layouts: 38.1 us -> 34.1 us
    ppermute x12, waiting for transfers between devices: 37.5 us -> 24 us  [head_shift(): lax.ppermute(values, 'head', [(i, (i - shift) % count) for i in range(cou...]
    ppermute x7 -> x5, waiting for transfers between devices: 7.6 us -> 0.01 us  [the longest x3 0.01 us: gather_places(): lax.ppermute(total, 'txt', perm)]
    ppermute x4, waiting for transfers between devices: 7.63 us -> 1.18 us  [local(): lax.ppermute(cap_back[:, step * cap_here:(step + 1) * cap_here], ('vid',...]
    unnamed x98 -> x94, local copies, waits for them, and re-layouts: 12.7 us -> 7.72 us
    ppermute x4, starting transfers between devices: 15.3 us -> 10.3 us  [local(): lax.ppermute(cap_back[:, step * cap_here:(step + 1) * cap_here], ('vid',...]
    ppermute x3, waiting for transfers between devices: 3.33 us -> 8.02 us  [reduce_over_group(): total = total + lax.ppermute(chunk, 'txt', perm).astype(F32)]
    ppermute x7 -> x5, starting transfers between devices: 14.6 us -> 11.1 us  [the longest x1 7.17 us: local(): lax.ppermute(jnp.where(z == 0, half_then, down1), 'head', [(1, 0), (2, 1)...]
    pallas_call x5 -> x4, Pallas kernels: 122 us -> 121 us  [call(): pl.pallas_call(kernel, name=name, grid_spec=pltpu.PrefetchScalarGridSpec(...]
  transfers between devices with their start and end apart: 43 -> 41, of which waited for: 12 -> 11; matrix products, arithmetic and copies ran while one was open for 11% -> 13% of each run, Pallas kernels for 29% -> 32%
where the time goes in v2:
time: 323 us; the launch traced here: 321 us
  Pallas kernels  129 us (40%)
  starting transfers between devices  63.3 us (20%)
  waiting for transfers between devices  37.4 us (12%)
  local copies, waits for them, and re-layouts  34.1 us (11%)
  other arithmetic  26.7 us (8%)
  between operations  17 us (5%)
  matrix products  14 us (4%)
    pallas_call x4, Pallas kernels, call(): pl.pallas_call(kernel, name=name, grid_spec=pltpu.PrefetchScalarGridSpec(...  121 us
    ppermute x12, waiting for transfers between devices, head_shift(): lax.ppermute(values, 'head', [(i, (i - shift) % count) for i in range(cou...  24 us
    ppermute x12, starting transfers between devices, head_shift(): lax.ppermute(values, 'head', [(i, (i - shift) % count) for i in range(cou...  17.7 us
    dot_general x9, matrix products, dot(): return jnp.einsum(spec, a, b, preferred_element_type=F32)  14 us
    ppermute x4, starting transfers between devices, local(): lax.ppermute(cap_back[:, step * cap_here:(step + 1) * cap_here], ('vid',...  10.3 us
    ppermute x4, starting transfers between devices, local(): lax.ppermute(block, ('vid', 'txt'), caption_perm(step, 2, txt_count, 2))  10.2 us
    ppermute x3, waiting for transfers between devices, reduce_over_group(): total = total + lax.ppermute(chunk, 'txt', perm).astype(F32)  8.02 us
    unnamed x94, local copies, waits for them, and re-layouts  7.72 us
  transfers between devices with their start and end apart: 41, of which 11 were waited for; matrix products, arithmetic and copies ran while one was open for 13% of the time, Pallas kernels for 32%

profile of v2, /device:TPU:0, one launch (start us, length us, event | category | flops | bytes accessed | tf_op | source)
XLA Modules:
  0.0 321.2 jit_solution(6666266924388221986)
XLA Ops:
  7.3 3.9 %constant_dynamic-slice_fusion.6 = bf16[4,512,768]{2,1,0:T(8,128)(2,1)} fusion(bf16[8,512,768]{2,1,0:T(8,128)(2,1)} %own_ref.3, s32[]{:T(128)S(6)} %select_n.285), kind=kLoop, calls=%fused_computation.131 | loop fusion | bytes 6291460 | tf_op jit(solution)/shard_map/dynamic_slice | solution.py:401
  12.0 5.5 %collective-permute-start.2 = (bf16[2,192,768]{2,1,0:T(8,128)(2,1)S(1)}, bf16[2,192,768]{2,1,0:T(8,128)(2,1)}, u32[]{:S(2)}, u32[]{:S(2)}) collective-permute-start(bf16[2,192,768]{2,1,0:T(8,128)(2,1)S(1)} %constant_dynamic-slice_fusion.5), channel_id=1, source_target_pairs={{0,1},{1,2},{2,3},{4,5},{5,6},{6,7},{8,9},{9,10},{10,11},{12,13},{... | collective-permute-start | bytes 1769480 | tf_op jit(solution)/shard_map/ppermute | solution.py:741
  28.3 3.4 %collective-permute-start.5 = (bf16[4,16,896]{2,1,0:T(8,128)(2,1)}, bf16[4,16,896]{2,1,0:T(8,128)(2,1)S(1)}, u32[]{:S(2)}, u32[]{:S(2)}) collective-permute-start(bf16[4,16,896]{2,1,0:T(8,128)(2,1)} %get-tuple-element.188), channel_id=1, source_target_pairs={{0,16},{4,4},{8,20},{12,0},{16,24},{20,12},{24,28},{28,8},{1,17},{... | collective-permute-start | bytes 344072 | tf_op jit(solution)/shard_map/ppermute | solution.py:773
  33.0 4.7 %collective-permute-start.7 = (bf16[4,16,896]{2,1,0:T(8,128)(2,1)S(1)}, bf16[4,16,896]{2,1,0:T(8,128)(2,1)S(1)}, u32[]{:S(2)}, u32[]{:S(2)}) collective-permute-start(bf16[4,16,896]{2,1,0:T(8,128)(2,1)S(1)} %copy-done.30), channel_id=1, source_target_pairs={{0,20},{4,0},{8,16},{12,4},{16,28},{20,8},{24,24},{28,12},{1,21},{... | collective-permute-start | bytes 344072 | tf_op jit(solution)/shard_map/ppermute | solution.py:773
  37.6 10.7 %token_norm.1.tok_ref = bf16[4,1024,768]{2,1,0:T(8,128)(2,1)} custom-call(s32[4]{0:T(128)} %add_add_fusion.1.s_ref, bf16[8,512,768]{2,1,0:T(8,128)(2,1)} %own_ref.3, bf16[4,512,768]{2,1,0:T(8,128)(2,1)} %collective-permute-done.1.other_ref, f32[1,768]{1,0:T(1,128)} %broadcast_in_dim.124.gain_ref), custom_call_target="tpu_custom_call" | custom-call | flops 9900000256 | bytes 9000000 | tf_op jit(solution)/shard_map/token_norm/pallas_call | solution.py:804
  51.7 2.3 broadcast_select_fusion.1
  55.2 7.2 %collective-permute-start.10 = (bf16[2,192,768]{2,1,0:T(8,128)(2,1)}, bf16[2,192,768]{2,1,0:T(8,128)(2,1)S(1)}, u32[]{:S(2)}, u32[]{:S(2)}) collective-permute-start(bf16[2,192,768]{2,1,0:T(8,128)(2,1)} %get-tuple-element.184), channel_id=1, source_target_pairs={{1,0},{2,1},{0,3},{5,4},{6,5},{4,7},{9,8},{10,9},{8,11},{13,12},{1... | collective-permute-start | bytes 1769480 | tf_op jit(solution)/shard_map/ppermute | solution.py:846
  63.9 27.4 %attention_forward.2 = (bf16[4,128,768]{2,1,0:T(8,128)(2,1)}, bf16[4,1088,768]{2,1,0:T(8,128)(2,1)}, bf16[4,1088,768]{2,1,0:T(8,128)(2,1)}, f32[4,2,8,256]{3,2,1,0:T(8,128)}, f32[4,128,768]{2,1,0:T(8,128)}) custom-call(s32[4]{0:T(128)} %add_add_fusion.1.s_ref, bf16[4,1024,768]{2,1,0:T(8,128)(2,1)} %token_norm.1.tok_ref, bf16[4,64,896]{2,1,0:T(8,128)(2,1)} %copy-done.23, ...), custom_call_target="tpu_custom_call" | custom-call | flops 25300000768 | bytes 23000000 | tf_op jit(solution)/shard_map/attention_forward/pallas_call | solution.py:804
  100.2 27.4 %attention_forward.3 = (bf16[4,128,768]{2,1,0:T(8,128)(2,1)}, bf16[4,1088,768]{2,1,0:T(8,128)(2,1)}, bf16[4,1088,768]{2,1,0:T(8,128)(2,1)}, f32[4,2,8,256]{3,2,1,0:T(8,128)}, f32[4,128,768]{2,1,0:T(8,128)}) custom-call(s32[4]{0:T(128)} %add_add_fusion.s_ref, ...), custom_call_target="tpu_custom_call", output_to_operand_aliasing={{0}: (8, {}), {1}: (9, {}), {2}: (10, {}), {3}: (11, {}), {... | custom-call | flops 25300000768 | bytes 23000000 | tf_op jit(solution)/shard_map/attention_forward/pallas_call | solution.py:804
  131.6 3.9 %multiply_convert_fusion.1 = (bf16[4,128,768]{2,1,0:T(8,128)(2,1)S(1)}, f32[4,128,768]{2,1,0:T(8,128)S(1)}, f32[4,128,768]{2,1,0:T(8,128)S(1)}) fusion(bf16[768,768]{1,0:T(8,128)(2,1)S(1)} %copy-done, f32[4,128,768]{2,1,0:T(8,128)S(1)} %get-tuple-element.159, f32[768]{0:T(1024)S(1)} %copy-done.36, f32[4,128]{1,0:T(4,128)S(1)} %add_rsqrt_fusion, ...), kind=kOutput, calls=%fused_computation.19 | convolution fusion | flops 631111680 | bytes 6691840 | tf_op jit(solution)/shard_map/bld,df->blf/dot_general | solution.py:737
  139.1 2.8 collective-permute-start.12
  147.4 7.5 %collective-permute-done.13 = bf16[128,768]{1,0:T(8,128)(2,1)S(1)} collective-permute-done((bf16[128,768]{1,0:T(8,128)(2,1)S(1)}, bf16[128,768]{1,0:T(8,128)(2,1)S(1)}, u32[]{:S(2)}, u32[]{:S(2)}) %collective-permute-start.13) | collective-permute-done | bytes 196640 | tf_op jit(solution)/shard_map/ppermute | solution.py:397
  155.1 5.0 %collective-permute-start.15 = (bf16[128,768]{1,0:T(8,128)(2,1)S(1)}, bf16[128,768]{1,0:T(8,128)(2,1)S(1)}, u32[]{:S(2)}, u32[]{:S(2)}) collective-permute-start(bf16[128,768]{1,0:T(8,128)(2,1)S(1)} %get-tuple-element.155), channel_id=1, source_target_pairs={{0,3},{1,0},{2,1},{3,2},{4,7},{5,4},{6,5},{7,6},{8,11},{9,8},{10,9... | collective-permute-start | bytes 589832 | tf_op jit(solution)/shard_map/ppermute | solution.py:397
  162.6 2.7 collective-permute-done.15
  165.4 12.2 %collective-permute-done.16 = bf16[128,768]{1,0:T(8,128)(2,1)S(1)} collective-permute-done((bf16[128,768]{1,0:T(8,128)(2,1)S(1)}, bf16[128,768]{1,0:T(8,128)(2,1)S(1)}, u32[]{:S(2)}, u32[]{:S(2)}) %collective-permute-start.16) | collective-permute-done | bytes 196640 | tf_op jit(solution)/shard_map/ppermute | solution.py:397
  184.0 2.9 collective-permute-start.19
  193.3 55.6 %attention_backward.1 = (f32[8,512,768]{2,1,0:T(8,128)}, bf16[4,576,768]{2,1,0:T(8,128)(2,1)}, bf16[4,64,768]{2,1,0:T(8,128)(2,1)}, f32[8,64,768]{2,1,0:T(8,128)}, bf16[896,768]{1,0:T(8,128)(2,1)}) custom-call(s32[4]{0:T(128)} %add_add_fusion.1.s_ref, bf16[4,128,768]{2,1,0:T(8,128)(2,1)} %get-tuple-element.111.q_ref, ...), custom_call_target="tpu_custom_call" | custom-call | flops 3300000000 | bytes 3000000 | tf_op jit(solution)/shard_map/attention_backward/pallas_call | solution.py:804
  254.3 2.5 fusion.40
  260.9 5.1 %collective-permute-done.25 = bf16[112,768]{1,0:T(8,128)(2,1)S(1)} collective-permute-done((bf16[112,768]{1,0:T(8,128)(2,1)}, bf16[112,768]{1,0:T(8,128)(2,1)S(1)}, u32[]{:S(2)}, u32[]{:S(2)}) %collective-permute-start.25) | collective-permute-done | bytes 172064 | tf_op jit(solution)/shard_map/ppermute | solution.py:439
  266.0 2.9 collective-permute-done.24
  274.2 3.8 %select_convert_fusion = (f32[768,768]{1,0:T(8,128)}, f32[768,768]{1,0:T(8,128)}) fusion(bf16[768,768]{1,0:T(8,128)(2,1)} %collective-permute-done.26, bf16[768,768]{1,0:T(8,128)(2,1)S(1)} %copy-done.16, pred[]{:T(512)S(6)} %eq.65), kind=kLoop, calls=%fused_computation.53 | loop fusion | flops 2359296 | bytes 7077889 | tf_op jit(solution)/shard_map/convert_element_type | solution.py:1064
  278.0 7.6 %place_rows.1 = (f32[8,512,768]{2,1,0:T(8,128)}, f32[8,64,768]{2,1,0:T(8,128)}) custom-call(s32[4]{0:T(128)} %add_add_fusion.1.s_ref, f32[8,512,768]{2,1,0:T(8,128)} %get-tuple-element.128.video_in, f32[8,64,768]{2,1,0:T(8,128)} %get-tuple-element.129.lat_in, ...), custom_call_target="tpu_custom_call", output_to_operand_aliasing={{0}: (1, {}), {1}: (2, {})} | custom-call | flops 6000000000 | bytes 10000000 | tf_op jit(solution)/shard_map/place_rows/pallas_call | solution.py:988
  290.4 5.7 %collective-permute-start.32 = (bf16[4,16,768]{2,1,0:T(8,128)(2,1)S(1)}, bf16[4,16,768]{2,1,0:T(8,128)(2,1)S(1)}, u32[]{:S(2)}, u32[]{:S(2)}) collective-permute-start(bf16[4,16,768]{2,1,0:T(8,128)(2,1)S(1)} %copy-done.34), channel_id=1, source_target_pairs={{16,0},{4,4},{20,8},{0,12},{24,16},{12,20},{28,24},{8,28},{17,1},{... | collective-permute-start | bytes 294920 | tf_op jit(solution)/shard_map/ppermute | solution.py:1029
  298.1 3.9 %collective-permute-start.34 = (bf16[4,16,768]{2,1,0:T(8,128)(2,1)S(1)}, bf16[4,16,768]{2,1,0:T(8,128)(2,1)S(1)}, u32[]{:S(2)}, u32[]{:S(2)}) collective-permute-start(bf16[4,16,768]{2,1,0:T(8,128)(2,1)S(1)} %copy-done.32), channel_id=1, source_target_pairs={{20,0},{0,4},{16,8},{4,12},{28,16},{8,20},{24,24},{12,28},{21,1},{... | collective-permute-start | bytes 294920 | tf_op jit(solution)/shard_map/ppermute | solution.py:1029
  (257 shorter events, 87.7 us)
Async XLA Ops:
  7.2 243.1 %all-reduce.2.cloned.1.call-start = ((), (), s32[]{:S(2)}) async-start(), calls=%async_computation | async-start | bytes 2359296 | tf_op jit(solution)/shard_map/psum | solution.py:917
  11.2 21.8 %collective-permute-start.1 = (bf16[4,512,768]{2,1,0:T(8,128)(2,1)}, bf16[4,512,768]{2,1,0:T(8,128)(2,1)}, u32[]{:S(2)}, u32[]{:S(2)}) collective-permute-start(bf16[4,512,768]{2,1,0:T(8,128)(2,1)} %constant_dynamic-slice_fusion.6), channel_id=1, source_target_pairs={{0,16},{16,0},{1,17},{17,1},{2,18},{18,2},{3,19},{19,3},{4,20},{20... | collective-permute-start | bytes 9437192 | tf_op jit(solution)/shard_map/ppermute | solution.py:393
  12.0 36.4 %collective-permute-start.2 = (bf16[2,192,768]{2,1,0:T(8,128)(2,1)S(1)}, bf16[2,192,768]{2,1,0:T(8,128)(2,1)}, u32[]{:S(2)}, u32[]{:S(2)}) collective-permute-start(bf16[2,192,768]{2,1,0:T(8,128)(2,1)S(1)} %constant_dynamic-slice_fusion.5), channel_id=1, source_target_pairs={{0,1},{1,2},{2,3},{4,5},{5,6},{6,7},{8,9},{9,10},{10,11},{12,13},{... | collective-permute-start | bytes 1769480 | tf_op jit(solution)/shard_map/ppermute | solution.py:741
  17.4 30.9 %collective-permute-start.3 = (bf16[2,192,768]{2,1,0:T(8,128)(2,1)S(1)}, bf16[2,192,768]{2,1,0:T(8,128)(2,1)}, u32[]{:S(2)}, u32[]{:S(2)}) collective-permute-start(bf16[2,192,768]{2,1,0:T(8,128)(2,1)S(1)} %constant_dynamic-slice_fusion.5), channel_id=1, source_target_pairs={{1,0},{2,1},{3,2},{5,4},{6,5},{7,6},{9,8},{10,9},{11,10},{13,12},{... | collective-permute-start | bytes 1769480 | tf_op jit(solution)/shard_map/ppermute | solution.py:742
  28.3 20.0 %collective-permute-start.5 = (bf16[4,16,896]{2,1,0:T(8,128)(2,1)}, bf16[4,16,896]{2,1,0:T(8,128)(2,1)S(1)}, u32[]{:S(2)}, u32[]{:S(2)}) collective-permute-start(bf16[4,16,896]{2,1,0:T(8,128)(2,1)} %get-tuple-element.188), channel_id=1, source_target_pairs={{0,16},{4,4},{8,20},{12,0},{16,24},{20,12},{24,28},{28,8},{1,17},{... | collective-permute-start | bytes 344072 | tf_op jit(solution)/shard_map/ppermute | solution.py:773
  32.9 15.4 %collective-permute-start.6 = (bf16[4,16,896]{2,1,0:T(8,128)(2,1)S(1)}, bf16[4,16,896]{2,1,0:T(8,128)(2,1)S(1)}, u32[]{:S(2)}, u32[]{:S(2)}) collective-permute-start(bf16[4,16,896]{2,1,0:T(8,128)(2,1)S(1)} %copy-done.31), channel_id=1, source_target_pairs={{0,4},{4,20},{8,0},{12,16},{16,12},{20,28},{24,8},{28,24},{1,5},{5... | collective-permute-start | bytes 344072 | tf_op jit(solution)/shard_map/ppermute | solution.py:773
  33.0 15.4 %collective-permute-start.7 = (bf16[4,16,896]{2,1,0:T(8,128)(2,1)S(1)}, bf16[4,16,896]{2,1,0:T(8,128)(2,1)S(1)}, u32[]{:S(2)}, u32[]{:S(2)}) collective-permute-start(bf16[4,16,896]{2,1,0:T(8,128)(2,1)S(1)} %copy-done.30), channel_id=1, source_target_pairs={{0,20},{4,0},{8,16},{12,4},{16,28},{20,8},{24,24},{28,12},{1,21},{... | collective-permute-start | bytes 344072 | tf_op jit(solution)/shard_map/ppermute | solution.py:773
  53.9 37.3 %collective-permute-start.9 = (bf16[2,192,768]{2,1,0:T(8,128)(2,1)}, bf16[2,192,768]{2,1,0:T(8,128)(2,1)S(1)}, u32[]{:S(2)}, u32[]{:S(2)}) collective-permute-start(bf16[2,192,768]{2,1,0:T(8,128)(2,1)} %get-tuple-element.185), channel_id=1, source_target_pairs={{1,2},{2,3},{3,0},{5,6},{6,7},{7,4},{9,10},{10,11},{11,8},{13,14},... | collective-permute-start | bytes 1769480 | tf_op jit(solution)/shard_map/ppermute | solution.py:845
  55.2 36.1 %collective-permute-start.10 = (bf16[2,192,768]{2,1,0:T(8,128)(2,1)}, bf16[2,192,768]{2,1,0:T(8,128)(2,1)S(1)}, u32[]{:S(2)}, u32[]{:S(2)}) collective-permute-start(bf16[2,192,768]{2,1,0:T(8,128)(2,1)} %get-tuple-element.184), channel_id=1, source_target_pairs={{1,0},{2,1},{0,3},{5,4},{6,5},{4,7},{9,8},{10,9},{8,11},{13,12},{1... | collective-permute-start | bytes 1769480 | tf_op jit(solution)/shard_map/ppermute | solution.py:846
  137.7 17.2 %collective-permute-start.13 = (bf16[128,768]{1,0:T(8,128)(2,1)S(1)}, bf16[128,768]{1,0:T(8,128)(2,1)S(1)}, u32[]{:S(2)}, u32[]{:S(2)}) collective-permute-start(bf16[128,768]{1,0:T(8,128)(2,1)S(1)} %get-tuple-element.178), channel_id=1, source_target_pairs={{0,2},{1,3},{2,0},{3,1},{4,6},{5,7},{6,4},{7,5},{8,10},{9,11},{10,... | collective-permute-start | bytes 589832 | tf_op jit(solution)/shard_map/ppermute | solution.py:397
  139.1 15.9 %collective-permute-start.12 = (bf16[128,768]{1,0:T(8,128)(2,1)S(1)}, bf16[128,768]{1,0:T(8,128)(2,1)S(1)}, u32[]{:S(2)}, u32[]{:S(2)}) collective-permute-start(bf16[128,768]{1,0:T(8,128)(2,1)S(1)} %get-tuple-element.176), channel_id=1, source_target_pairs={{0,3},{1,0},{2,1},{3,2},{4,7},{5,4},{6,5},{7,6},{8,11},{9,8},{10,9... | collective-permute-start | bytes 589832 | tf_op jit(solution)/shard_map/ppermute | solution.py:397
  143.7 34.0 %collective-permute-start.18 = (bf16[768,768]{1,0:T(8,128)(2,1)S(1)}, bf16[768,768]{1,0:T(8,128)(2,1)S(1)}, u32[]{:S(2)}, u32[]{:S(2)}) collective-permute-start(bf16[768,768]{1,0:T(8,128)(2,1)S(1)} %get-tuple-element.195), channel_id=1, source_target_pairs={{0,16},{16,0},{1,17},{17,1},{2,18},{18,2},{3,19},{19,3},{4,20},{20... | collective-permute-start | bytes 3538952 | tf_op jit(solution)/shard_map/ppermute | solution.py:393
  162.0 15.6 %collective-permute-start.16 = (bf16[128,768]{1,0:T(8,128)(2,1)S(1)}, bf16[128,768]{1,0:T(8,128)(2,1)S(1)}, u32[]{:S(2)}, u32[]{:S(2)}) collective-permute-start(bf16[128,768]{1,0:T(8,128)(2,1)S(1)} %get-tuple-element.155), channel_id=1, source_target_pairs={{0,2},{1,3},{2,0},{3,1},{4,6},{5,7},{6,4},{7,5},{8,10},{9,11},{10,... | collective-permute-start | bytes 589832 | tf_op jit(solution)/shard_map/ppermute | solution.py:397
  181.5 67.3 %collective-permute-start.21 = (bf16[128,768]{1,0:T(8,128)(2,1)}, bf16[128,768]{1,0:T(8,128)(2,1)}, u32[]{:S(2)}, u32[]{:S(2)}) collective-permute-start(bf16[128,768]{1,0:T(8,128)(2,1)} %get-tuple-element.174), channel_id=1, source_target_pairs={{0,1},{1,2},{2,3},{3,0},{4,5},{5,6},{6,7},{7,4},{8,9},{9,10},{10,1... | collective-permute-start | bytes 589832 | tf_op jit(solution)/shard_map/ppermute | solution.py:397
  182.0 66.8 %collective-permute-start.20 = (bf16[128,768]{1,0:T(8,128)(2,1)}, bf16[128,768]{1,0:T(8,128)(2,1)}, u32[]{:S(2)}, u32[]{:S(2)}) collective-permute-start(bf16[128,768]{1,0:T(8,128)(2,1)} %get-tuple-element.175), channel_id=1, source_target_pairs={{0,2},{1,3},{2,0},{3,1},{4,6},{5,7},{6,4},{7,5},{8,10},{9,11},{10,... | collective-permute-start | bytes 589832 | tf_op jit(solution)/shard_map/ppermute | solution.py:397
  184.0 64.9 %collective-permute-start.19 = (bf16[128,768]{1,0:T(8,128)(2,1)}, bf16[128,768]{1,0:T(8,128)(2,1)}, u32[]{:S(2)}, u32[]{:S(2)}) collective-permute-start(bf16[128,768]{1,0:T(8,128)(2,1)} %get-tuple-element.173), channel_id=1, source_target_pairs={{0,3},{1,0},{2,1},{3,2},{4,7},{5,4},{6,5},{7,6},{8,11},{9,8},{10,9... | collective-permute-start | bytes 589832 | tf_op jit(solution)/shard_map/ppermute | solution.py:397
  253.8 16.5 %collective-permute-start.27 = (bf16[4,576,768]{2,1,0:T(8,128)(2,1)}, bf16[4,576,768]{2,1,0:T(8,128)(2,1)}, u32[]{:S(2)}, u32[]{:S(2)}) collective-permute-start(bf16[4,576,768]{2,1,0:T(8,128)(2,1)} %get-tuple-element.125), channel_id=1, source_target_pairs={{0,16},{16,0},{1,17},{17,1},{2,18},{18,2},{3,19},{19,3},{4,20},{20... | collective-permute-start | bytes 10616840 | tf_op jit(solution)/shard_map/ppermute | solution.py:393
  253.9 16.4 %collective-permute-start.26 = (bf16[768,768]{1,0:T(8,128)(2,1)}, bf16[768,768]{1,0:T(8,128)(2,1)}, u32[]{:S(2)}, u32[]{:S(2)}) collective-permute-start(bf16[768,768]{1,0:T(8,128)(2,1)} %all-reduce.2.cloned.1.call-done), channel_id=1, source_target_pairs={{0,16},{16,0},{1,17},{17,1},{2,18},{18,2},{3,19},{19,3},{4,20},{20... | collective-permute-start | bytes 3538952 | tf_op jit(solution)/shard_map/ppermute | solution.py:393
  270.3 15.5 %collective-permute-start.28 = (bf16[112,768]{1,0:T(8,128)(2,1)S(1)}, bf16[112,768]{1,0:T(8,128)(2,1)}, u32[]{:S(2)}, u32[]{:S(2)}) collective-permute-start(bf16[112,768]{1,0:T(8,128)(2,1)S(1)} %add_convert_fusion.3), channel_id=1, source_target_pairs={{0,12},{4,0},{8,4},{12,8},{1,13},{5,1},{9,5},{13,9},{2,14},{6,2},{... | collective-permute-start | bytes 516104 | tf_op jit(solution)/shard_map/ppermute | solution.py:449
  272.1 16.7 %collective-permute-start.29 = (bf16[112,768]{1,0:T(8,128)(2,1)S(1)}, bf16[112,768]{1,0:T(8,128)(2,1)}, u32[]{:S(2)}, u32[]{:S(2)}) collective-permute-start(bf16[112,768]{1,0:T(8,128)(2,1)S(1)} %add_convert_fusion.3), channel_id=1, source_target_pairs={{0,8},{4,12},{8,0},{12,4},{1,9},{5,13},{9,1},{13,5},{2,10},{6,14},... | collective-permute-start | bytes 516104 | tf_op jit(solution)/shard_map/ppermute | solution.py:449
  272.5 18.0 %collective-permute-start.30 = (bf16[112,768]{1,0:T(8,128)(2,1)S(1)}, bf16[112,768]{1,0:T(8,128)(2,1)}, u32[]{:S(2)}, u32[]{:S(2)}) collective-permute-start(bf16[112,768]{1,0:T(8,128)(2,1)S(1)} %add_convert_fusion.3), channel_id=1, source_target_pairs={{0,4},{4,8},{8,12},{12,0},{1,5},{5,9},{9,13},{13,1},{2,6},{6,10},{... | collective-permute-start | bytes 516104 | tf_op jit(solution)/shard_map/ppermute | solution.py:449
  273.0 24.1 %collective-permute-start.35 = (bf16[128,768]{1,0:T(8,128)(2,1)S(1)}, bf16[128,768]{1,0:T(8,128)(2,1)}, u32[]{:S(2)}, u32[]{:S(2)}) collective-permute-start(bf16[128,768]{1,0:T(8,128)(2,1)S(1)} %fusion.26), channel_id=1, source_target_pairs={{0,3},{1,0},{2,1},{3,2},{4,7},{5,4},{6,5},{7,6},{8,11},{9,8},{10,9... | collective-permute-start | bytes 589832 | tf_op jit(solution)/shard_map/ppermute | solution.py:397
  273.0 25.1 %collective-permute-start.36 = (bf16[128,768]{1,0:T(8,128)(2,1)S(1)}, bf16[128,768]{1,0:T(8,128)(2,1)}, u32[]{:S(2)}, u32[]{:S(2)}) collective-permute-start(bf16[128,768]{1,0:T(8,128)(2,1)S(1)} %fusion.26), channel_id=1, source_target_pairs={{0,2},{1,3},{2,0},{3,1},{4,6},{5,7},{6,4},{7,5},{8,10},{9,11},{10,... | collective-permute-start | bytes 589832 | tf_op jit(solution)/shard_map/ppermute | solution.py:397
  285.8 17.2 %collective-permute-start.37 = (bf16[128,768]{1,0:T(8,128)(2,1)S(1)}, bf16[128,768]{1,0:T(8,128)(2,1)S(1)}, u32[]{:S(2)}, u32[]{:S(2)}) collective-permute-start(bf16[128,768]{1,0:T(8,128)(2,1)S(1)} %fusion.26), channel_id=1, source_target_pairs={{0,1},{1,2},{2,3},{3,0},{4,5},{5,6},{6,7},{7,4},{8,9},{9,10},{10,1... | collective-permute-start | bytes 589832 | tf_op jit(solution)/shard_map/ppermute | solution.py:397
  (62 other events, 586.2 us)
Sparse Core Ops, SparseCore 0:
  187.0 51.7 all-reduce.1

commit v3 on v2

--- a/solution.py
+++ b/solution.py
@@ -401,12 +401,19 @@
     return lax.dynamic_slice_in_dim(values, index * size, size, axis)
 
 
-def reduce_over_head(part, place, count):
+def head_chunks(part, place, count):
     low = part.astype(BF16)
-    total = lax.dynamic_index_in_dim(part, place, 0, False)
+    others = [
+        lax.dynamic_index_in_dim(low, (place - shift) % count, 0, False)
+        for shift in range(1, count)
+    ]
+    return [lax.dynamic_index_in_dim(part, place, 0, False)] + others
+
+
+def reduce_over_head(chunks, count):
+    total = chunks[0]
     for shift in range(1, count):
-        chunk = lax.dynamic_index_in_dim(low, (place - shift) % count, 0, False)
-        total = total + head_shift(chunk, shift, count).astype(F32)
+        total = total + head_shift(chunks[shift], shift, count).astype(F32)
     return total.astype(BF16)
 
 
@@ -627,12 +634,15 @@
         gain_out[...] = jnp.zeros_like(gain_out)
         sums_ref[...] = jnp.zeros_like(sums_ref)
 
-    wide = sums_ref.shape[0] // 3
+    wide = sums_ref.shape[0] // 4
     window = pl.ds(pl.multiple_of(s_ref[2], PAIR), wide)
     video_rows = pl.ds(0, keys - cap)
     cap_norm = layer_norm(cap_ref[:, pl.ds(0, D)].astype(F32), gain).astype(BF16)
     latn = layer_norm(lat_ref[...].astype(F32), gain_lat_ref[...]).astype(BF16)
     sums_ref[pl.ds(0, wide), :] += dot_tn(dq_ref[:, window], latn)
+    keep = (1 - s_ref[4 + item]).astype(F32)
+    mixed = (o_ref[:, window] * keep).astype(BF16)
+    sums_ref[pl.ds(3 * wide, wide), :] += dot_tn(mixed, after_ref[...].astype(BF16))
 
     def both(rows):
         return jnp.concatenate([dk_ref[rows, window], dv_ref[rows, window]], axis=1)
@@ -680,16 +690,16 @@
     @pl.when(item == pl.num_programs(0) - 1)
     def _():
         width = D // 4
-        for n in range(3):
+        for n in range(4):
             mine = pl.ds(pl.multiple_of(s_ref[3] + n * wide, PAIR // 2), width)
             late_ref[pl.ds(n * width, width), :] = sums_ref[mine, :].astype(BF16)
         ready = ready_ref.shape[0]
-        late_ref[pl.ds(3 * width, ready), :] = ready_ref[...]
+        late_ref[pl.ds(4 * width, ready), :] = ready_ref[...]
         gains = [jnp.sum(gain_out[pl.ds(8 * row, 8), :], axis=0, keepdims=True) for row in (0, 1)]
         gains = jnp.concatenate(gains + [jnp.zeros((14, D), F32)], axis=0)
-        late_ref[pl.ds(3 * width + ready, 16), :] = gains.astype(BF16)
-        spare = late_ref.shape[0] - 3 * width - ready - 16
-        late_ref[pl.ds(3 * width + ready + 16, spare), :] = jnp.zeros((spare, D), BF16)
+        late_ref[pl.ds(4 * width + ready, 16), :] = gains.astype(BF16)
+        spare = late_ref.shape[0] - 4 * width - ready - 16
+        late_ref[pl.ds(4 * width + ready + 16, spare), :] = jnp.zeros((spare, D), BF16)
 
 
 def place_kernel(s_ref, video_in, lat_in, video_part, lat_part, video_ref, lat_ref):
@@ -749,18 +759,21 @@
         chunk = chunk.reshape((-1, 2, 1) + chunk.shape[-2:])
         return lax.dynamic_update_slice(whole, chunk, (at_core, zero, at_chunk, zero, zero))
 
-    video_other = swap_cores(take_block(video_tokens, 1 - core, own))
-    both = jnp.concatenate([latents, cotangent], axis=1)
-    both_own = take_block(both, core, own)
-    both_other = swap_cores(take_block(both, 1 - core, own))
+    both_own = take_block(jnp.concatenate([latents, cotangent], axis=1), core, own)
+    video_other = swap_cores(
+        jnp.concatenate(
+            [take_block(a, 1 - core, own) for a in (video_tokens, latents, cotangent)], axis=1
+        )
+    )
+    both_other = video_other[:, video_here:]
     lat = jnp.concatenate([both_own[:, :lat_half], both_other[:, :lat_half]], axis=1)
     cot = jnp.concatenate([both_own[:, lat_half:], both_other[:, lat_half:]], axis=1)
     drop_own = take_block(drop_flags, core, own)
     keep = (1 - drop_own).astype(F32)
     window = z * head_width // PAIR * PAIR
     inside = z * head_width - window
-    scalars = jnp.stack([core, near_at, window, inside])
-    scalars_far = jnp.stack([core, 1 - near_at, window, inside])
+    scalars = jnp.concatenate([jnp.stack([core, near_at, window, inside]), drop_own])
+    scalars_far = jnp.concatenate([jnp.stack([core, 1 - near_at, window, inside]), drop_own])
 
     place_slots = place_index * cap_here + jnp.arange(cap_here, dtype=jnp.int32)
     cap_valid = (place_slots[None, :] < caption_len[:, None]) & (key_mask == 1)
@@ -903,29 +916,29 @@
     d_pre = gelu_pull(dot("bld,fd->blf", cot, down_weight))[0].astype(BF16)
     d_mlp_part = dot("blf,df->bld", d_pre, up_weight)
     d_mlp_part, activ, d_pre = lax.optimization_barrier((d_mlp_part, activ, d_pre))
-    d_mlp_norm = gather_head(reduce_over_head(d_mlp_part, z, head_count), z, head_count)
+    d_mlp_total = reduce_over_head(head_chunks(d_mlp_part, z, head_count), head_count)
     grad_down = dot("blf,bld->fd", activ, cot).astype(BF16)
     grad_up = dot("bld,blf->df", mlp_norm, d_pre).astype(BF16)
     near, far, _ = lax.optimization_barrier((near, far, d_mlp_part))
     weights = both_halves(near, far)
     early = jnp.where(core == 0, grad_up, grad_down).astype(F32)
     early = early + swap_cores(jnp.where(core == 0, grad_down, grad_up)).astype(F32)
-    growth = dot("blf,fd->bld", activ, down_weight)
-    growth, d_mlp_norm, early, weights = lax.optimization_barrier(
-        (growth, d_mlp_norm, early.astype(BF16), weights)
-    )
-    early = lax.psum(early, "txt")
-    growth = reduce_over_head(growth, z, head_count)
+    d_mlp_total, early = lax.optimization_barrier((d_mlp_total, early))
+    early = reduce_over_group(early, place_index, txt_count)
+    d_mlp_norm = gather_head(d_mlp_total, z, head_count)
+    growth = dot("blf,fd->bld", activ, down_weight).astype(BF16)
+    growth, d_mlp_norm, weights, early = lax.optimization_barrier(
+        (growth, d_mlp_norm, weights, early)
+    )
+    early = gather_places(early, place_index, txt_count)
+    growth = lax.psum(growth, "head")
 
     d_after_norm, gain_mlp_part = norm_back_rows(after_attn, gain_mlp, d_mlp_norm.astype(F32))
     d_after = cot.astype(F32) + d_after_norm
     d_branch = d_after.astype(BF16)
     d_att = (dot("bld,ed->ble", d_branch, w_out) * keep[:, None, None]).astype(BF16)
-    mixed_mine = lax.dynamic_slice_in_dim(mixed_in, z * head_width, head_width, 2)
-    grad_out = dot("ble,bld->ed", mixed_mine, d_branch)
     ready = jnp.concatenate(
         [
-            grad_out,
             jnp.sum(gain_mlp_part, axis=0)[None],
             jnp.full((1, D), jnp.sum(keep)),
             jnp.zeros((14, D), F32),
@@ -979,18 +992,18 @@
             pltpu.VMEM(pair_shape, BF16),
             pltpu.VMEM(pair_shape, BF16),
             pltpu.VMEM((256, D), F32),
-            pltpu.VMEM((6 * PAIR, D), F32),
+            pltpu.VMEM((8 * PAIR, D), F32),
             pltpu.VMEM((16, D), F32),
         ],
     )
     def place(video_grad, latent_grad, part):
-        piece = video_here // 2
+        piece = video_here
         return pl.pallas_call(
             place_kernel,
             name="place_rows",
             grid_spec=pltpu.PrefetchScalarGridSpec(
                 num_scalar_prefetch=1,
-                grid=(own, 2),
+                grid=(own, 1),
                 in_specs=[
                     pl.BlockSpec(memory_space=pl.ANY),
                     pl.BlockSpec(memory_space=pl.ANY),
@@ -1012,16 +1025,15 @@
             ),
         )(scalars, video_grad, latent_grad, part, part)
 
-    growth, early, late = lax.optimization_barrier((growth, early, late))
+    early, growth, late = lax.optimization_barrier((early, growth, late))
     late_half, late_swapped = reduce_over_cores(late, core)
     other_back, early, _ = lax.optimization_barrier((other_back, early, late_swapped))
     other_here = swap_cores(other_back)
     early_other = swap_cores(early)
     late_total = reduce_over_group(late_half, place_index, txt_count)
-    late_total, growth, early_other, other_here, cap_back = lax.optimization_barrier(
-        (late_total, growth, early_other, other_here, cap_back)
-    )
-    growth = gather_head(growth, z, head_count)
+    late_total, early_other, other_here, cap_back = lax.optimization_barrier(
+        (late_total, early_other, other_here, cap_back)
+    )
     cap_parts = []
     for step in range(txt_count):
         perm = [(b, a) for a, b in caption_perm(step, 2, txt_count, 2)]
@@ -1030,8 +1042,8 @@
         )
     late = gather_places(late_total, place_index, txt_count)
     video_grad, latent_grad = place(video_grad, latent_grad, other_here)
-    late, video_grad, latent_grad, cap_parts, growth = lax.optimization_barrier(
-        (late, video_grad, latent_grad, cap_parts, growth)
+    late, video_grad, latent_grad, cap_parts = lax.optimization_barrier(
+        (late, video_grad, latent_grad, cap_parts)
     )
     late = gather_cores(late, core).astype(F32)
     caption_grad = jnp.zeros((txt_count, own, cap_here, D), F32)

time: 323 us -> 322 us (level)
  local copies, waits for them, and re-layouts: 34.1 us -> 43.8 us
  waiting for transfers between devices: 37.4 us -> 32.1 us
    ppermute x12 -> x6, starting transfers between devices: 17.7 us -> 7.27 us  [head_shift(): lax.ppermute(values, 'head', [(i, (i - shift) % count) for i in range(cou...]
    ppermute x3 -> x6, starting transfers between devices: 3.3 us -> 8.61 us  [reduce_over_group(): total = total + lax.ppermute(chunk, 'txt', perm).astype(F32)]
    convert_element_type x4 -> x2, other arithmetic: 4.78 us -> 0.08 us  [the longest x1 0.08 us: head_chunks(): low = part.astype(BF16)]
    ppermute x12 -> x6, waiting for transfers between devices: 24 us -> 20.2 us  [head_shift(): lax.ppermute(values, 'head', [(i, (i - shift) % count) for i in range(cou...]
    ppermute x3 -> x6, starting transfers between devices: 2.68 us -> 6.02 us  [gather_places(): lax.ppermute(total, 'txt', perm)]
    ppermute x3 -> x6, waiting for transfers between devices: 8.02 us -> 4.71 us  [reduce_over_group(): total = total + lax.ppermute(chunk, 'txt', perm).astype(F32)]
    unnamed x94 -> x87, local copies, waits for them, and re-layouts: 7.72 us -> 11 us
    dynamic_slice x5 -> x6, local copies, waits for them, and re-layouts: 6.84 us -> 4.44 us  [take_block(): return lax.dynamic_slice_in_dim(values, index * size, size, axis)]
  transfers between devices with their start and end apart: 41 -> 40, of which waited for: 11 -> 9; matrix products, arithmetic and copies ran while one was open for 13% -> 14% of each run, Pallas kernels for 32% -> 31%
where the time goes in v3:
time: 322 us; the launch traced here: 320 us
  Pallas kernels  127 us (39%)
  starting transfers between devices  61 us (19%)
  local copies, waits for them, and re-layouts  43.8 us (14%)
  waiting for transfers between devices  32.1 us (10%)
  other arithmetic  24.4 us (8%)
  between operations  17 us (5%)
  matrix products  14.8 us (5%)
    pallas_call x4, Pallas kernels, call(): pl.pallas_call(kernel, name=name, grid_spec=pltpu.PrefetchScalarGridSpec(...  122 us
    ppermute x6, waiting for transfers between devices, head_shift(): lax.ppermute(values, 'head', [(i, (i - shift) % count) for i in range(cou...  20.2 us
    dot_general x8, matrix products, dot(): return jnp.einsum(spec, a, b, preferred_element_type=F32)  14.8 us
    unnamed x87, local copies, waits for them, and re-layouts  11 us
    ppermute x4, starting transfers between devices, local(): lax.ppermute(block, ('vid', 'txt'), caption_perm(step, 2, txt_count, 2))  10.1 us
    ppermute x4, starting transfers between devices, local(): lax.ppermute(cap_back[:, step * cap_here:(step + 1) * cap_here], ('vid',...  9.99 us
    ppermute x6, starting transfers between devices, reduce_over_group(): total = total + lax.ppermute(chunk, 'txt', perm).astype(F32)  8.61 us
    ppermute x6, starting transfers between devices, head_shift(): lax.ppermute(values, 'head', [(i, (i - shift) % count) for i in range(cou...  7.27 us
  transfers between devices with their start and end apart: 40, of which 9 were waited for; matrix products, arithmetic and copies ran while one was open for 14% of the time, Pallas kernels for 31%

profile of v3, /device:TPU:0, one launch (start us, length us, event | category | flops | bytes accessed | tf_op | source)
XLA Modules:
  0.0 320.4 jit_solution(3999927524541333633)
XLA Ops:
  7.3 2.2 constant_dynamic-slice_fusion.10
  13.7 5.4 %collective-permute-start.1 = (bf16[2,192,768]{2,1,0:T(8,128)(2,1)S(1)}, bf16[2,192,768]{2,1,0:T(8,128)(2,1)}, u32[]{:S(2)}, u32[]{:S(2)}) collective-permute-start(bf16[2,192,768]{2,1,0:T(8,128)(2,1)S(1)} %constant_dynamic-slice_fusion.7), channel_id=1, source_target_pairs={{0,1},{1,2},{2,3},{4,5},{5,6},{6,7},{8,9},{9,10},{10,11},{12,13},{... | collective-permute-start | bytes 1769480 | tf_op jit(solution)/shard_map/ppermute | solution.py:751
  21.4 2.1 collective-permute-start.3
  23.6 3.3 %collective-permute-start.4 = (bf16[4,16,896]{2,1,0:T(8,128)(2,1)}, bf16[4,16,896]{2,1,0:T(8,128)(2,1)}, u32[]{:S(2)}, u32[]{:S(2)}) collective-permute-start(bf16[4,16,896]{2,1,0:T(8,128)(2,1)} %get-tuple-element.184), channel_id=1, source_target_pairs={{0,16},{4,4},{8,20},{12,0},{16,24},{20,12},{24,28},{28,8},{1,17},{... | collective-permute-start | bytes 344072 | tf_op jit(solution)/shard_map/ppermute | solution.py:786
  33.5 4.2 %collective-permute-start.6 = (bf16[4,16,896]{2,1,0:T(8,128)(2,1)S(1)}, bf16[4,16,896]{2,1,0:T(8,128)(2,1)S(1)}, u32[]{:S(2)}, u32[]{:S(2)}) collective-permute-start(bf16[4,16,896]{2,1,0:T(8,128)(2,1)S(1)} %get-tuple-element.182), channel_id=1, source_target_pairs={{0,20},{4,0},{8,16},{12,4},{16,28},{20,8},{24,24},{28,12},{1,21},{... | collective-permute-start | bytes 344072 | tf_op jit(solution)/shard_map/ppermute | solution.py:786
  37.7 10.7 %token_norm.1.tok_ref = bf16[4,1024,768]{2,1,0:T(8,128)(2,1)} custom-call(s32[8]{0:T(128)} %concatenate.32.s_ref, bf16[8,512,768]{2,1,0:T(8,128)(2,1)} %own_ref.3, bf16[4,640,768]{2,1,0:T(8,128)(2,1)} %collective-permute-done.other_ref, f32[1,768]{1,0:T(1,128)} %broadcast_in_dim.118.gain_ref), custom_call_target="tpu_custom_call" | custom-call | flops 9900000256 | bytes 9000000 | tf_op jit(solution)/shard_map/token_norm/pallas_call | solution.py:817
  51.7 2.1 fusion.38
  57.2 7.1 %collective-permute-start.9 = (bf16[2,192,768]{2,1,0:T(8,128)(2,1)S(1)}, bf16[2,192,768]{2,1,0:T(8,128)(2,1)S(1)}, u32[]{:S(2)}, u32[]{:S(2)}) collective-permute-start(bf16[2,192,768]{2,1,0:T(8,128)(2,1)S(1)} %get-tuple-element.180), channel_id=1, source_target_pairs={{1,0},{2,1},{0,3},{5,4},{6,5},{4,7},{9,8},{10,9},{8,11},{13,12},{1... | collective-permute-start | bytes 1769480 | tf_op jit(solution)/shard_map/ppermute | solution.py:859
  65.9 27.4 %attention_forward.2 = (bf16[4,128,768]{2,1,0:T(8,128)(2,1)}, bf16[4,1088,768]{2,1,0:T(8,128)(2,1)}, bf16[4,1088,768]{2,1,0:T(8,128)(2,1)}, f32[4,2,8,256]{3,2,1,0:T(8,128)}, f32[4,128,768]{2,1,0:T(8,128)}) custom-call(s32[8]{0:T(128)} %concatenate.32.s_ref, bf16[4,1024,768]{2,1,0:T(8,128)(2,1)} %token_norm.1.tok_ref, bf16[4,64,896]{2,1,0:T(8,128)(2,1)} %copy-done.25, ...), custom_call_target="tpu_custom_call" | custom-call | flops 25300000768 | bytes 23000000 | tf_op jit(solution)/shard_map/attention_forward/pallas_call | solution.py:817
  101.0 27.5 %attention_forward.3 = (bf16[4,128,768]{2,1,0:T(8,128)(2,1)}, bf16[4,1088,768]{2,1,0:T(8,128)(2,1)}, bf16[4,1088,768]{2,1,0:T(8,128)(2,1)}, f32[4,2,8,256]{3,2,1,0:T(8,128)}, f32[4,128,768]{2,1,0:T(8,128)}) custom-call(s32[8]{0:T(128)} %concatenate.31.s_ref, ...), custom_call_target="tpu_custom_call", output_to_operand_aliasing={{0}: (8, {}), {1}: (9, {}), {2}: (10, {}), {3}: (11, {}), {... | custom-call | flops 25300000768 | bytes 23000000 | tf_op jit(solution)/shard_map/attention_forward/pallas_call | solution.py:817
  128.5 2.3 fusion.42
  131.5 3.9 %multiply_convert_fusion.1 = (bf16[4,128,768]{2,1,0:T(8,128)(2,1)S(1)}, f32[4,128,768]{2,1,0:T(8,128)S(1)}, f32[4,128,768]{2,1,0:T(8,128)S(1)}) fusion(bf16[768,768]{1,0:T(8,128)(2,1)S(1)} %copy-done, f32[4,128,768]{2,1,0:T(8,128)S(1)} %get-tuple-element.191, f32[768]{0:T(1024)S(1)} %copy-done.32, f32[4,128]{1,0:T(4,128)S(1)} %add_rsqrt_fusion, ...), kind=kOutput, calls=%fused_computation.22 | convolution fusion | flops 631111680 | bytes 6691840 | tf_op jit(solution)/shard_map/bld,df->blf/dot_general | solution.py:747
  139.6 2.3 broadcast_select_fusion
  146.5 2.6 broadcast_in_dim.132
  154.8 7.7 %collective-permute-done.12 = bf16[128,768]{1,0:T(8,128)(2,1)} collective-permute-done((bf16[128,768]{1,0:T(8,128)(2,1)S(1)}, bf16[128,768]{1,0:T(8,128)(2,1)}, u32[]{:S(2)}, u32[]{:S(2)}) %collective-permute-start.12) | collective-permute-done | bytes 196640 | tf_op jit(solution)/shard_map/ppermute | solution.py:397
  173.2 12.1 %collective-permute-done.16 = bf16[128,768]{1,0:T(8,128)(2,1)S(1)} collective-permute-done((bf16[128,768]{1,0:T(8,128)(2,1)S(1)}, bf16[128,768]{1,0:T(8,128)(2,1)S(1)}, u32[]{:S(2)}, u32[]{:S(2)}) %collective-permute-start.16) | collective-permute-done | bytes 196640 | tf_op jit(solution)/shard_map/ppermute | solution.py:397
  193.7 55.9 %attention_backward.1 = (f32[8,512,768]{2,1,0:T(8,128)}, bf16[4,576,768]{2,1,0:T(8,128)(2,1)}, bf16[4,64,768]{2,1,0:T(8,128)(2,1)}, f32[8,64,768]{2,1,0:T(8,128)}, bf16[896,768]{1,0:T(8,128)(2,1)}) custom-call(s32[8]{0:T(128)} %concatenate.32.s_ref, bf16[4,128,768]{2,1,0:T(8,128)(2,1)} %get-tuple-element.113.q_ref, ...), custom_call_target="tpu_custom_call" | custom-call | flops 3300000000 | bytes 3000000 | tf_op jit(solution)/shard_map/attention_backward/pallas_call | solution.py:817
  258.8 2.3 collective-permute-done.25
  265.2 2.3 collective-permute-start.26
  273.0 4.7 %collective-permute-done.27 = bf16[112,768]{1,0:T(8,128)(2,1)} collective-permute-done((bf16[112,768]{1,0:T(8,128)(2,1)}, bf16[112,768]{1,0:T(8,128)(2,1)}, u32[]{:S(2)}, u32[]{:S(2)}) %collective-permute-start.27) | collective-permute-done | bytes 172064 | tf_op jit(solution)/shard_map/ppermute | solution.py:446
  282.1 4.1 %select_convert_fusion = (f32[768,768]{1,0:T(8,128)}, f32[768,768]{1,0:T(8,128)}) fusion(bf16[768,768]{1,0:T(8,128)(2,1)} %collective-permute-done.29, bf16[768,768]{1,0:T(8,128)(2,1)} %constant_dynamic-update-slice_fusion.7, pred[]{:T(512)S(6)} %eq.65), kind=kLoop, calls=%fused_computation.54 | loop fusion | flops 2359296 | bytes 7077889 | tf_op jit(solution)/shard_map/convert_element_type | solution.py:1076
  286.9 5.3 %collective-permute-start.35 = (bf16[4,16,768]{2,1,0:T(8,128)(2,1)S(1)}, bf16[4,16,768]{2,1,0:T(8,128)(2,1)S(1)}, u32[]{:S(2)}, u32[]{:S(2)}) collective-permute-start(bf16[4,16,768]{2,1,0:T(8,128)(2,1)S(1)} %get-tuple-element.188), channel_id=1, source_target_pairs={{16,0},{4,4},{20,8},{0,12},{24,16},{12,20},{28,24},{8,28},{17,1},{... | collective-permute-start | bytes 294920 | tf_op jit(solution)/shard_map/ppermute | solution.py:1041
  292.3 6.0 %place_rows.1 = (f32[8,512,768]{2,1,0:T(8,128)}, f32[8,64,768]{2,1,0:T(8,128)}) custom-call(s32[8]{0:T(128)} %concatenate.32.s_ref, f32[8,512,768]{2,1,0:T(8,128)} %get-tuple-element.130.video_in, f32[8,64,768]{2,1,0:T(8,128)} %get-tuple-element.131.lat_in, ...), custom_call_target="tpu_custom_call", output_to_operand_aliasing={{0}: (1, {}), {1}: (2, {})} | custom-call | flops 6000000000 | bytes 10000000 | tf_op jit(solution)/shard_map/place_rows/pallas_call | solution.py:1001
  298.4 3.9 %collective-permute-start.37 = (bf16[4,16,768]{2,1,0:T(8,128)(2,1)S(1)}, bf16[4,16,768]{2,1,0:T(8,128)(2,1)S(1)}, u32[]{:S(2)}, u32[]{:S(2)}) collective-permute-start(bf16[4,16,768]{2,1,0:T(8,128)(2,1)S(1)} %get-tuple-element.186), channel_id=1, source_target_pairs={{20,0},{0,4},{16,8},{4,12},{28,16},{8,20},{24,24},{12,28},{21,1},{... | collective-permute-start | bytes 294920 | tf_op jit(solution)/shard_map/ppermute | solution.py:1041
  (250 shorter events, 95.8 us)
Async XLA Ops:
  7.2 250.3 %all-reduce.2.cloned.1.call-start = ((), (), s32[]{:S(2)}) async-start(), calls=%async_computation | async-start | bytes 1572864 | tf_op jit(solution)/shard_map/psum | solution.py:934
  11.8 21.7 %collective-permute-start = (bf16[4,640,768]{2,1,0:T(8,128)(2,1)}, bf16[4,640,768]{2,1,0:T(8,128)(2,1)}, u32[]{:S(2)}, u32[]{:S(2)}) collective-permute-start(bf16[4,640,768]{2,1,0:T(8,128)(2,1)} %pad_maximum_fusion), channel_id=1, source_target_pairs={{0,16},{16,0},{1,17},{17,1},{2,18},{18,2},{3,19},{19,3},{4,20},{20... | collective-permute-start | bytes 11796488 | tf_op jit(solution)/shard_map/ppermute | solution.py:393
  13.7 34.8 %collective-permute-start.1 = (bf16[2,192,768]{2,1,0:T(8,128)(2,1)S(1)}, bf16[2,192,768]{2,1,0:T(8,128)(2,1)}, u32[]{:S(2)}, u32[]{:S(2)}) collective-permute-start(bf16[2,192,768]{2,1,0:T(8,128)(2,1)S(1)} %constant_dynamic-slice_fusion.7), channel_id=1, source_target_pairs={{0,1},{1,2},{2,3},{4,5},{5,6},{6,7},{8,9},{9,10},{10,11},{12,13},{... | collective-permute-start | bytes 1769480 | tf_op jit(solution)/shard_map/ppermute | solution.py:751
  19.1 29.3 %collective-permute-start.2 = (bf16[2,192,768]{2,1,0:T(8,128)(2,1)S(1)}, bf16[2,192,768]{2,1,0:T(8,128)(2,1)}, u32[]{:S(2)}, u32[]{:S(2)}) collective-permute-start(bf16[2,192,768]{2,1,0:T(8,128)(2,1)S(1)} %constant_dynamic-slice_fusion.7), channel_id=1, source_target_pairs={{1,0},{2,1},{3,2},{5,4},{6,5},{7,6},{9,8},{10,9},{11,10},{13,12},{... | collective-permute-start | bytes 1769480 | tf_op jit(solution)/shard_map/ppermute | solution.py:752
  23.6 24.9 %collective-permute-start.4 = (bf16[4,16,896]{2,1,0:T(8,128)(2,1)}, bf16[4,16,896]{2,1,0:T(8,128)(2,1)}, u32[]{:S(2)}, u32[]{:S(2)}) collective-permute-start(bf16[4,16,896]{2,1,0:T(8,128)(2,1)} %get-tuple-element.184), channel_id=1, source_target_pairs={{0,16},{4,4},{8,20},{12,0},{16,24},{20,12},{24,28},{28,8},{1,17},{... | collective-permute-start | bytes 344072 | tf_op jit(solution)/shard_map/ppermute | solution.py:786
  33.1 15.3 %collective-permute-start.5 = (bf16[4,16,896]{2,1,0:T(8,128)(2,1)S(1)}, bf16[4,16,896]{2,1,0:T(8,128)(2,1)S(1)}, u32[]{:S(2)}, u32[]{:S(2)}) collective-permute-start(bf16[4,16,896]{2,1,0:T(8,128)(2,1)S(1)} %copy-done.31), channel_id=1, source_target_pairs={{0,4},{4,20},{8,0},{12,16},{16,12},{20,28},{24,8},{28,24},{1,5},{5... | collective-permute-start | bytes 344072 | tf_op jit(solution)/shard_map/ppermute | solution.py:786
  55.9 37.3 %collective-permute-start.8 = (bf16[2,192,768]{2,1,0:T(8,128)(2,1)S(1)}, bf16[2,192,768]{2,1,0:T(8,128)(2,1)S(1)}, u32[]{:S(2)}, u32[]{:S(2)}) collective-permute-start(bf16[2,192,768]{2,1,0:T(8,128)(2,1)S(1)} %get-tuple-element.181), channel_id=1, source_target_pairs={{1,2},{2,3},{3,0},{5,6},{6,7},{7,4},{9,10},{10,11},{11,8},{13,14},... | collective-permute-start | bytes 1769480 | tf_op jit(solution)/shard_map/ppermute | solution.py:858
  57.2 36.0 %collective-permute-start.9 = (bf16[2,192,768]{2,1,0:T(8,128)(2,1)S(1)}, bf16[2,192,768]{2,1,0:T(8,128)(2,1)S(1)}, u32[]{:S(2)}, u32[]{:S(2)}) collective-permute-start(bf16[2,192,768]{2,1,0:T(8,128)(2,1)S(1)} %get-tuple-element.180), channel_id=1, source_target_pairs={{1,0},{2,1},{0,3},{5,4},{6,5},{4,7},{9,8},{10,9},{8,11},{13,12},{1... | collective-permute-start | bytes 1769480 | tf_op jit(solution)/shard_map/ppermute | solution.py:859
  141.9 22.0 %collective-permute-start.14 = (bf16[768,768]{1,0:T(8,128)(2,1)}, bf16[768,768]{1,0:T(8,128)(2,1)}, u32[]{:S(2)}, u32[]{:S(2)}) collective-permute-start(bf16[768,768]{1,0:T(8,128)(2,1)} %get-tuple-element.193), channel_id=1, source_target_pairs={{0,16},{16,0},{1,17},{17,1},{2,18},{18,2},{3,19},{19,3},{4,20},{20... | collective-permute-start | bytes 3538952 | tf_op jit(solution)/shard_map/ppermute | solution.py:393
  142.9 19.6 %collective-permute-start.12 = (bf16[128,768]{1,0:T(8,128)(2,1)S(1)}, bf16[128,768]{1,0:T(8,128)(2,1)}, u32[]{:S(2)}, u32[]{:S(2)}) collective-permute-start(bf16[128,768]{1,0:T(8,128)(2,1)S(1)} %get-tuple-element.174), channel_id=1, source_target_pairs={{0,2},{1,3},{2,0},{3,1},{4,6},{5,7},{6,4},{7,5},{8,10},{9,11},{10,... | collective-permute-start | bytes 589832 | tf_op jit(solution)/shard_map/ppermute | solution.py:397
  144.5 18.0 %collective-permute-start.13 = (bf16[128,768]{1,0:T(8,128)(2,1)S(1)}, bf16[128,768]{1,0:T(8,128)(2,1)}, u32[]{:S(2)}, u32[]{:S(2)}) collective-permute-start(bf16[128,768]{1,0:T(8,128)(2,1)S(1)} %get-tuple-element.173), channel_id=1, source_target_pairs={{0,1},{1,2},{2,3},{3,0},{4,5},{5,6},{6,7},{7,4},{8,9},{9,10},{10,1... | collective-permute-start | bytes 589832 | tf_op jit(solution)/shard_map/ppermute | solution.py:397
  165.6 19.7 %collective-permute-start.16 = (bf16[128,768]{1,0:T(8,128)(2,1)S(1)}, bf16[128,768]{1,0:T(8,128)(2,1)S(1)}, u32[]{:S(2)}, u32[]{:S(2)}) collective-permute-start(bf16[128,768]{1,0:T(8,128)(2,1)S(1)} %fusion.28), channel_id=1, source_target_pairs={{0,2},{1,3},{2,0},{3,1},{4,6},{5,7},{6,4},{7,5},{8,10},{9,11},{10,... | collective-permute-start | bytes 589832 | tf_op jit(solution)/shard_map/ppermute | solution.py:397
  167.3 18.0 %collective-permute-start.17 = (bf16[128,768]{1,0:T(8,128)(2,1)S(1)}, bf16[128,768]{1,0:T(8,128)(2,1)S(1)}, u32[]{:S(2)}, u32[]{:S(2)}) collective-permute-start(bf16[128,768]{1,0:T(8,128)(2,1)S(1)} %fusion.28), channel_id=1, source_target_pairs={{0,1},{1,2},{2,3},{3,0},{4,5},{5,6},{6,7},{7,4},{8,9},{9,10},{10,1... | collective-permute-start | bytes 589832 | tf_op jit(solution)/shard_map/ppermute | solution.py:397
  169.5 15.9 %collective-permute-start.18 = (bf16[192,768]{1,0:T(8,128)(2,1)S(1)}, bf16[192,768]{1,0:T(8,128)(2,1)S(1)}, u32[]{:S(2)}, u32[]{:S(2)}) collective-permute-start(bf16[192,768]{1,0:T(8,128)(2,1)S(1)} %get-tuple-element.165), channel_id=1, source_target_pairs={{0,12},{4,0},{8,4},{12,8},{1,13},{5,1},{9,5},{13,9},{2,14},{6,2},{... | collective-permute-start | bytes 884744 | tf_op jit(solution)/shard_map/ppermute | solution.py:446
  186.3 66.1 %collective-permute-start.21 = (bf16[192,768]{1,0:T(8,128)(2,1)}, bf16[192,768]{1,0:T(8,128)(2,1)}, u32[]{:S(2)}, u32[]{:S(2)}) collective-permute-start(bf16[192,768]{1,0:T(8,128)(2,1)} %add_convert_fusion.2), channel_id=1, source_target_pairs={{0,12},{4,0},{8,4},{12,8},{1,13},{5,1},{9,5},{13,9},{2,14},{6,2},{... | collective-permute-start | bytes 884744 | tf_op jit(solution)/shard_map/ppermute | solution.py:456
  187.5 66.6 %collective-permute-start.22 = (bf16[192,768]{1,0:T(8,128)(2,1)}, bf16[192,768]{1,0:T(8,128)(2,1)}, u32[]{:S(2)}, u32[]{:S(2)}) collective-permute-start(bf16[192,768]{1,0:T(8,128)(2,1)} %add_convert_fusion.2), channel_id=1, source_target_pairs={{0,8},{4,12},{8,0},{12,4},{1,9},{5,13},{9,1},{13,5},{2,10},{6,14},... | collective-permute-start | bytes 884744 | tf_op jit(solution)/shard_map/ppermute | solution.py:456
  188.5 67.4 %collective-permute-start.23 = (bf16[192,768]{1,0:T(8,128)(2,1)}, bf16[192,768]{1,0:T(8,128)(2,1)}, u32[]{:S(2)}, u32[]{:S(2)}) collective-permute-start(bf16[192,768]{1,0:T(8,128)(2,1)} %add_convert_fusion.2), channel_id=1, source_target_pairs={{0,4},{4,8},{8,12},{12,0},{1,5},{5,9},{9,13},{13,1},{2,6},{6,10},{... | collective-permute-start | bytes 884744 | tf_op jit(solution)/shard_map/ppermute | solution.py:456
  261.1 17.7 %collective-permute-start.30 = (bf16[4,576,768]{2,1,0:T(8,128)(2,1)}, bf16[4,576,768]{2,1,0:T(8,128)(2,1)}, u32[]{:S(2)}, u32[]{:S(2)}) collective-permute-start(bf16[4,576,768]{2,1,0:T(8,128)(2,1)} %get-tuple-element.127), channel_id=1, source_target_pairs={{0,16},{16,0},{1,17},{17,1},{2,18},{18,2},{3,19},{19,3},{4,20},{20... | collective-permute-start | bytes 10616840 | tf_op jit(solution)/shard_map/ppermute | solution.py:393
  261.2 17.6 %collective-permute-start.29 = (bf16[768,768]{1,0:T(8,128)(2,1)}, bf16[768,768]{1,0:T(8,128)(2,1)}, u32[]{:S(2)}, u32[]{:S(2)}) collective-permute-start(bf16[768,768]{1,0:T(8,128)(2,1)} %constant_dynamic-update-slice_fusion.7), channel_id=1, source_target_pairs={{0,16},{16,0},{1,17},{17,1},{2,18},{18,2},{3,19},{19,3},{4,20},{20... | collective-permute-start | bytes 3538952 | tf_op jit(solution)/shard_map/ppermute | solution.py:393
  278.9 19.5 %collective-permute-start.31 = (bf16[112,768]{1,0:T(8,128)(2,1)S(1)}, bf16[112,768]{1,0:T(8,128)(2,1)S(1)}, u32[]{:S(2)}, u32[]{:S(2)}) collective-permute-start(bf16[112,768]{1,0:T(8,128)(2,1)S(1)} %add_convert_fusion.3), channel_id=1, source_target_pairs={{0,12},{4,0},{8,4},{12,8},{1,13},{5,1},{9,5},{13,9},{2,14},{6,2},{... | collective-permute-start | bytes 516104 | tf_op jit(solution)/shard_map/ppermute | solution.py:456
  280.2 18.2 %collective-permute-start.32 = (bf16[112,768]{1,0:T(8,128)(2,1)S(1)}, bf16[112,768]{1,0:T(8,128)(2,1)S(1)}, u32[]{:S(2)}, u32[]{:S(2)}) collective-permute-start(bf16[112,768]{1,0:T(8,128)(2,1)S(1)} %add_convert_fusion.3), channel_id=1, source_target_pairs={{0,8},{4,12},{8,0},{12,4},{1,9},{5,13},{9,1},{13,5},{2,10},{6,14},... | collective-permute-start | bytes 516104 | tf_op jit(solution)/shard_map/ppermute | solution.py:456
  281.3 21.0 %collective-permute-start.33 = (bf16[112,768]{1,0:T(8,128)(2,1)S(1)}, bf16[112,768]{1,0:T(8,128)(2,1)S(1)}, u32[]{:S(2)}, u32[]{:S(2)}) collective-permute-start(bf16[112,768]{1,0:T(8,128)(2,1)S(1)} %add_convert_fusion.3), channel_id=1, source_target_pairs={{0,4},{4,8},{8,12},{12,0},{1,5},{5,9},{9,13},{13,1},{2,6},{6,10},{... | collective-permute-start | bytes 516104 | tf_op jit(solution)/shard_map/ppermute | solution.py:456
  286.2 16.2 %collective-permute-start.34 = (bf16[4,16,768]{2,1,0:T(8,128)(2,1)S(1)}, bf16[4,16,768]{2,1,0:T(8,128)(2,1)S(1)}, u32[]{:S(2)}, u32[]{:S(2)}) collective-permute-start(bf16[4,16,768]{2,1,0:T(8,128)(2,1)S(1)} %get-tuple-element.189), channel_id=1, source_target_pairs={{0,0},{16,4},{4,8},{20,12},{8,16},{24,20},{12,24},{28,28},{1,1},{1... | collective-permute-start | bytes 294920 | tf_op jit(solution)/shard_map/ppermute | solution.py:1041
  286.9 15.5 %collective-permute-start.35 = (bf16[4,16,768]{2,1,0:T(8,128)(2,1)S(1)}, bf16[4,16,768]{2,1,0:T(8,128)(2,1)S(1)}, u32[]{:S(2)}, u32[]{:S(2)}) collective-permute-start(bf16[4,16,768]{2,1,0:T(8,128)(2,1)S(1)} %get-tuple-element.188), channel_id=1, source_target_pairs={{16,0},{4,4},{20,8},{0,12},{24,16},{12,20},{28,24},{8,28},{17,1},{... | collective-permute-start | bytes 294920 | tf_op jit(solution)/shard_map/ppermute | solution.py:1041
  (58 other events, 566.9 us)
Sparse Core Ops, SparseCore 0:
  193.8 43.3 all-reduce.1

commit v4 on v3

--- a/solution.py
+++ b/solution.py
@@ -410,11 +410,14 @@
     return [lax.dynamic_index_in_dim(part, place, 0, False)] + others
 
 
-def reduce_over_head(chunks, count):
-    total = chunks[0]
-    for shift in range(1, count):
-        total = total + head_shift(chunks[shift], shift, count).astype(F32)
-    return total.astype(BF16)
+def head_exchange(chunks, count):
+    return [head_shift(chunks[shift], shift, count) for shift in range(1, count)]
+
+
+def head_sum(own, received):
+    for part in received:
+        own = own + part.astype(F32)
+    return own.astype(BF16)
 
 
 def gather_head(total, place, count):
@@ -916,22 +919,24 @@
     d_pre = gelu_pull(dot("bld,fd->blf", cot, down_weight))[0].astype(BF16)
     d_mlp_part = dot("blf,df->bld", d_pre, up_weight)
     d_mlp_part, activ, d_pre = lax.optimization_barrier((d_mlp_part, activ, d_pre))
-    d_mlp_total = reduce_over_head(head_chunks(d_mlp_part, z, head_count), head_count)
+    chunks = head_chunks(d_mlp_part, z, head_count)
+    received = head_exchange(chunks, head_count)
+    activ, d_pre, received[0] = lax.optimization_barrier((activ, d_pre, received[0]))
+    d_mlp_total = head_sum(chunks[0], received)
     grad_down = dot("blf,bld->fd", activ, cot).astype(BF16)
     grad_up = dot("bld,blf->df", mlp_norm, d_pre).astype(BF16)
     near, far, _ = lax.optimization_barrier((near, far, d_mlp_part))
     weights = both_halves(near, far)
     early = jnp.where(core == 0, grad_up, grad_down).astype(F32)
     early = early + swap_cores(jnp.where(core == 0, grad_down, grad_up)).astype(F32)
-    d_mlp_total, early = lax.optimization_barrier((d_mlp_total, early))
-    early = reduce_over_group(early, place_index, txt_count)
     d_mlp_norm = gather_head(d_mlp_total, z, head_count)
-    growth = dot("blf,fd->bld", activ, down_weight).astype(BF16)
+    activ, _ = lax.optimization_barrier((activ, d_mlp_total))
+    growth = head_chunks(dot("blf,fd->bld", activ, down_weight), z, head_count)
     growth, d_mlp_norm, weights, early = lax.optimization_barrier(
-        (growth, d_mlp_norm, weights, early)
-    )
-    early = gather_places(early, place_index, txt_count)
-    growth = lax.psum(growth, "head")
+        (growth, d_mlp_norm, weights, early.astype(BF16))
+    )
+    early = lax.psum(early, "txt")
+    growth_received = head_exchange(growth, head_count)
 
     d_after_norm, gain_mlp_part = norm_back_rows(after_attn, gain_mlp, d_mlp_norm.astype(F32))
     d_after = cot.astype(F32) + d_after_norm
@@ -1025,15 +1030,18 @@
             ),
         )(scalars, video_grad, latent_grad, part, part)
 
-    early, growth, late = lax.optimization_barrier((early, growth, late))
+    early, growth_received, late = lax.optimization_barrier((early, growth_received, late))
     late_half, late_swapped = reduce_over_cores(late, core)
     other_back, early, _ = lax.optimization_barrier((other_back, early, late_swapped))
     other_here = swap_cores(other_back)
+    growth_received, _ = lax.optimization_barrier((growth_received, late_swapped))
+    growth = head_sum(growth[0], growth_received)
     early_other = swap_cores(early)
     late_total = reduce_over_group(late_half, place_index, txt_count)
-    late_total, early_other, other_here, cap_back = lax.optimization_barrier(
-        (late_total, early_other, other_here, cap_back)
-    )
+    late_total, growth, early_other, other_here, cap_back = lax.optimization_barrier(
+        (late_total, growth, early_other, other_here, cap_back)
+    )
+    growth = gather_head(growth, z, head_count)
     cap_parts = []
     for step in range(txt_count):
         perm = [(b, a) for a, b in caption_perm(step, 2, txt_count, 2)]
@@ -1042,8 +1050,8 @@
         )
     late = gather_places(late_total, place_index, txt_count)
     video_grad, latent_grad = place(video_grad, latent_grad, other_here)
-    late, video_grad, latent_grad, cap_parts = lax.optimization_barrier(
-        (late, video_grad, latent_grad, cap_parts)
+    late, video_grad, latent_grad, cap_parts, growth = lax.optimization_barrier(
+        (late, video_grad, latent_grad, cap_parts, growth)
     )
     late = gather_cores(late, core).astype(F32)
     caption_grad = jnp.zeros((txt_count, own, cap_here, D), F32)

time: 322 us -> 316 us (0.981)
  local copies, waits for them, and re-layouts: 43.8 us -> 33.5 us
  waiting for transfers between devices: 32.1 us -> 41.7 us
  starting transfers between devices: 61 us -> 55 us
    ppermute x6 -> x12, starting transfers between devices: 7.27 us -> 13.6 us  [head_shift(): lax.ppermute(values, 'head', [(i, (i - shift) % count) for i in range(cou...]
    ppermute x6 -> x3, starting transfers between devices: 8.61 us -> 2.65 us  [reduce_over_group(): total = total + lax.ppermute(chunk, 'txt', perm).astype(F32)]
    ppermute x6 -> x12, waiting for transfers between devices: 20.2 us -> 25.2 us  [head_shift(): lax.ppermute(values, 'head', [(i, (i - shift) % count) for i in range(cou...]
    dynamic_update_slice x6 -> x3, local copies, waits for them, and re-layouts: 5.17 us -> 1.89 us  [gather_places(): lax.dynamic_update_slice_in_dim(mine, lax.ppermute(total, 'txt', perm), (...]
    ppermute x6 -> x3, waiting for transfers between devices: 4.71 us -> 7.68 us  [reduce_over_group(): total = total + lax.ppermute(chunk, 'txt', perm).astype(F32)]
    unnamed x87 -> x91, local copies, waits for them, and re-layouts: 11 us -> 9.38 us
  transfers between devices with their start and end apart: 40 -> 40, of which waited for: 9 -> 9; matrix products, arithmetic and copies ran while one was open for 14% -> 12% of each run, Pallas kernels for 31% -> 32%
where the time goes in v4:
time: 316 us; the launch traced here: 314 us
  Pallas kernels  128 us (41%)
  starting transfers between devices  55 us (17%)
  waiting for transfers between devices  41.7 us (13%)
  local copies, waits for them, and re-layouts  33.5 us (11%)
  other arithmetic  26.7 us (8%)
  between operations  17.2 us (5%)
  matrix products  12.5 us (4%)
    pallas_call x4, Pallas kernels, call(): pl.pallas_call(kernel, name=name, grid_spec=pltpu.PrefetchScalarGridSpec(...  122 us
    ppermute x12, waiting for transfers between devices, head_shift(): lax.ppermute(values, 'head', [(i, (i - shift) % count) for i in range(cou...  25.2 us
    ppermute x12, starting transfers between devices, head_shift(): lax.ppermute(values, 'head', [(i, (i - shift) % count) for i in range(cou...  13.6 us
    dot_general x8, matrix products, dot(): return jnp.einsum(spec, a, b, preferred_element_type=F32)  12.5 us
    ppermute x4, starting transfers between devices, local(): lax.ppermute(block, ('vid', 'txt'), caption_perm(step, 2, txt_count, 2))  10.1 us
    unnamed x91, local copies, waits for them, and re-layouts  9.38 us
    ppermute x3, waiting for transfers between devices, reduce_over_group(): total = total + lax.ppermute(chunk, 'txt', perm).astype(F32)  7.68 us
    ppermute x4, starting transfers between devices, local(): lax.ppermute(cap_back[:, step * cap_here:(step + 1) * cap_here], ('vid',...  7.45 us
  transfers between devices with their start and end apart: 40, of which 9 were waited for; matrix products, arithmetic and copies ran while one was open for 12% of the time, Pallas kernels for 32%

profile of v4, /device:TPU:0, one launch (start us, length us, event | category | flops | bytes accessed | tf_op | source)
XLA Modules:
  0.0 314.0 jit_solution(17074608438035362537)
XLA Ops:
  7.3 2.2 constant_dynamic-slice_fusion.7
  14.6 5.4 %collective-permute-start.1 = (bf16[2,192,768]{2,1,0:T(8,128)(2,1)}, bf16[2,192,768]{2,1,0:T(8,128)(2,1)}, u32[]{:S(2)}, u32[]{:S(2)}) collective-permute-start(bf16[2,192,768]{2,1,0:T(8,128)(2,1)} %constant_dynamic-slice_fusion.4), channel_id=1, source_target_pairs={{0,1},{1,2},{2,3},{4,5},{5,6},{6,7},{8,9},{9,10},{10,11},{12,13},{... | collective-permute-start | bytes 1769480 | tf_op jit(solution)/shard_map/ppermute | solution.py:754
  23.0 2.1 collective-permute-start.3
  25.1 3.3 %collective-permute-start.4 = (bf16[4,16,896]{2,1,0:T(8,128)(2,1)}, bf16[4,16,896]{2,1,0:T(8,128)(2,1)}, u32[]{:S(2)}, u32[]{:S(2)}) collective-permute-start(bf16[4,16,896]{2,1,0:T(8,128)(2,1)} %get-tuple-element.210), channel_id=1, source_target_pairs={{0,16},{4,4},{8,20},{12,0},{16,24},{20,12},{24,28},{28,8},{1,17},{... | collective-permute-start | bytes 344072 | tf_op jit(solution)/shard_map/ppermute | solution.py:789
  35.6 4.3 %collective-permute-start.6 = (bf16[4,16,896]{2,1,0:T(8,128)(2,1)S(1)}, bf16[4,16,896]{2,1,0:T(8,128)(2,1)S(1)}, u32[]{:S(2)}, u32[]{:S(2)}) collective-permute-start(bf16[4,16,896]{2,1,0:T(8,128)(2,1)S(1)} %copy-done.32), channel_id=1, source_target_pairs={{0,20},{4,0},{8,16},{12,4},{16,28},{20,8},{24,24},{28,12},{1,21},{... | collective-permute-start | bytes 344072 | tf_op jit(solution)/shard_map/ppermute | solution.py:789
  39.9 10.7 %token_norm.1.tok_ref = bf16[4,1024,768]{2,1,0:T(8,128)(2,1)} custom-call(s32[8]{0:T(128)} %concatenate.32.s_ref, bf16[8,512,768]{2,1,0:T(8,128)(2,1)} %own_ref.3, bf16[4,640,768]{2,1,0:T(8,128)(2,1)} %collective-permute-done.other_ref, f32[1,768]{1,0:T(1,128)} %broadcast_in_dim.124.gain_ref), custom_call_target="tpu_custom_call" | custom-call | flops 9900000256 | bytes 9000000 | tf_op jit(solution)/shard_map/token_norm/pallas_call | solution.py:820
  58.9 7.2 %collective-permute-start.9 = (bf16[2,192,768]{2,1,0:T(8,128)(2,1)S(1)}, bf16[2,192,768]{2,1,0:T(8,128)(2,1)S(1)}, u32[]{:S(2)}, u32[]{:S(2)}) collective-permute-start(bf16[2,192,768]{2,1,0:T(8,128)(2,1)S(1)} %get-tuple-element.206), channel_id=1, source_target_pairs={{1,0},{2,1},{0,3},{5,4},{6,5},{4,7},{9,8},{10,9},{8,11},{13,12},{1... | collective-permute-start | bytes 1769480 | tf_op jit(solution)/shard_map/ppermute | solution.py:862
  67.7 27.4 %attention_forward.2 = (bf16[4,128,768]{2,1,0:T(8,128)(2,1)}, bf16[4,1088,768]{2,1,0:T(8,128)(2,1)}, bf16[4,1088,768]{2,1,0:T(8,128)(2,1)}, f32[4,2,8,256]{3,2,1,0:T(8,128)}, f32[4,128,768]{2,1,0:T(8,128)}) custom-call(s32[8]{0:T(128)} %concatenate.32.s_ref, bf16[4,1024,768]{2,1,0:T(8,128)(2,1)} %token_norm.1.tok_ref, bf16[4,64,896]{2,1,0:T(8,128)(2,1)} %copy-done.26, ...), custom_call_target="tpu_custom_call" | custom-call | flops 25300000768 | bytes 23000000 | tf_op jit(solution)/shard_map/attention_forward/pallas_call | solution.py:820
  103.4 27.5 %attention_forward.3 = (bf16[4,128,768]{2,1,0:T(8,128)(2,1)}, bf16[4,1088,768]{2,1,0:T(8,128)(2,1)}, bf16[4,1088,768]{2,1,0:T(8,128)(2,1)}, f32[4,2,8,256]{3,2,1,0:T(8,128)}, f32[4,128,768]{2,1,0:T(8,128)}) custom-call(s32[8]{0:T(128)} %concatenate.31.s_ref, ...), custom_call_target="tpu_custom_call", output_to_operand_aliasing={{0}: (8, {}), {1}: (9, {}), {2}: (10, {}), {3}: (11, {}), {... | custom-call | flops 25300000768 | bytes 23000000 | tf_op jit(solution)/shard_map/attention_forward/pallas_call | solution.py:820
  131.0 2.3 fusion.44
  134.0 3.9 %multiply_convert_fusion.1 = (bf16[4,128,768]{2,1,0:T(8,128)(2,1)S(1)}, f32[4,128,768]{2,1,0:T(8,128)S(1)}, f32[4,128,768]{2,1,0:T(8,128)S(1)}) fusion(bf16[768,768]{1,0:T(8,128)(2,1)S(1)} %copy-done, f32[4,128,768]{2,1,0:T(8,128)S(1)} %get-tuple-element.217, f32[768]{0:T(1024)S(1)} %copy-done.38, f32[4,128]{1,0:T(4,128)S(1)} %add_rsqrt_fusion, ...), kind=kOutput, calls=%fused_computation.22 | convolution fusion | flops 631111680 | bytes 6691840 | tf_op jit(solution)/shard_map/bld,df->blf/dot_general | solution.py:750
  145.9 2.2 collective-permute-done.11
  148.0 11.6 %collective-permute-done.12 = bf16[128,768]{1,0:T(8,128)(2,1)S(1)} collective-permute-done((bf16[128,768]{1,0:T(8,128)(2,1)S(1)}, bf16[128,768]{1,0:T(8,128)(2,1)S(1)}, u32[]{:S(2)}, u32[]{:S(2)}) %collective-permute-start.12) | collective-permute-done | bytes 196640 | tf_op jit(solution)/shard_map/ppermute | solution.py:397
  167.6 11.4 %collective-permute-done.15 = bf16[128,768]{1,0:T(8,128)(2,1)S(1)} collective-permute-done((bf16[128,768]{1,0:T(8,128)(2,1)S(1)}, bf16[128,768]{1,0:T(8,128)(2,1)S(1)}, u32[]{:S(2)}, u32[]{:S(2)}) %collective-permute-start.15) | collective-permute-done | bytes 196640 | tf_op jit(solution)/shard_map/ppermute | solution.py:397
  191.6 56.0 %attention_backward.1 = (f32[8,512,768]{2,1,0:T(8,128)}, bf16[4,576,768]{2,1,0:T(8,128)(2,1)}, bf16[4,64,768]{2,1,0:T(8,128)(2,1)}, f32[8,64,768]{2,1,0:T(8,128)}, bf16[896,768]{1,0:T(8,128)(2,1)}) custom-call(s32[8]{0:T(128)} %concatenate.32.s_ref, bf16[4,128,768]{2,1,0:T(8,128)(2,1)} %get-tuple-element.129.q_ref, ...), custom_call_target="tpu_custom_call" | custom-call | flops 3300000000 | bytes 3000000 | tf_op jit(solution)/shard_map/attention_backward/pallas_call | solution.py:820
  248.8 2.1 collective-permute-done.21
  256.7 3.4 %collective-permute-done.22 = bf16[112,768]{1,0:T(8,128)(2,1)S(1)} collective-permute-done((bf16[112,768]{1,0:T(8,128)(2,1)S(1)}, bf16[112,768]{1,0:T(8,128)(2,1)S(1)}, u32[]{:S(2)}, u32[]{:S(2)}) %collective-permute-start.22) | collective-permute-done | bytes 172064 | tf_op jit(solution)/shard_map/ppermute | solution.py:449
  260.2 4.3 %collective-permute-done.23 = bf16[112,768]{1,0:T(8,128)(2,1)S(1)} collective-permute-done((bf16[112,768]{1,0:T(8,128)(2,1)S(1)}, bf16[112,768]{1,0:T(8,128)(2,1)S(1)}, u32[]{:S(2)}, u32[]{:S(2)}) %collective-permute-start.23) | collective-permute-done | bytes 172064 | tf_op jit(solution)/shard_map/ppermute | solution.py:449
  270.3 3.8 %select_convert_fusion = (f32[768,768]{1,0:T(8,128)}, f32[768,768]{1,0:T(8,128)}) fusion(bf16[768,768]{1,0:T(8,128)(2,1)} %collective-permute-done.25, bf16[768,768]{1,0:T(8,128)(2,1)S(1)} %copy-done.22, pred[]{:T(512)S(6)} %eq.65), kind=kLoop, calls=%fused_computation.54 | loop fusion | flops 2359296 | bytes 7077889 | tf_op jit(solution)/shard_map/convert_element_type | solution.py:1084
  274.8 6.0 %place_rows.1 = (f32[8,512,768]{2,1,0:T(8,128)}, f32[8,64,768]{2,1,0:T(8,128)}) custom-call(s32[8]{0:T(128)} %concatenate.32.s_ref, f32[8,512,768]{2,1,0:T(8,128)} %get-tuple-element.152.video_in, f32[8,64,768]{2,1,0:T(8,128)} %get-tuple-element.153.lat_in, ...), custom_call_target="tpu_custom_call", output_to_operand_aliasing={{0}: (1, {}), {1}: (2, {})} | custom-call | flops 6000000000 | bytes 10000000 | tf_op jit(solution)/shard_map/place_rows/pallas_call | solution.py:1006
  284.5 2.9 collective-permute-done.29
  287.3 2.8 collective-permute-start.31
  291.3 3.9 %collective-permute-start.33 = (bf16[4,16,768]{2,1,0:T(8,128)(2,1)S(1)}, bf16[4,16,768]{2,1,0:T(8,128)(2,1)S(1)}, u32[]{:S(2)}, u32[]{:S(2)}) collective-permute-start(bf16[4,16,768]{2,1,0:T(8,128)(2,1)S(1)} %copy-done.34), channel_id=1, source_target_pairs={{20,0},{0,4},{16,8},{4,12},{28,16},{8,20},{24,24},{12,28},{21,1},{... | collective-permute-start | bytes 294920 | tf_op jit(solution)/shard_map/ppermute | solution.py:1049
  295.3 2.1 collective-permute-done.33
  (253 shorter events, 88.0 us)
Async XLA Ops:
  7.2 240.4 %all-reduce.2.cloned.1.call-start = ((), (), s32[]{:S(2)}) async-start(), calls=%async_computation | async-start | bytes 2359296 | tf_op jit(solution)/shard_map/psum | solution.py:938
  11.8 23.8 %collective-permute-start = (bf16[4,640,768]{2,1,0:T(8,128)(2,1)}, bf16[4,640,768]{2,1,0:T(8,128)(2,1)}, u32[]{:S(2)}, u32[]{:S(2)}) collective-permute-start(bf16[4,640,768]{2,1,0:T(8,128)(2,1)} %pad_maximum_fusion), channel_id=1, source_target_pairs={{0,16},{16,0},{1,17},{17,1},{2,18},{18,2},{3,19},{19,3},{4,20},{20... | collective-permute-start | bytes 11796488 | tf_op jit(solution)/shard_map/ppermute | solution.py:393
  14.6 36.0 %collective-permute-start.1 = (bf16[2,192,768]{2,1,0:T(8,128)(2,1)}, bf16[2,192,768]{2,1,0:T(8,128)(2,1)}, u32[]{:S(2)}, u32[]{:S(2)}) collective-permute-start(bf16[2,192,768]{2,1,0:T(8,128)(2,1)} %constant_dynamic-slice_fusion.4), channel_id=1, source_target_pairs={{0,1},{1,2},{2,3},{4,5},{5,6},{6,7},{8,9},{9,10},{10,11},{12,13},{... | collective-permute-start | bytes 1769480 | tf_op jit(solution)/shard_map/ppermute | solution.py:754
  20.0 30.7 %collective-permute-start.2 = (bf16[2,192,768]{2,1,0:T(8,128)(2,1)}, bf16[2,192,768]{2,1,0:T(8,128)(2,1)}, u32[]{:S(2)}, u32[]{:S(2)}) collective-permute-start(bf16[2,192,768]{2,1,0:T(8,128)(2,1)} %constant_dynamic-slice_fusion.4), channel_id=1, source_target_pairs={{1,0},{2,1},{3,2},{5,4},{6,5},{7,6},{9,8},{10,9},{11,10},{13,12},{... | collective-permute-start | bytes 1769480 | tf_op jit(solution)/shard_map/ppermute | solution.py:755
  25.1 25.5 %collective-permute-start.4 = (bf16[4,16,896]{2,1,0:T(8,128)(2,1)}, bf16[4,16,896]{2,1,0:T(8,128)(2,1)}, u32[]{:S(2)}, u32[]{:S(2)}) collective-permute-start(bf16[4,16,896]{2,1,0:T(8,128)(2,1)} %get-tuple-element.210), channel_id=1, source_target_pairs={{0,16},{4,4},{8,20},{12,0},{16,24},{20,12},{24,28},{28,8},{1,17},{... | collective-permute-start | bytes 344072 | tf_op jit(solution)/shard_map/ppermute | solution.py:789
  35.2 15.4 %collective-permute-start.5 = (bf16[4,16,896]{2,1,0:T(8,128)(2,1)S(1)}, bf16[4,16,896]{2,1,0:T(8,128)(2,1)S(1)}, u32[]{:S(2)}, u32[]{:S(2)}) collective-permute-start(bf16[4,16,896]{2,1,0:T(8,128)(2,1)S(1)} %copy-done.33), channel_id=1, source_target_pairs={{0,4},{4,20},{8,0},{12,16},{16,12},{20,28},{24,8},{28,24},{1,5},{5... | collective-permute-start | bytes 344072 | tf_op jit(solution)/shard_map/ppermute | solution.py:789
  35.6 15.0 %collective-permute-start.6 = (bf16[4,16,896]{2,1,0:T(8,128)(2,1)S(1)}, bf16[4,16,896]{2,1,0:T(8,128)(2,1)S(1)}, u32[]{:S(2)}, u32[]{:S(2)}) collective-permute-start(bf16[4,16,896]{2,1,0:T(8,128)(2,1)S(1)} %copy-done.32), channel_id=1, source_target_pairs={{0,20},{4,0},{8,16},{12,4},{16,28},{20,8},{24,24},{28,12},{1,21},{... | collective-permute-start | bytes 344072 | tf_op jit(solution)/shard_map/ppermute | solution.py:789
  57.6 37.4 %collective-permute-start.8 = (bf16[2,192,768]{2,1,0:T(8,128)(2,1)S(1)}, bf16[2,192,768]{2,1,0:T(8,128)(2,1)S(1)}, u32[]{:S(2)}, u32[]{:S(2)}) collective-permute-start(bf16[2,192,768]{2,1,0:T(8,128)(2,1)S(1)} %get-tuple-element.207), channel_id=1, source_target_pairs={{1,2},{2,3},{3,0},{5,6},{6,7},{7,4},{9,10},{10,11},{11,8},{13,14},... | collective-permute-start | bytes 1769480 | tf_op jit(solution)/shard_map/ppermute | solution.py:861
  58.9 36.2 %collective-permute-start.9 = (bf16[2,192,768]{2,1,0:T(8,128)(2,1)S(1)}, bf16[2,192,768]{2,1,0:T(8,128)(2,1)S(1)}, u32[]{:S(2)}, u32[]{:S(2)}) collective-permute-start(bf16[2,192,768]{2,1,0:T(8,128)(2,1)S(1)} %get-tuple-element.206), channel_id=1, source_target_pairs={{1,0},{2,1},{0,3},{5,4},{6,5},{4,7},{9,8},{10,9},{8,11},{13,12},{1... | collective-permute-start | bytes 1769480 | tf_op jit(solution)/shard_map/ppermute | solution.py:862
  140.1 19.6 %collective-permute-start.12 = (bf16[128,768]{1,0:T(8,128)(2,1)S(1)}, bf16[128,768]{1,0:T(8,128)(2,1)S(1)}, u32[]{:S(2)}, u32[]{:S(2)}) collective-permute-start(bf16[128,768]{1,0:T(8,128)(2,1)S(1)} %get-tuple-element.198), channel_id=1, source_target_pairs={{0,2},{1,3},{2,0},{3,1},{4,6},{5,7},{6,4},{7,5},{8,10},{9,11},{10,... | collective-permute-start | bytes 589832 | tf_op jit(solution)/shard_map/ppermute | solution.py:397
  141.6 18.0 %collective-permute-start.13 = (bf16[128,768]{1,0:T(8,128)(2,1)S(1)}, bf16[128,768]{1,0:T(8,128)(2,1)S(1)}, u32[]{:S(2)}, u32[]{:S(2)}) collective-permute-start(bf16[128,768]{1,0:T(8,128)(2,1)S(1)} %get-tuple-element.199), channel_id=1, source_target_pairs={{0,1},{1,2},{2,3},{3,0},{4,5},{5,6},{6,7},{7,4},{8,9},{9,10},{10,1... | collective-permute-start | bytes 589832 | tf_op jit(solution)/shard_map/ppermute | solution.py:397
  159.9 19.1 %collective-permute-start.15 = (bf16[128,768]{1,0:T(8,128)(2,1)S(1)}, bf16[128,768]{1,0:T(8,128)(2,1)S(1)}, u32[]{:S(2)}, u32[]{:S(2)}) collective-permute-start(bf16[128,768]{1,0:T(8,128)(2,1)S(1)} %get-tuple-element.179), channel_id=1, source_target_pairs={{0,2},{1,3},{2,0},{3,1},{4,6},{5,7},{6,4},{7,5},{8,10},{9,11},{10,... | collective-permute-start | bytes 589832 | tf_op jit(solution)/shard_map/ppermute | solution.py:397
  161.3 17.7 %collective-permute-start.16 = (bf16[128,768]{1,0:T(8,128)(2,1)S(1)}, bf16[128,768]{1,0:T(8,128)(2,1)S(1)}, u32[]{:S(2)}, u32[]{:S(2)}) collective-permute-start(bf16[128,768]{1,0:T(8,128)(2,1)S(1)} %get-tuple-element.179), channel_id=1, source_target_pairs={{0,1},{1,2},{2,3},{3,0},{4,5},{5,6},{6,7},{7,4},{8,9},{9,10},{10,1... | collective-permute-start | bytes 589832 | tf_op jit(solution)/shard_map/ppermute | solution.py:397
  165.1 14.0 %collective-permute-start.17 = (bf16[768,768]{1,0:T(8,128)(2,1)S(1)}, bf16[768,768]{1,0:T(8,128)(2,1)S(1)}, u32[]{:S(2)}, u32[]{:S(2)}) collective-permute-start(bf16[768,768]{1,0:T(8,128)(2,1)S(1)} %get-tuple-element.221), channel_id=1, source_target_pairs={{0,16},{16,0},{1,17},{17,1},{2,18},{18,2},{3,19},{19,3},{4,20},{20... | collective-permute-start | bytes 3538952 | tf_op jit(solution)/shard_map/ppermute | solution.py:393
  188.5 59.0 %collective-permute-start.18 = (bf16[128,768]{1,0:T(8,128)(2,1)S(1)}, bf16[128,768]{1,0:T(8,128)(2,1)}, u32[]{:S(2)}, u32[]{:S(2)}) collective-permute-start(bf16[128,768]{1,0:T(8,128)(2,1)S(1)} %copy-done.31), channel_id=1, source_target_pairs={{0,3},{1,0},{2,1},{3,2},{4,7},{5,4},{6,5},{7,6},{8,11},{9,8},{10,9... | collective-permute-start | bytes 589832 | tf_op jit(solution)/shard_map/ppermute | solution.py:397
  188.6 59.0 %collective-permute-start.19 = (bf16[128,768]{1,0:T(8,128)(2,1)S(1)}, bf16[128,768]{1,0:T(8,128)(2,1)}, u32[]{:S(2)}, u32[]{:S(2)}) collective-permute-start(bf16[128,768]{1,0:T(8,128)(2,1)S(1)} %copy-done.30), channel_id=1, source_target_pairs={{0,2},{1,3},{2,0},{3,1},{4,6},{5,7},{6,4},{7,5},{8,10},{9,11},{10,... | collective-permute-start | bytes 589832 | tf_op jit(solution)/shard_map/ppermute | solution.py:397
  189.6 58.0 %collective-permute-start.20 = (bf16[128,768]{1,0:T(8,128)(2,1)S(1)}, bf16[128,768]{1,0:T(8,128)(2,1)}, u32[]{:S(2)}, u32[]{:S(2)}) collective-permute-start(bf16[128,768]{1,0:T(8,128)(2,1)S(1)} %copy-done.29), channel_id=1, source_target_pairs={{0,1},{1,2},{2,3},{3,0},{4,5},{5,6},{6,7},{7,4},{8,9},{9,10},{10,1... | collective-permute-start | bytes 589832 | tf_op jit(solution)/shard_map/ppermute | solution.py:397
  251.0 13.5 %collective-permute-start.26 = (bf16[4,576,768]{2,1,0:T(8,128)(2,1)}, bf16[4,576,768]{2,1,0:T(8,128)(2,1)}, u32[]{:S(2)}, u32[]{:S(2)}) collective-permute-start(bf16[4,576,768]{2,1,0:T(8,128)(2,1)} %get-tuple-element.149), channel_id=1, source_target_pairs={{0,16},{16,0},{1,17},{17,1},{2,18},{18,2},{3,19},{19,3},{4,20},{20... | collective-permute-start | bytes 10616840 | tf_op jit(solution)/shard_map/ppermute | solution.py:393
  251.1 13.4 %collective-permute-start.25 = (bf16[768,768]{1,0:T(8,128)(2,1)}, bf16[768,768]{1,0:T(8,128)(2,1)}, u32[]{:S(2)}, u32[]{:S(2)}) collective-permute-start(bf16[768,768]{1,0:T(8,128)(2,1)} %all-reduce.2.cloned.1.call-done), channel_id=1, source_target_pairs={{0,16},{16,0},{1,17},{17,1},{2,18},{18,2},{3,19},{19,3},{4,20},{20... | collective-permute-start | bytes 3538952 | tf_op jit(solution)/shard_map/ppermute | solution.py:393
  264.5 25.7 %collective-permute-start.34 = (bf16[128,768]{1,0:T(8,128)(2,1)S(1)}, bf16[128,768]{1,0:T(8,128)(2,1)}, u32[]{:S(2)}, u32[]{:S(2)}) collective-permute-start(bf16[128,768]{1,0:T(8,128)(2,1)S(1)} %add_convert_fusion.3), channel_id=1, source_target_pairs={{0,3},{1,0},{2,1},{3,2},{4,7},{5,4},{6,5},{7,6},{8,11},{9,8},{10,9... | collective-permute-start | bytes 589832 | tf_op jit(solution)/shard_map/ppermute | solution.py:397
  266.6 24.6 %collective-permute-start.35 = (bf16[128,768]{1,0:T(8,128)(2,1)S(1)}, bf16[128,768]{1,0:T(8,128)(2,1)S(1)}, u32[]{:S(2)}, u32[]{:S(2)}) collective-permute-start(bf16[128,768]{1,0:T(8,128)(2,1)S(1)} %add_convert_fusion.3), channel_id=1, source_target_pairs={{0,2},{1,3},{2,0},{3,1},{4,6},{5,7},{6,4},{7,5},{8,10},{9,11},{10,... | collective-permute-start | bytes 589832 | tf_op jit(solution)/shard_map/ppermute | solution.py:397
  266.6 28.6 %collective-permute-start.36 = (bf16[128,768]{1,0:T(8,128)(2,1)S(1)}, bf16[128,768]{1,0:T(8,128)(2,1)S(1)}, u32[]{:S(2)}, u32[]{:S(2)}) collective-permute-start(bf16[128,768]{1,0:T(8,128)(2,1)S(1)} %add_convert_fusion.3), channel_id=1, source_target_pairs={{0,1},{1,2},{2,3},{3,0},{4,5},{5,6},{6,7},{7,4},{8,9},{9,10},{10,1... | collective-permute-start | bytes 589832 | tf_op jit(solution)/shard_map/ppermute | solution.py:397
  268.2 12.8 %collective-permute-start.27 = (bf16[112,768]{1,0:T(8,128)(2,1)S(1)}, bf16[112,768]{1,0:T(8,128)(2,1)}, u32[]{:S(2)}, u32[]{:S(2)}) collective-permute-start(bf16[112,768]{1,0:T(8,128)(2,1)S(1)} %add_convert_fusion.4), channel_id=1, source_target_pairs={{0,12},{4,0},{8,4},{12,8},{1,13},{5,1},{9,5},{13,9},{2,14},{6,2},{... | collective-permute-start | bytes 516104 | tf_op jit(solution)/shard_map/ppermute | solution.py:459
  268.9 14.0 %collective-permute-start.28 = (bf16[112,768]{1,0:T(8,128)(2,1)S(1)}, bf16[112,768]{1,0:T(8,128)(2,1)}, u32[]{:S(2)}, u32[]{:S(2)}) collective-permute-start(bf16[112,768]{1,0:T(8,128)(2,1)S(1)} %add_convert_fusion.4), channel_id=1, source_target_pairs={{0,8},{4,12},{8,0},{12,4},{1,9},{5,13},{9,1},{13,5},{2,10},{6,14},... | collective-permute-start | bytes 516104 | tf_op jit(solution)/shard_map/ppermute | solution.py:459
  (60 other events, 753.6 us)
Sparse Core Ops, SparseCore 0:
  182.1 52.4 all-reduce.1

commit v5 on v4

--- a/solution.py
+++ b/solution.py
@@ -420,14 +420,19 @@
     return own.astype(BF16)
 
 
-def gather_head(total, place, count):
+def place_head(total, parts, place, count):
     result = jnp.zeros((count,) + total.shape, BF16)
     result = lax.dynamic_update_index_in_dim(result, total, place, 0)
     for shift in range(1, count):
         result = lax.dynamic_update_index_in_dim(
-            result, head_shift(total, shift, count), (place + shift) % count, 0
+            result, parts[shift - 1], (place + shift) % count, 0
         )
     return result
+
+
+def gather_head(total, place, count):
+    parts = [head_shift(total, shift, count) for shift in range(1, count)]
+    return place_head(total, parts, place, count)
 
 
 def group_steps(count):
@@ -450,15 +455,17 @@
     return total.astype(BF16)
 
 
-def gather_places(total, place, count):
+def gather_places(total, place, count, after):
     part = total.shape[0]
+    received = [lax.ppermute(total, "txt", perm) for _, perm in group_steps(count)]
+    received[0], after = lax.optimization_barrier((received[0], after))
     mine = jnp.zeros((part * count, total.shape[1]), BF16)
     mine = lax.dynamic_update_slice_in_dim(mine, total, place * part, 0)
-    for step, perm in group_steps(count):
+    for step in range(1, count):
         mine = lax.dynamic_update_slice_in_dim(
-            mine, lax.ppermute(total, "txt", perm), (place + step) % count * part, 0
-        )
-    return mine
+            mine, received[step - 1], (place + step) % count * part, 0
+        )
+    return mine, after
 
 
 def gather_cores(mine, core):
@@ -590,16 +597,39 @@
 
 
 def backward_kernel(
-    s_ref, q_ref, k_ref, v_ref, lse_ref, o_ref, datt_ref, own_ref, other_ref, cap_ref,
-    wk_ref, wv_ref, gain_ref, tok_ref, wq_ref, lat_ref, after_ref, gain_lat_ref, ready_ref,
+    s_ref, q_ref, k_ref, v_ref, lse_ref, o_ref, up_ref, attn_ref, cot_ref, own_ref, other_ref, cap_ref,
+    wk_ref, wv_ref, gain_ref, tok_ref, wq_ref, wo_ref, lat_ref, gain_lat_ref, gain_mlp_ref,
     own_out, other_out, cap_out, lat_out, late_ref,
     dq_ref, dk_ref, dv_ref, s_scr, dp_scr, p_scr, ds_scr, up_scr, sums_ref, gain_out,
+    datt_ref, after_ref,
 ):
     item = pl.program_id(0)
     keys = k_ref.shape[0]
     cap = cap_ref.shape[0]
     cap_rows = pl.ds(keys - cap, cap)
     pieces = [pl.ds(start, 64) for start in range(0, keys, 64)]
+
+    @pl.when(item == 0)
+    def _():
+        gain_out[...] = jnp.zeros_like(gain_out)
+        sums_ref[...] = jnp.zeros_like(sums_ref)
+
+    def norm_back(x, up, gain, row):
+        center = x - jnp.mean(x, axis=-1, keepdims=True)
+        rate = lax.rsqrt(jnp.mean(center * center, axis=-1, keepdims=True) + 1e-05)
+        hat = center * rate
+        gain_out[pl.ds(8 * row, 8), :] += jnp.sum((up * hat).reshape(-1, 8, D), axis=0)
+        scaled = up * gain
+        first = jnp.mean(scaled, axis=-1, keepdims=True)
+        second = jnp.mean(scaled * hat, axis=-1, keepdims=True)
+        return rate * (scaled - first - hat * second)
+
+    keep = (1 - s_ref[4 + item]).astype(F32)
+    after_ref[...] = cot_ref[...].astype(F32) + norm_back(
+        attn_ref[...], up_ref[...].astype(F32), gain_mlp_ref[...], 2
+    )
+    d_branch = after_ref[...].astype(BF16)
+    datt_ref[...] = (dot_nt(d_branch, square(wo_ref)) * keep).astype(BF16)
 
     def pair(p, carry):
         cols = pl.ds(pl.multiple_of(p * PAIR, PAIR), PAIR)
@@ -632,18 +662,12 @@
     lax.fori_loop(0, D // PAIR, pair, 0)
     gain = gain_ref[...]
 
-    @pl.when(item == 0)
-    def _():
-        gain_out[...] = jnp.zeros_like(gain_out)
-        sums_ref[...] = jnp.zeros_like(sums_ref)
-
     wide = sums_ref.shape[0] // 4
     window = pl.ds(pl.multiple_of(s_ref[2], PAIR), wide)
     video_rows = pl.ds(0, keys - cap)
     cap_norm = layer_norm(cap_ref[:, pl.ds(0, D)].astype(F32), gain).astype(BF16)
     latn = layer_norm(lat_ref[...].astype(F32), gain_lat_ref[...]).astype(BF16)
     sums_ref[pl.ds(0, wide), :] += dot_tn(dq_ref[:, window], latn)
-    keep = (1 - s_ref[4 + item]).astype(F32)
     mixed = (o_ref[:, window] * keep).astype(BF16)
     sums_ref[pl.ds(3 * wide, wide), :] += dot_tn(mixed, after_ref[...].astype(BF16))
 
@@ -653,16 +677,6 @@
     sums_ref[pl.ds(wide, 2 * wide), :] += dot_tn(both(video_rows), tok_ref[...]) + dot_tn(
         both(cap_rows), cap_norm
     )
-
-    def norm_back(x, up, gain, row):
-        center = x - jnp.mean(x, axis=-1, keepdims=True)
-        rate = lax.rsqrt(jnp.mean(center * center, axis=-1, keepdims=True) + 1e-05)
-        hat = center * rate
-        gain_out[pl.ds(8 * row, 8), :] += jnp.sum((up * hat).reshape(-1, 8, D), axis=0)
-        scaled = up * gain
-        first = jnp.mean(scaled, axis=-1, keepdims=True)
-        second = jnp.mean(scaled * hat, axis=-1, keepdims=True)
-        return rate * (scaled - first - hat * second)
 
     half = lat_out.shape[0]
     lat_grad = after_ref[...] + norm_back(
@@ -696,13 +710,13 @@
         for n in range(4):
             mine = pl.ds(pl.multiple_of(s_ref[3] + n * wide, PAIR // 2), width)
             late_ref[pl.ds(n * width, width), :] = sums_ref[mine, :].astype(BF16)
-        ready = ready_ref.shape[0]
-        late_ref[pl.ds(4 * width, ready), :] = ready_ref[...]
-        gains = [jnp.sum(gain_out[pl.ds(8 * row, 8), :], axis=0, keepdims=True) for row in (0, 1)]
-        gains = jnp.concatenate(gains + [jnp.zeros((14, D), F32)], axis=0)
-        late_ref[pl.ds(4 * width + ready, 16), :] = gains.astype(BF16)
-        spare = late_ref.shape[0] - 4 * width - ready - 16
-        late_ref[pl.ds(4 * width + ready + 16, spare), :] = jnp.zeros((spare, D), BF16)
+        gains = [jnp.sum(gain_out[pl.ds(8 * row, 8), :], axis=0, keepdims=True) for row in range(3)]
+        kept = 4 - s_ref[4] - s_ref[5] - s_ref[6] - s_ref[7]
+        gains.append(jnp.full((1, D), kept.astype(F32)))
+        gains = jnp.concatenate(gains + [jnp.zeros((12, D), F32)], axis=0)
+        late_ref[pl.ds(4 * width, 16), :] = gains.astype(BF16)
+        spare = late_ref.shape[0] - 4 * width - 16
+        late_ref[pl.ds(4 * width + 16, spare), :] = jnp.zeros((spare, D), BF16)
 
 
 def place_kernel(s_ref, video_in, lat_in, video_part, lat_part, video_ref, lat_ref):
@@ -932,27 +946,16 @@
     d_mlp_norm = gather_head(d_mlp_total, z, head_count)
     activ, _ = lax.optimization_barrier((activ, d_mlp_total))
     growth = head_chunks(dot("blf,fd->bld", activ, down_weight), z, head_count)
+    d_mlp_norm = d_mlp_norm.reshape(after_attn.shape)
     growth, d_mlp_norm, weights, early = lax.optimization_barrier(
         (growth, d_mlp_norm, weights, early.astype(BF16))
     )
     early = lax.psum(early, "txt")
     growth_received = head_exchange(growth, head_count)
 
-    d_after_norm, gain_mlp_part = norm_back_rows(after_attn, gain_mlp, d_mlp_norm.astype(F32))
-    d_after = cot.astype(F32) + d_after_norm
-    d_branch = d_after.astype(BF16)
-    d_att = (dot("bld,ed->ble", d_branch, w_out) * keep[:, None, None]).astype(BF16)
-    ready = jnp.concatenate(
-        [
-            jnp.sum(gain_mlp_part, axis=0)[None],
-            jnp.full((1, D), jnp.sum(keep)),
-            jnp.zeros((14, D), F32),
-        ]
-    ).astype(BF16)
-    late_size = 4 * head_width + 32
+    late_size = 4 * head_width + 16
     late_size = late_size + -late_size % (32 * txt_count)
     pair_shape = (keys_here, 2 * lat_rows)
-    d_att, ready = lax.optimization_barrier((d_att, ready))
     video_grad, other_back, cap_back, latent_grad, late = call(
         backward_kernel,
         "attention_backward",
@@ -963,6 +966,8 @@
             pl.BlockSpec((None, 2, 8, 2 * lat_rows), lambda i, s: (i, 0, 0, 0)),
             item_spec(lat_rows),
             item_spec(lat_rows),
+            item_spec(lat_rows),
+            item_spec(lat_rows),
             own_spec(video_here),
             item_spec(video_here),
             item_spec(cap_rows, D + PAIR),
@@ -971,10 +976,10 @@
             row_spec,
             item_spec(2 * video_here),
             weight_spec(2),
-            item_spec(lat_rows),
+            weight_spec(3),
             item_spec(lat_rows),
             row_spec,
-            whole_spec(*ready.shape),
+            row_spec,
         ],
         [
             (own_spec(video_here), video_tokens.shape, F32),
@@ -984,8 +989,9 @@
             (whole_spec(late_size, D), (late_size, D), BF16),
         ],
         (
-            queries, keys, values, lse, attended, d_att, video_tokens, video_other, cap,
-            weights, weights, gain_tok_row, tok_norm, weights, lat, d_after, gain_lat_row, ready,
+            queries, keys, values, lse, attended, d_mlp_norm, after_attn, cot, video_tokens,
+            video_other, cap, weights, weights, gain_tok_row, tok_norm, weights, weights, lat,
+            gain_lat_row, gain_mlp_row,
         ),
         BACK_COST,
         [
@@ -998,7 +1004,9 @@
             pltpu.VMEM(pair_shape, BF16),
             pltpu.VMEM((256, D), F32),
             pltpu.VMEM((8 * PAIR, D), F32),
-            pltpu.VMEM((16, D), F32),
+            pltpu.VMEM((24, D), F32),
+            pltpu.VMEM((lat_rows, D), BF16),
+            pltpu.VMEM((lat_rows, D), F32),
         ],
     )
     def place(video_grad, latent_grad, part):
@@ -1041,18 +1049,20 @@
     late_total, growth, early_other, other_here, cap_back = lax.optimization_barrier(
         (late_total, growth, early_other, other_here, cap_back)
     )
-    growth = gather_head(growth, z, head_count)
+    late, growth = gather_places(late_total, place_index, txt_count, growth)
+    growth_parts = [head_shift(growth, shift, head_count) for shift in range(1, head_count)]
+    growth_parts[0], cap_back = lax.optimization_barrier((growth_parts[0], cap_back))
     cap_parts = []
     for step in range(txt_count):
         perm = [(b, a) for a, b in caption_perm(step, 2, txt_count, 2)]
         cap_parts.append(
             lax.ppermute(cap_back[:, step * cap_here : (step + 1) * cap_here], ("vid", "txt"), perm)
         )
-    late = gather_places(late_total, place_index, txt_count)
     video_grad, latent_grad = place(video_grad, latent_grad, other_here)
-    late, video_grad, latent_grad, cap_parts, growth = lax.optimization_barrier(
-        (late, video_grad, latent_grad, cap_parts, growth)
-    )
+    late, video_grad, latent_grad, cap_parts, growth_parts = lax.optimization_barrier(
+        (late, video_grad, latent_grad, cap_parts, growth_parts)
+    )
+    growth = place_head(growth, growth_parts, z, head_count)
     late = gather_cores(late, core).astype(F32)
     caption_grad = jnp.zeros((txt_count, own, cap_here, D), F32)
     for step, part in enumerate(cap_parts):
@@ -1070,7 +1080,7 @@
         return lax.dynamic_update_slice_in_dim(whole, other, (1 - core) * own, 0)
 
     latents_out = give_back(out_mine)
-    kept_count = gains[1, 0].astype(jnp.int32)
+    kept_count = gains[3, 0].astype(jnp.int32)
     return (
         latents_out,
         latent_grad,
@@ -1082,22 +1092,11 @@
         late[3 * head_width : 4 * head_width],
         jnp.where(core == 0, early, early_other).astype(F32),
         jnp.where(core == 0, early_other, early).astype(F32),
-        gains[17],
-        gains[16],
+        gains[1],
         gains[0],
+        gains[2],
         kept_count,
     )
-
-
-def norm_back_rows(values, gain, upstream):
-    mean = jnp.mean(values, axis=-1, keepdims=True)
-    center = values - mean
-    rate = lax.rsqrt(jnp.mean(center * center, axis=-1, keepdims=True) + 1e-05)
-    hat = center * rate
-    scaled = upstream * gain
-    first = jnp.mean(scaled, axis=-1, keepdims=True)
-    second = jnp.mean(scaled * hat, axis=-1, keepdims=True)
-    return rate * (scaled - first - hat * second), jnp.sum(upstream * hat, axis=-2)
 
 
 def fits(mesh):

time: 316 us -> 318 us (level)
  waiting for transfers between devices: 41.7 us -> 49.6 us
  other arithmetic: 26.7 us -> 20.3 us
  local copies, waits for them, and re-layouts: 33.5 us -> 27.8 us
  Pallas kernels: 128 us -> 132 us
    ppermute x12, waiting for transfers between devices: 25.2 us -> 33.7 us  [head_shift(): lax.ppermute(values, 'head', [(i, (i - shift) % count) for i in range(cou...]
    pallas_call x4, Pallas kernels: 122 us -> 125 us  [call(): pl.pallas_call(kernel, name=name, grid_spec=pltpu.PrefetchScalarGridSpec(...]
    dot_general x8 -> x7, matrix products: 12.5 us -> 10.7 us  [dot(): return jnp.einsum(spec, a, b, preferred_element_type=F32)]
    unnamed x91 -> x81, local copies, waits for them, and re-layouts: 9.38 us -> 9.35 us
  transfers between devices with their start and end apart: 40 -> 40, of which waited for: 9 -> 11; matrix products, arithmetic and copies ran while one was open for 12% -> 8% of each run, Pallas kernels for 32% -> 33%
where the time goes in v5:
time: 318 us; the launch traced here: 313 us
  Pallas kernels  132 us (42%)
  starting transfers between devices  56.2 us (18%)
  waiting for transfers between devices  49.6 us (16%)
  local copies, waits for them, and re-layouts  27.8 us (9%)
  other arithmetic  20.3 us (6%)
  between operations  17 us (5%)
  matrix products  10.7 us (3%)
    pallas_call x4, Pallas kernels, call(): pl.pallas_call(kernel, name=name, grid_spec=pltpu.PrefetchScalarGridSpec(...  125 us
    ppermute x12, waiting for transfers between devices, head_shift(): lax.ppermute(values, 'head', [(i, (i - shift) % count) for i in range(cou...  33.7 us
    ppermute x12, starting transfers between devices, head_shift(): lax.ppermute(values, 'head', [(i, (i - shift) % count) for i in range(cou...  14.2 us
    dot_general x7, matrix products, dot(): return jnp.einsum(spec, a, b, preferred_element_type=F32)  10.7 us
    ppermute x4, starting transfers between devices, local(): lax.ppermute(block, ('vid', 'txt'), caption_perm(step, 2, txt_count, 2))  10.1 us
    unnamed x81, local copies, waits for them, and re-layouts  9.35 us
    ppermute x4, starting transfers between devices, local(): lax.ppermute(cap_back[:, step * cap_here:(step + 1) * cap_here], ('vid',...  9.31 us
    ppermute x3, waiting for transfers between devices, reduce_over_group(): total = total + lax.ppermute(chunk, 'txt', perm).astype(F32)  8.81 us
  transfers between devices with their start and end apart: 40, of which 11 were waited for; matrix products, arithmetic and copies ran while one was open for 8% of the time, Pallas kernels for 33%

profile of v5, /device:TPU:0, one launch (start us, length us, event | category | flops | bytes accessed | tf_op | source)
XLA Modules:
  0.0 313.2 jit_solution(988448235629412751)
XLA Ops:
  7.3 2.2 constant_dynamic-slice_fusion.7
  14.6 5.3 %collective-permute-start.1 = (bf16[2,192,768]{2,1,0:T(8,128)(2,1)}, bf16[2,192,768]{2,1,0:T(8,128)(2,1)}, u32[]{:S(2)}, u32[]{:S(2)}) collective-permute-start(bf16[2,192,768]{2,1,0:T(8,128)(2,1)} %constant_dynamic-slice_fusion.4), channel_id=1, source_target_pairs={{0,1},{1,2},{2,3},{4,5},{5,6},{6,7},{8,9},{9,10},{10,11},{12,13},{... | collective-permute-start | bytes 1769480 | tf_op jit(solution)/shard_map/ppermute | solution.py:768
  24.4 3.9 %collective-permute-start.4 = (bf16[4,16,896]{2,1,0:T(8,128)(2,1)}, bf16[4,16,896]{2,1,0:T(8,128)(2,1)S(1)}, u32[]{:S(2)}, u32[]{:S(2)}) collective-permute-start(bf16[4,16,896]{2,1,0:T(8,128)(2,1)} %get-tuple-element.215), channel_id=1, source_target_pairs={{0,16},{4,4},{8,20},{12,0},{16,24},{20,12},{24,28},{28,8},{1,17},{... | collective-permute-start | bytes 344072 | tf_op jit(solution)/shard_map/ppermute | solution.py:803
  35.2 4.6 %collective-permute-start.6 = (bf16[4,16,896]{2,1,0:T(8,128)(2,1)S(1)}, bf16[4,16,896]{2,1,0:T(8,128)(2,1)S(1)}, u32[]{:S(2)}, u32[]{:S(2)}) collective-permute-start(bf16[4,16,896]{2,1,0:T(8,128)(2,1)S(1)} %copy-done.33), channel_id=1, source_target_pairs={{0,20},{4,0},{8,16},{12,4},{16,28},{20,8},{24,24},{28,12},{1,21},{... | collective-permute-start | bytes 344072 | tf_op jit(solution)/shard_map/ppermute | solution.py:803
  39.9 10.7 %token_norm.1.tok_ref = bf16[4,1024,768]{2,1,0:T(8,128)(2,1)} custom-call(s32[8]{0:T(128)} %concatenate.28.s_ref, bf16[8,512,768]{2,1,0:T(8,128)(2,1)} %own_ref.3, bf16[4,640,768]{2,1,0:T(8,128)(2,1)} %collective-permute-done.other_ref, f32[1,768]{1,0:T(1,128)} %broadcast_in_dim.111.gain_ref), custom_call_target="tpu_custom_call" | custom-call | flops 9900000256 | bytes 9000000 | tf_op jit(solution)/shard_map/token_norm/pallas_call | solution.py:834
  52.0 2.1 fusion.28
  57.8 7.3 %collective-permute-start.9 = (bf16[2,192,768]{2,1,0:T(8,128)(2,1)S(1)}, bf16[2,192,768]{2,1,0:T(8,128)(2,1)S(1)}, u32[]{:S(2)}, u32[]{:S(2)}) collective-permute-start(bf16[2,192,768]{2,1,0:T(8,128)(2,1)S(1)} %get-tuple-element.211), channel_id=1, source_target_pairs={{1,0},{2,1},{0,3},{5,4},{6,5},{4,7},{9,8},{10,9},{8,11},{13,12},{1... | collective-permute-start | bytes 1769480 | tf_op jit(solution)/shard_map/ppermute | solution.py:876
  66.6 27.4 %attention_forward.2 = (bf16[4,128,768]{2,1,0:T(8,128)(2,1)}, bf16[4,1088,768]{2,1,0:T(8,128)(2,1)}, bf16[4,1088,768]{2,1,0:T(8,128)(2,1)}, f32[4,2,8,256]{3,2,1,0:T(8,128)}, f32[4,128,768]{2,1,0:T(8,128)}) custom-call(s32[8]{0:T(128)} %concatenate.28.s_ref, bf16[4,1024,768]{2,1,0:T(8,128)(2,1)} %token_norm.1.tok_ref, bf16[4,64,896]{2,1,0:T(8,128)(2,1)} %copy-done.30, ...), custom_call_target="tpu_custom_call" | custom-call | flops 25300000768 | bytes 23000000 | tf_op jit(solution)/shard_map/attention_forward/pallas_call | solution.py:834
  102.1 27.5 %attention_forward.3 = (bf16[4,128,768]{2,1,0:T(8,128)(2,1)}, bf16[4,1088,768]{2,1,0:T(8,128)(2,1)}, bf16[4,1088,768]{2,1,0:T(8,128)(2,1)}, f32[4,2,8,256]{3,2,1,0:T(8,128)}, f32[4,128,768]{2,1,0:T(8,128)}) custom-call(s32[8]{0:T(128)} %concatenate.27.s_ref, ...), custom_call_target="tpu_custom_call", output_to_operand_aliasing={{0}: (8, {}), {1}: (9, {}), {2}: (10, {}), {3}: (11, {}), {... | custom-call | flops 25300000768 | bytes 23000000 | tf_op jit(solution)/shard_map/attention_forward/pallas_call | solution.py:834
  129.7 2.3 fusion.32
  132.7 3.9 %multiply_convert_fusion = (bf16[4,128,768]{2,1,0:T(8,128)(2,1)S(1)}, f32[4,128,768]{2,1,0:T(8,128)S(1)}, f32[4,128,768]{2,1,0:T(8,128)S(1)}) fusion(bf16[768,768]{1,0:T(8,128)(2,1)S(1)} %copy-done, f32[4,128,768]{2,1,0:T(8,128)S(1)} %get-tuple-element.222.attn_ref, f32[768]{0:T(1024)S(1)} %copy-done.38, f32[4,128]{1,0:T(4,128)S(1)} %add_rsqrt_fusion, ...), kind=kOutput, calls=%fused_computation.11 | convolution fusion | flops 631111680 | bytes 6691840 | tf_op jit(solution)/shard_map/bld,df->blf/dot_general | solution.py:764
  146.3 11.8 %collective-permute-done.12 = bf16[128,768]{1,0:T(8,128)(2,1)S(1)} collective-permute-done((bf16[128,768]{1,0:T(8,128)(2,1)S(1)}, bf16[128,768]{1,0:T(8,128)(2,1)S(1)}, u32[]{:S(2)}, u32[]{:S(2)}) %collective-permute-start.12) | collective-permute-done | bytes 196640 | tf_op jit(solution)/shard_map/ppermute | solution.py:397
  165.4 12.1 %collective-permute-done.15 = bf16[128,768]{1,0:T(8,128)(2,1)S(1)} collective-permute-done((bf16[128,768]{1,0:T(8,128)(2,1)S(1)}, bf16[128,768]{1,0:T(8,128)(2,1)S(1)}, u32[]{:S(2)}, u32[]{:S(2)}) %collective-permute-start.15) | collective-permute-done | bytes 196640 | tf_op jit(solution)/shard_map/ppermute | solution.py:397
  183.7 59.9 %attention_backward.1 = (f32[8,512,768]{2,1,0:T(8,128)}, bf16[4,576,768]{2,1,0:T(8,128)(2,1)}, bf16[4,64,768]{2,1,0:T(8,128)(2,1)}, f32[8,64,768]{2,1,0:T(8,128)}, bf16[896,768]{1,0:T(8,128)(2,1)}) custom-call(s32[8]{0:T(128)} %concatenate.28.s_ref, bf16[4,128,768]{2,1,0:T(8,128)(2,1)} %get-tuple-element.133.q_ref, ...), custom_call_target="tpu_custom_call" | custom-call | flops 3300000000 | bytes 3000000 | tf_op jit(solution)/shard_map/attention_backward/pallas_call | solution.py:834
  244.9 2.3 collective-permute-done.21
  251.6 4.8 %collective-permute-done.22 = bf16[112,768]{1,0:T(8,128)(2,1)S(1)} collective-permute-done((bf16[112,768]{1,0:T(8,128)(2,1)S(1)}, bf16[112,768]{1,0:T(8,128)(2,1)S(1)}, u32[]{:S(2)}, u32[]{:S(2)}) %collective-permute-start.22) | collective-permute-done | bytes 172064 | tf_op jit(solution)/shard_map/ppermute | solution.py:454
  256.3 4.0 %collective-permute-done.23 = bf16[112,768]{1,0:T(8,128)(2,1)S(1)} collective-permute-done((bf16[112,768]{1,0:T(8,128)(2,1)S(1)}, bf16[112,768]{1,0:T(8,128)(2,1)S(1)}, u32[]{:S(2)}, u32[]{:S(2)}) %collective-permute-start.23) | collective-permute-done | bytes 172064 | tf_op jit(solution)/shard_map/ppermute | solution.py:454
  263.5 6.1 %place_rows.1 = (f32[8,512,768]{2,1,0:T(8,128)}, f32[8,64,768]{2,1,0:T(8,128)}) custom-call(s32[8]{0:T(128)} %concatenate.28.s_ref, f32[8,512,768]{2,1,0:T(8,128)} %get-tuple-element.157.video_in, f32[8,64,768]{2,1,0:T(8,128)} %get-tuple-element.158.lat_in, ...), custom_call_target="tpu_custom_call", output_to_operand_aliasing={{0}: (1, {}), {1}: (2, {})} | custom-call | flops 6000000000 | bytes 10000000 | tf_op jit(solution)/shard_map/place_rows/pallas_call | solution.py:1014
  269.6 3.8 %select_convert_fusion = (f32[768,768]{1,0:T(8,128)}, f32[768,768]{1,0:T(8,128)}) fusion(bf16[768,768]{1,0:T(8,128)(2,1)} %collective-permute-done.25, bf16[768,768]{1,0:T(8,128)(2,1)S(1)} %copy-done.26, pred[]{:T(512)S(6)} %eq.65), kind=kLoop, calls=%fused_computation.42 | loop fusion | flops 2359296 | bytes 7077889 | tf_op jit(solution)/shard_map/convert_element_type | solution.py:1094
  277.6 3.1 collective-permute-done.30
  281.4 5.2 %collective-permute-start.32 = (bf16[4,16,768]{2,1,0:T(8,128)(2,1)S(1)}, bf16[4,16,768]{2,1,0:T(8,128)(2,1)S(1)}, u32[]{:S(2)}, u32[]{:S(2)}) collective-permute-start(bf16[4,16,768]{2,1,0:T(8,128)(2,1)S(1)} %get-tuple-element.219), channel_id=1, source_target_pairs={{16,0},{4,4},{20,8},{0,12},{24,16},{12,20},{28,24},{8,28},{17,1},{... | collective-permute-start | bytes 294920 | tf_op jit(solution)/shard_map/ppermute | solution.py:1059
  286.7 5.0 %collective-permute-done.35 = bf16[128,768]{1,0:T(8,128)(2,1)S(1)} collective-permute-done((bf16[128,768]{1,0:T(8,128)(2,1)S(1)}, bf16[128,768]{1,0:T(8,128)(2,1)S(1)}, u32[]{:S(2)}, u32[]{:S(2)}) %collective-permute-start.35) | collective-permute-done | bytes 196640 | tf_op jit(solution)/shard_map/ppermute | solution.py:397
  291.8 3.4 %collective-permute-start.34 = (bf16[4,16,768]{2,1,0:T(8,128)(2,1)S(1)}, bf16[4,16,768]{2,1,0:T(8,128)(2,1)S(1)}, u32[]{:S(2)}, u32[]{:S(2)}) collective-permute-start(bf16[4,16,768]{2,1,0:T(8,128)(2,1)S(1)} %get-tuple-element.217), channel_id=1, source_target_pairs={{20,0},{0,4},{16,8},{4,12},{28,16},{8,20},{24,24},{12,28},{21,1},{... | collective-permute-start | bytes 294920 | tf_op jit(solution)/shard_map/ppermute | solution.py:1059
  295.2 2.5 collective-permute-done.34
  (234 shorter events, 75.0 us)
Async XLA Ops:
  7.2 236.4 %all-reduce.2.cloned.1.call-start = ((), (), s32[]{:S(2)}) async-start(), calls=%async_computation | async-start | bytes 2359296 | tf_op jit(solution)/shard_map/psum | solution.py:953
  11.8 23.4 %collective-permute-start = (bf16[4,640,768]{2,1,0:T(8,128)(2,1)}, bf16[4,640,768]{2,1,0:T(8,128)(2,1)}, u32[]{:S(2)}, u32[]{:S(2)}) collective-permute-start(bf16[4,640,768]{2,1,0:T(8,128)(2,1)} %pad_maximum_fusion), channel_id=1, source_target_pairs={{0,16},{16,0},{1,17},{17,1},{2,18},{18,2},{3,19},{19,3},{4,20},{20... | collective-permute-start | bytes 11796488 | tf_op jit(solution)/shard_map/ppermute | solution.py:393
  14.6 36.0 %collective-permute-start.1 = (bf16[2,192,768]{2,1,0:T(8,128)(2,1)}, bf16[2,192,768]{2,1,0:T(8,128)(2,1)}, u32[]{:S(2)}, u32[]{:S(2)}) collective-permute-start(bf16[2,192,768]{2,1,0:T(8,128)(2,1)} %constant_dynamic-slice_fusion.4), channel_id=1, source_target_pairs={{0,1},{1,2},{2,3},{4,5},{5,6},{6,7},{8,9},{9,10},{10,11},{12,13},{... | collective-permute-start | bytes 1769480 | tf_op jit(solution)/shard_map/ppermute | solution.py:768
  19.9 30.7 %collective-permute-start.2 = (bf16[2,192,768]{2,1,0:T(8,128)(2,1)}, bf16[2,192,768]{2,1,0:T(8,128)(2,1)}, u32[]{:S(2)}, u32[]{:S(2)}) collective-permute-start(bf16[2,192,768]{2,1,0:T(8,128)(2,1)} %constant_dynamic-slice_fusion.4), channel_id=1, source_target_pairs={{1,0},{2,1},{3,2},{5,4},{6,5},{7,6},{9,8},{10,9},{11,10},{13,12},{... | collective-permute-start | bytes 1769480 | tf_op jit(solution)/shard_map/ppermute | solution.py:769
  24.4 26.2 %collective-permute-start.4 = (bf16[4,16,896]{2,1,0:T(8,128)(2,1)}, bf16[4,16,896]{2,1,0:T(8,128)(2,1)S(1)}, u32[]{:S(2)}, u32[]{:S(2)}) collective-permute-start(bf16[4,16,896]{2,1,0:T(8,128)(2,1)} %get-tuple-element.215), channel_id=1, source_target_pairs={{0,16},{4,4},{8,20},{12,0},{16,24},{20,12},{24,28},{28,8},{1,17},{... | collective-permute-start | bytes 344072 | tf_op jit(solution)/shard_map/ppermute | solution.py:803
  35.2 15.4 %collective-permute-start.5 = (bf16[4,16,896]{2,1,0:T(8,128)(2,1)S(1)}, bf16[4,16,896]{2,1,0:T(8,128)(2,1)S(1)}, u32[]{:S(2)}, u32[]{:S(2)}) collective-permute-start(bf16[4,16,896]{2,1,0:T(8,128)(2,1)S(1)} %copy-done.34), channel_id=1, source_target_pairs={{0,4},{4,20},{8,0},{12,16},{16,12},{20,28},{24,8},{28,24},{1,5},{5... | collective-permute-start | bytes 344072 | tf_op jit(solution)/shard_map/ppermute | solution.py:803
  35.2 15.4 %collective-permute-start.6 = (bf16[4,16,896]{2,1,0:T(8,128)(2,1)S(1)}, bf16[4,16,896]{2,1,0:T(8,128)(2,1)S(1)}, u32[]{:S(2)}, u32[]{:S(2)}) collective-permute-start(bf16[4,16,896]{2,1,0:T(8,128)(2,1)S(1)} %copy-done.33), channel_id=1, source_target_pairs={{0,20},{4,0},{8,16},{12,4},{16,28},{20,8},{24,24},{28,12},{1,21},{... | collective-permute-start | bytes 344072 | tf_op jit(solution)/shard_map/ppermute | solution.py:803
  56.5 37.5 %collective-permute-start.8 = (bf16[2,192,768]{2,1,0:T(8,128)(2,1)S(1)}, bf16[2,192,768]{2,1,0:T(8,128)(2,1)S(1)}, u32[]{:S(2)}, u32[]{:S(2)}) collective-permute-start(bf16[2,192,768]{2,1,0:T(8,128)(2,1)S(1)} %get-tuple-element.212), channel_id=1, source_target_pairs={{1,2},{2,3},{3,0},{5,6},{6,7},{7,4},{9,10},{10,11},{11,8},{13,14},... | collective-permute-start | bytes 1769480 | tf_op jit(solution)/shard_map/ppermute | solution.py:875
  57.8 36.3 %collective-permute-start.9 = (bf16[2,192,768]{2,1,0:T(8,128)(2,1)S(1)}, bf16[2,192,768]{2,1,0:T(8,128)(2,1)S(1)}, u32[]{:S(2)}, u32[]{:S(2)}) collective-permute-start(bf16[2,192,768]{2,1,0:T(8,128)(2,1)S(1)} %get-tuple-element.211), channel_id=1, source_target_pairs={{1,0},{2,1},{0,3},{5,4},{6,5},{4,7},{9,8},{10,9},{8,11},{13,12},{1... | collective-permute-start | bytes 1769480 | tf_op jit(solution)/shard_map/ppermute | solution.py:876
  138.7 19.4 %collective-permute-start.12 = (bf16[128,768]{1,0:T(8,128)(2,1)S(1)}, bf16[128,768]{1,0:T(8,128)(2,1)S(1)}, u32[]{:S(2)}, u32[]{:S(2)}) collective-permute-start(bf16[128,768]{1,0:T(8,128)(2,1)S(1)} %get-tuple-element.203), channel_id=1, source_target_pairs={{0,2},{1,3},{2,0},{3,1},{4,6},{5,7},{6,4},{7,5},{8,10},{9,11},{10,... | collective-permute-start | bytes 589832 | tf_op jit(solution)/shard_map/ppermute | solution.py:397
  140.4 17.8 %collective-permute-start.13 = (bf16[128,768]{1,0:T(8,128)(2,1)S(1)}, bf16[128,768]{1,0:T(8,128)(2,1)S(1)}, u32[]{:S(2)}, u32[]{:S(2)}) collective-permute-start(bf16[128,768]{1,0:T(8,128)(2,1)S(1)} %get-tuple-element.204), channel_id=1, source_target_pairs={{0,1},{1,2},{2,3},{3,0},{4,5},{5,6},{6,7},{7,4},{8,9},{9,10},{10,1... | collective-permute-start | bytes 589832 | tf_op jit(solution)/shard_map/ppermute | solution.py:397
  158.3 19.2 %collective-permute-start.15 = (bf16[128,768]{1,0:T(8,128)(2,1)S(1)}, bf16[128,768]{1,0:T(8,128)(2,1)S(1)}, u32[]{:S(2)}, u32[]{:S(2)}) collective-permute-start(bf16[128,768]{1,0:T(8,128)(2,1)S(1)} %get-tuple-element.182), channel_id=1, source_target_pairs={{0,2},{1,3},{2,0},{3,1},{4,6},{5,7},{6,4},{7,5},{8,10},{9,11},{10,... | collective-permute-start | bytes 589832 | tf_op jit(solution)/shard_map/ppermute | solution.py:397
  159.9 17.7 %collective-permute-start.16 = (bf16[128,768]{1,0:T(8,128)(2,1)S(1)}, bf16[128,768]{1,0:T(8,128)(2,1)S(1)}, u32[]{:S(2)}, u32[]{:S(2)}) collective-permute-start(bf16[128,768]{1,0:T(8,128)(2,1)S(1)} %get-tuple-element.182), channel_id=1, source_target_pairs={{0,1},{1,2},{2,3},{3,0},{4,5},{5,6},{6,7},{7,4},{8,9},{9,10},{10,1... | collective-permute-start | bytes 589832 | tf_op jit(solution)/shard_map/ppermute | solution.py:397
  163.6 14.0 %collective-permute-start.17 = (bf16[768,768]{1,0:T(8,128)(2,1)S(1)}, bf16[768,768]{1,0:T(8,128)(2,1)S(1)}, u32[]{:S(2)}, u32[]{:S(2)}) collective-permute-start(bf16[768,768]{1,0:T(8,128)(2,1)S(1)} %get-tuple-element.226), channel_id=1, source_target_pairs={{0,16},{16,0},{1,17},{17,1},{2,18},{18,2},{3,19},{19,3},{4,20},{20... | collective-permute-start | bytes 3538952 | tf_op jit(solution)/shard_map/ppermute | solution.py:393
  180.7 62.9 %collective-permute-start.18 = (bf16[128,768]{1,0:T(8,128)(2,1)}, bf16[128,768]{1,0:T(8,128)(2,1)S(1)}, u32[]{:S(2)}, u32[]{:S(2)}) collective-permute-start(bf16[128,768]{1,0:T(8,128)(2,1)} %get-tuple-element.130), channel_id=1, source_target_pairs={{0,3},{1,0},{2,1},{3,2},{4,7},{5,4},{6,5},{7,6},{8,11},{9,8},{10,9... | collective-permute-start | bytes 589832 | tf_op jit(solution)/shard_map/ppermute | solution.py:397
  180.7 62.9 %collective-permute-start.19 = (bf16[128,768]{1,0:T(8,128)(2,1)}, bf16[128,768]{1,0:T(8,128)(2,1)S(1)}, u32[]{:S(2)}, u32[]{:S(2)}) collective-permute-start(bf16[128,768]{1,0:T(8,128)(2,1)} %get-tuple-element.131), channel_id=1, source_target_pairs={{0,2},{1,3},{2,0},{3,1},{4,6},{5,7},{6,4},{7,5},{8,10},{9,11},{10,... | collective-permute-start | bytes 589832 | tf_op jit(solution)/shard_map/ppermute | solution.py:397
  181.6 61.9 %collective-permute-start.20 = (bf16[128,768]{1,0:T(8,128)(2,1)}, bf16[128,768]{1,0:T(8,128)(2,1)S(1)}, u32[]{:S(2)}, u32[]{:S(2)}) collective-permute-start(bf16[128,768]{1,0:T(8,128)(2,1)} %get-tuple-element.132), channel_id=1, source_target_pairs={{0,1},{1,2},{2,3},{3,0},{4,5},{5,6},{6,7},{7,4},{8,9},{9,10},{10,1... | collective-permute-start | bytes 589832 | tf_op jit(solution)/shard_map/ppermute | solution.py:397
  247.2 13.3 %collective-permute-start.26 = (bf16[4,576,768]{2,1,0:T(8,128)(2,1)}, bf16[4,576,768]{2,1,0:T(8,128)(2,1)}, u32[]{:S(2)}, u32[]{:S(2)}) collective-permute-start(bf16[4,576,768]{2,1,0:T(8,128)(2,1)} %get-tuple-element.151), channel_id=1, source_target_pairs={{0,16},{16,0},{1,17},{17,1},{2,18},{18,2},{3,19},{19,3},{4,20},{20... | collective-permute-start | bytes 10616840 | tf_op jit(solution)/shard_map/ppermute | solution.py:393
  261.2 16.3 %collective-permute-start.28 = (bf16[112,768]{1,0:T(8,128)(2,1)S(1)}, bf16[112,768]{1,0:T(8,128)(2,1)S(1)}, u32[]{:S(2)}, u32[]{:S(2)}) collective-permute-start(bf16[112,768]{1,0:T(8,128)(2,1)S(1)} %add_convert_fusion.4), channel_id=1, source_target_pairs={{0,8},{4,12},{8,0},{12,4},{1,9},{5,13},{9,1},{13,5},{2,10},{6,14},... | collective-permute-start | bytes 516104 | tf_op jit(solution)/shard_map/ppermute | solution.py:460
  262.6 24.1 %collective-permute-start.29 = (bf16[112,768]{1,0:T(8,128)(2,1)S(1)}, bf16[112,768]{1,0:T(8,128)(2,1)S(1)}, u32[]{:S(2)}, u32[]{:S(2)}) collective-permute-start(bf16[112,768]{1,0:T(8,128)(2,1)S(1)} %add_convert_fusion.4), channel_id=1, source_target_pairs={{0,4},{4,8},{8,12},{12,0},{1,5},{5,9},{9,13},{13,1},{2,6},{6,10},{... | collective-permute-start | bytes 516104 | tf_op jit(solution)/shard_map/ppermute | solution.py:460
  275.4 16.4 %collective-permute-start.35 = (bf16[128,768]{1,0:T(8,128)(2,1)S(1)}, bf16[128,768]{1,0:T(8,128)(2,1)S(1)}, u32[]{:S(2)}, u32[]{:S(2)}) collective-permute-start(bf16[128,768]{1,0:T(8,128)(2,1)S(1)} %add_convert_fusion.3), channel_id=1, source_target_pairs={{0,2},{1,3},{2,0},{3,1},{4,6},{5,7},{6,4},{7,5},{8,10},{9,11},{10,... | collective-permute-start | bytes 589832 | tf_op jit(solution)/shard_map/ppermute | solution.py:397
  275.5 19.6 %collective-permute-start.36 = (bf16[128,768]{1,0:T(8,128)(2,1)S(1)}, bf16[128,768]{1,0:T(8,128)(2,1)S(1)}, u32[]{:S(2)}, u32[]{:S(2)}) collective-permute-start(bf16[128,768]{1,0:T(8,128)(2,1)S(1)} %add_convert_fusion.3), channel_id=1, source_target_pairs={{0,1},{1,2},{2,3},{3,0},{4,5},{5,6},{6,7},{7,4},{8,9},{9,10},{10,1... | collective-permute-start | bytes 589832 | tf_op jit(solution)/shard_map/ppermute | solution.py:397
  280.7 14.4 %collective-permute-start.31 = (bf16[4,16,768]{2,1,0:T(8,128)(2,1)S(1)}, bf16[4,16,768]{2,1,0:T(8,128)(2,1)S(1)}, u32[]{:S(2)}, u32[]{:S(2)}) collective-permute-start(bf16[4,16,768]{2,1,0:T(8,128)(2,1)S(1)} %get-tuple-element.220), channel_id=1, source_target_pairs={{0,0},{16,4},{4,8},{20,12},{8,16},{24,20},{12,24},{28,28},{1,1},{1... | collective-permute-start | bytes 294920 | tf_op jit(solution)/shard_map/ppermute | solution.py:1059
  281.4 13.8 %collective-permute-start.32 = (bf16[4,16,768]{2,1,0:T(8,128)(2,1)S(1)}, bf16[4,16,768]{2,1,0:T(8,128)(2,1)S(1)}, u32[]{:S(2)}, u32[]{:S(2)}) collective-permute-start(bf16[4,16,768]{2,1,0:T(8,128)(2,1)S(1)} %get-tuple-element.219), channel_id=1, source_target_pairs={{16,0},{4,4},{20,8},{0,12},{24,16},{12,20},{28,24},{8,28},{17,1},{... | collective-permute-start | bytes 294920 | tf_op jit(solution)/shard_map/ppermute | solution.py:1059
  (55 other events, 514.2 us)
Sparse Core Ops, SparseCore 0:
  179.3 51.9 all-reduce.1

commit v6 on v5

--- a/solution.py
+++ b/solution.py
@@ -420,19 +420,14 @@
     return own.astype(BF16)
 
 
-def place_head(total, parts, place, count):
+def gather_head(total, place, count):
     result = jnp.zeros((count,) + total.shape, BF16)
     result = lax.dynamic_update_index_in_dim(result, total, place, 0)
     for shift in range(1, count):
         result = lax.dynamic_update_index_in_dim(
-            result, parts[shift - 1], (place + shift) % count, 0
+            result, head_shift(total, shift, count), (place + shift) % count, 0
         )
     return result
-
-
-def gather_head(total, place, count):
-    parts = [head_shift(total, shift, count) for shift in range(1, count)]
-    return place_head(total, parts, place, count)
 
 
 def group_steps(count):
@@ -455,17 +450,15 @@
     return total.astype(BF16)
 
 
-def gather_places(total, place, count, after):
+def gather_places(total, place, count):
     part = total.shape[0]
-    received = [lax.ppermute(total, "txt", perm) for _, perm in group_steps(count)]
-    received[0], after = lax.optimization_barrier((received[0], after))
     mine = jnp.zeros((part * count, total.shape[1]), BF16)
     mine = lax.dynamic_update_slice_in_dim(mine, total, place * part, 0)
-    for step in range(1, count):
+    for step, perm in group_steps(count):
         mine = lax.dynamic_update_slice_in_dim(
-            mine, received[step - 1], (place + step) % count * part, 0
-        )
-    return mine, after
+            mine, lax.ppermute(total, "txt", perm), (place + step) % count * part, 0
+        )
+    return mine
 
 
 def gather_cores(mine, core):
@@ -796,12 +789,18 @@
     cap_valid = (place_slots[None, :] < caption_len[:, None]) & (key_mask == 1)
     flags = jnp.broadcast_to(cap_valid.astype(BF16)[:, :, None], cap_valid.shape + (PAIR,))
     cap_message = jnp.concatenate([caption_tokens, flags], axis=2)
-    cap_parts = []
-    for step in range(txt_count):
-        block = take_block(cap_message, (place_index + step) % txt_count, own)
-        cap_parts.append(
-            lax.ppermute(block, ("vid", "txt"), caption_perm(step, 2, txt_count, 2))
-        )
+    def send_captions(message, steps):
+        return [
+            lax.ppermute(
+                take_block(message, (place_index + step) % txt_count, own),
+                ("vid", "txt"),
+                caption_perm(step, 2, txt_count, 2),
+            )
+            for step in steps
+        ]
+
+    cap_parts = send_captions(cap_message, range(2))
+
     def item_spec(rows, width=D, first=0):
         return pl.BlockSpec((None, rows, width), lambda i, s: (first + i, 0, 0))
 
@@ -863,7 +862,8 @@
         (video_tokens, video_other, gain_tok_row),
         9,
     )
-    tok_norm, up1, down1, cap_parts = lax.optimization_barrier((tok_norm, up1, down1, cap_parts))
+    tok_norm, up1, down1, cap_message = lax.optimization_barrier((tok_norm, up1, down1, cap_message))
+    cap_parts = cap_parts + send_captions(cap_message, range(2, txt_count))
     cap = jnp.concatenate(cap_parts, axis=1)
     partner = jnp.where(z % 2 == 1, up1, down1)
     near = jnp.zeros(part_shape, BF16)
@@ -1049,20 +1049,18 @@
     late_total, growth, early_other, other_here, cap_back = lax.optimization_barrier(
         (late_total, growth, early_other, other_here, cap_back)
     )
-    late, growth = gather_places(late_total, place_index, txt_count, growth)
-    growth_parts = [head_shift(growth, shift, head_count) for shift in range(1, head_count)]
-    growth_parts[0], cap_back = lax.optimization_barrier((growth_parts[0], cap_back))
+    growth = gather_head(growth, z, head_count)
     cap_parts = []
     for step in range(txt_count):
         perm = [(b, a) for a, b in caption_perm(step, 2, txt_count, 2)]
         cap_parts.append(
             lax.ppermute(cap_back[:, step * cap_here : (step + 1) * cap_here], ("vid", "txt"), perm)
         )
+    late = gather_places(late_total, place_index, txt_count)
     video_grad, latent_grad = place(video_grad, latent_grad, other_here)
-    late, video_grad, latent_grad, cap_parts, growth_parts = lax.optimization_barrier(
-        (late, video_grad, latent_grad, cap_parts, growth_parts)
-    )
-    growth = place_head(growth, growth_parts, z, head_count)
+    late, video_grad, latent_grad, cap_parts, growth = lax.optimization_barrier(
+        (late, video_grad, latent_grad, cap_parts, growth)
+    )
     late = gather_cores(late, core).astype(F32)
     caption_grad = jnp.zeros((txt_count, own, cap_here, D), F32)
     for step, part in enumerate(cap_parts):

time: 318 us -> 312 us (0.981); the launches traced: 313 us -> 311 us
  waiting for transfers between devices: 49.6 us -> 46.4 us
    ppermute x12, waiting for transfers between devices: 33.7 us -> 25.6 us  [head_shift(): lax.ppermute(values, 'head', [(i, (i - shift) % count) for i in range(cou...]
    ppermute x3, waiting for transfers between devices: 0.01 us -> 4.82 us  [gather_places(): lax.ppermute(total, 'txt', perm)]
  transfers between devices with their start and end apart: 40 -> 40, of which waited for: 11 -> 13; matrix products, arithmetic and copies ran while one was open for 8% -> 9% of each run, Pallas kernels for 33% -> 33%
where the time goes in v6:
time: 312 us; the launch traced here: 311 us
  Pallas kernels  131 us (42%)
  starting transfers between devices  55.7 us (18%)
  waiting for transfers between devices  46.4 us (15%)
  local copies, waits for them, and re-layouts  29.4 us (9%)
  other arithmetic  20.4 us (7%)
  between operations  17 us (5%)
  matrix products  10.7 us (3%)
    pallas_call x4, Pallas kernels, call(): pl.pallas_call(kernel, name=name, grid_spec=pltpu.PrefetchScalarGridSpec(...  125 us
    ppermute x12, waiting for transfers between devices, head_shift(): lax.ppermute(values, 'head', [(i, (i - shift) % count) for i in range(cou...  25.6 us
    ppermute x12, starting transfers between devices, head_shift(): lax.ppermute(values, 'head', [(i, (i - shift) % count) for i in range(cou...  14.5 us
    unnamed x81, local copies, waits for them, and re-layouts  11.1 us
    dot_general x7, matrix products, dot(): return jnp.einsum(spec, a, b, preferred_element_type=F32)  10.7 us
    ppermute x4, starting transfers between devices, send_captions(): lax.ppermute(take_block(message, (place_index + step) % txt_count, own),...  9.01 us
    ppermute x4, starting transfers between devices, local(): lax.ppermute(cap_back[:, step * cap_here:(step + 1) * cap_here], ('vid',...  7.78 us
    ppermute x3, waiting for transfers between devices, reduce_over_group(): total = total + lax.ppermute(chunk, 'txt', perm).astype(F32)  7.48 us
  transfers between devices with their start and end apart: 40, of which 13 were waited for; matrix products, arithmetic and copies ran while one was open for 9% of the time, Pallas kernels for 33%

profile of v6, /device:TPU:0, one launch (start us, length us, event | category | flops | bytes accessed | tf_op | source)
XLA Modules:
  0.0 311.1 jit_solution(691476326771902913)
XLA Ops:
  7.3 2.2 constant_dynamic-slice_fusion.9
  9.7 2.1 pad_maximum_fusion
  14.6 5.3 %collective-permute-start.1 = (bf16[2,192,768]{2,1,0:T(8,128)(2,1)}, bf16[2,192,768]{2,1,0:T(8,128)(2,1)}, u32[]{:S(2)}, u32[]{:S(2)}) collective-permute-start(bf16[2,192,768]{2,1,0:T(8,128)(2,1)} %constant_dynamic-slice_fusion.6), channel_id=1, source_target_pairs={{0,1},{1,2},{2,3},{4,5},{5,6},{6,7},{8,9},{9,10},{10,11},{12,13},{... | collective-permute-start | bytes 1769480 | tf_op jit(solution)/shard_map/ppermute | solution.py:761
  23.4 2.1 collective-permute-start.3
  25.6 3.3 %collective-permute-start.4 = (bf16[4,16,896]{2,1,0:T(8,128)(2,1)}, bf16[4,16,896]{2,1,0:T(8,128)(2,1)}, u32[]{:S(2)}, u32[]{:S(2)}) collective-permute-start(bf16[4,16,896]{2,1,0:T(8,128)(2,1)} %get-tuple-element.197), channel_id=1, source_target_pairs={{0,16},{4,4},{8,20},{12,0},{16,24},{20,12},{24,28},{28,8},{1,17},{... | collective-permute-start | bytes 344072 | tf_op jit(solution)/shard_map/ppermute | solution.py:794
  36.8 10.7 %token_norm.1.tok_ref = bf16[4,1024,768]{2,1,0:T(8,128)(2,1)} custom-call(s32[8]{0:T(128)} %concatenate.28.s_ref, bf16[8,512,768]{2,1,0:T(8,128)(2,1)} %own_ref.3, bf16[4,640,768]{2,1,0:T(8,128)(2,1)} %collective-permute-done.other_ref, f32[1,768]{1,0:T(1,128)} %broadcast_in_dim.111.gain_ref), custom_call_target="tpu_custom_call" | custom-call | flops 9900000256 | bytes 9000000 | tf_op jit(solution)/shard_map/token_norm/pallas_call | solution.py:833
  50.7 2.9 collective-permute-start.6
  61.2 6.8 %collective-permute-start.9 = (bf16[2,192,768]{2,1,0:T(8,128)(2,1)S(1)}, bf16[2,192,768]{2,1,0:T(8,128)(2,1)S(1)}, u32[]{:S(2)}, u32[]{:S(2)}) collective-permute-start(bf16[2,192,768]{2,1,0:T(8,128)(2,1)S(1)} %get-tuple-element.193), channel_id=1, source_target_pairs={{1,0},{2,1},{0,3},{5,4},{6,5},{4,7},{9,8},{10,9},{8,11},{13,12},{1... | collective-permute-start | bytes 1769480 | tf_op jit(solution)/shard_map/ppermute | solution.py:876
  69.5 27.4 %attention_forward.2 = (bf16[4,128,768]{2,1,0:T(8,128)(2,1)}, bf16[4,1088,768]{2,1,0:T(8,128)(2,1)}, bf16[4,1088,768]{2,1,0:T(8,128)(2,1)}, f32[4,2,8,256]{3,2,1,0:T(8,128)}, f32[4,128,768]{2,1,0:T(8,128)}) custom-call(s32[8]{0:T(128)} %concatenate.28.s_ref, bf16[4,1024,768]{2,1,0:T(8,128)(2,1)} %token_norm.1.tok_ref, bf16[4,64,896]{2,1,0:T(8,128)(2,1)} %copy-done.31, ...), custom_call_target="tpu_custom_call" | custom-call | flops 25300000768 | bytes 23000000 | tf_op jit(solution)/shard_map/attention_forward/pallas_call | solution.py:833
  104.9 27.5 %attention_forward.3 = (bf16[4,128,768]{2,1,0:T(8,128)(2,1)}, bf16[4,1088,768]{2,1,0:T(8,128)(2,1)}, bf16[4,1088,768]{2,1,0:T(8,128)(2,1)}, f32[4,2,8,256]{3,2,1,0:T(8,128)}, f32[4,128,768]{2,1,0:T(8,128)}) custom-call(s32[8]{0:T(128)} %concatenate.27.s_ref, ...), custom_call_target="tpu_custom_call", output_to_operand_aliasing={{0}: (8, {}), {1}: (9, {}), {2}: (10, {}), {3}: (11, {}), {... | custom-call | flops 25300000768 | bytes 23000000 | tf_op jit(solution)/shard_map/attention_forward/pallas_call | solution.py:833
  132.5 2.3 fusion.30
  135.5 3.9 %multiply_convert_fusion = (bf16[4,128,768]{2,1,0:T(8,128)(2,1)S(1)}, f32[4,128,768]{2,1,0:T(8,128)S(1)}, f32[4,128,768]{2,1,0:T(8,128)S(1)}) fusion(bf16[768,768]{1,0:T(8,128)(2,1)S(1)} %copy-done, f32[4,128,768]{2,1,0:T(8,128)S(1)} %get-tuple-element.204.attn_ref, f32[768]{0:T(1024)S(1)} %copy-done.38, f32[4,128]{1,0:T(4,128)S(1)} %add_rsqrt_fusion, ...), kind=kOutput, calls=%fused_computation.11 | convolution fusion | flops 631111680 | bytes 6691840 | tf_op jit(solution)/shard_map/bld,df->blf/dot_general | solution.py:757
  149.0 11.9 %collective-permute-done.12 = bf16[128,768]{1,0:T(8,128)(2,1)S(1)} collective-permute-done((bf16[128,768]{1,0:T(8,128)(2,1)S(1)}, bf16[128,768]{1,0:T(8,128)(2,1)S(1)}, u32[]{:S(2)}, u32[]{:S(2)}) %collective-permute-start.12) | collective-permute-done | bytes 196640 | tf_op jit(solution)/shard_map/ppermute | solution.py:397
  168.1 12.1 %collective-permute-done.15 = bf16[128,768]{1,0:T(8,128)(2,1)S(1)} collective-permute-done((bf16[128,768]{1,0:T(8,128)(2,1)S(1)}, bf16[128,768]{1,0:T(8,128)(2,1)S(1)}, u32[]{:S(2)}, u32[]{:S(2)}) %collective-permute-start.15) | collective-permute-done | bytes 196640 | tf_op jit(solution)/shard_map/ppermute | solution.py:397
  186.5 59.9 %attention_backward.1 = (f32[8,512,768]{2,1,0:T(8,128)}, bf16[4,576,768]{2,1,0:T(8,128)(2,1)}, bf16[4,64,768]{2,1,0:T(8,128)(2,1)}, f32[8,64,768]{2,1,0:T(8,128)}, bf16[896,768]{1,0:T(8,128)(2,1)}) custom-call(s32[8]{0:T(128)} %concatenate.28.s_ref, bf16[4,128,768]{2,1,0:T(8,128)(2,1)} %get-tuple-element.121.q_ref, ...), custom_call_target="tpu_custom_call" | custom-call | flops 3300000000 | bytes 3000000 | tf_op jit(solution)/shard_map/attention_backward/pallas_call | solution.py:833
  247.7 2.3 collective-permute-done.21
  256.0 3.1 %collective-permute-done.22 = bf16[112,768]{1,0:T(8,128)(2,1)S(1)} collective-permute-done((bf16[112,768]{1,0:T(8,128)(2,1)S(1)}, bf16[112,768]{1,0:T(8,128)(2,1)S(1)}, u32[]{:S(2)}, u32[]{:S(2)}) %collective-permute-start.22) | collective-permute-done | bytes 172064 | tf_op jit(solution)/shard_map/ppermute | solution.py:449
  259.1 2.5 collective-permute-done.23
  263.6 2.3 collective-permute-start.34
  269.8 3.8 %select_convert_fusion = (f32[768,768]{1,0:T(8,128)}, f32[768,768]{1,0:T(8,128)}) fusion(bf16[768,768]{1,0:T(8,128)(2,1)} %collective-permute-done.25, bf16[768,768]{1,0:T(8,128)(2,1)S(1)} %copy-done.27, pred[]{:T(512)S(6)} %eq.65), kind=kLoop, calls=%fused_computation.42 | loop fusion | flops 2359296 | bytes 7077889 | tf_op jit(solution)/shard_map/convert_element_type | solution.py:1092
  273.6 6.0 %place_rows.1 = (f32[8,512,768]{2,1,0:T(8,128)}, f32[8,64,768]{2,1,0:T(8,128)}) custom-call(s32[8]{0:T(128)} %concatenate.28.s_ref, f32[8,512,768]{2,1,0:T(8,128)} %get-tuple-element.142.video_in, f32[8,64,768]{2,1,0:T(8,128)} %get-tuple-element.143.lat_in, ...), custom_call_target="tpu_custom_call", output_to_operand_aliasing={{0}: (1, {}), {1}: (2, {})} | custom-call | flops 6000000000 | bytes 10000000 | tf_op jit(solution)/shard_map/place_rows/pallas_call | solution.py:1014
  281.4 4.8 %collective-permute-done.29 = bf16[112,768]{1,0:T(8,128)(2,1)S(1)} collective-permute-done((bf16[112,768]{1,0:T(8,128)(2,1)S(1)}, bf16[112,768]{1,0:T(8,128)(2,1)S(1)}, u32[]{:S(2)}, u32[]{:S(2)}) %collective-permute-start.29) | collective-permute-done | bytes 172064 | tf_op jit(solution)/shard_map/ppermute | solution.py:459
  286.2 3.1 %collective-permute-start.31 = (bf16[4,16,768]{2,1,0:T(8,128)(2,1)S(1)}, bf16[4,16,768]{2,1,0:T(8,128)(2,1)S(1)}, u32[]{:S(2)}, u32[]{:S(2)}) collective-permute-start(bf16[4,16,768]{2,1,0:T(8,128)(2,1)S(1)} %get-tuple-element.201), channel_id=1, source_target_pairs={{16,0},{4,4},{20,8},{0,12},{24,16},{12,20},{28,24},{8,28},{17,1},{... | collective-permute-start | bytes 294920 | tf_op jit(solution)/shard_map/ppermute | solution.py:1057
  289.6 3.8 %collective-permute-start.33 = (bf16[4,16,768]{2,1,0:T(8,128)(2,1)S(1)}, bf16[4,16,768]{2,1,0:T(8,128)(2,1)S(1)}, u32[]{:S(2)}, u32[]{:S(2)}) collective-permute-start(bf16[4,16,768]{2,1,0:T(8,128)(2,1)S(1)} %get-tuple-element.199), channel_id=1, source_target_pairs={{20,0},{0,4},{16,8},{4,12},{28,16},{8,20},{24,24},{12,28},{21,1},{... | collective-permute-start | bytes 294920 | tf_op jit(solution)/shard_map/ppermute | solution.py:1057
  (236 shorter events, 82.1 us)
Async XLA Ops:
  7.2 239.2 %all-reduce.2.cloned.1.call-start = ((), (), s32[]{:S(2)}) async-start(), calls=%async_computation | async-start | bytes 2359296 | tf_op jit(solution)/shard_map/psum | solution.py:953
  11.8 25.0 %collective-permute-start = (bf16[4,640,768]{2,1,0:T(8,128)(2,1)}, bf16[4,640,768]{2,1,0:T(8,128)(2,1)}, u32[]{:S(2)}, u32[]{:S(2)}) collective-permute-start(bf16[4,640,768]{2,1,0:T(8,128)(2,1)} %pad_maximum_fusion), channel_id=1, source_target_pairs={{0,16},{16,0},{1,17},{17,1},{2,18},{18,2},{3,19},{19,3},{4,20},{20... | collective-permute-start | bytes 11796488 | tf_op jit(solution)/shard_map/ppermute | solution.py:393
  14.6 32.9 %collective-permute-start.1 = (bf16[2,192,768]{2,1,0:T(8,128)(2,1)}, bf16[2,192,768]{2,1,0:T(8,128)(2,1)}, u32[]{:S(2)}, u32[]{:S(2)}) collective-permute-start(bf16[2,192,768]{2,1,0:T(8,128)(2,1)} %constant_dynamic-slice_fusion.6), channel_id=1, source_target_pairs={{0,1},{1,2},{2,3},{4,5},{5,6},{6,7},{8,9},{9,10},{10,11},{12,13},{... | collective-permute-start | bytes 1769480 | tf_op jit(solution)/shard_map/ppermute | solution.py:761
  19.9 27.6 %collective-permute-start.2 = (bf16[2,192,768]{2,1,0:T(8,128)(2,1)}, bf16[2,192,768]{2,1,0:T(8,128)(2,1)}, u32[]{:S(2)}, u32[]{:S(2)}) collective-permute-start(bf16[2,192,768]{2,1,0:T(8,128)(2,1)} %constant_dynamic-slice_fusion.6), channel_id=1, source_target_pairs={{1,0},{2,1},{3,2},{5,4},{6,5},{7,6},{9,8},{10,9},{11,10},{13,12},{... | collective-permute-start | bytes 1769480 | tf_op jit(solution)/shard_map/ppermute | solution.py:762
  23.4 11.4 %collective-permute-start.3 = (bf16[4,16,896]{2,1,0:T(8,128)(2,1)}, bf16[4,16,896]{2,1,0:T(8,128)(2,1)}, u32[]{:S(2)}, u32[]{:S(2)}) collective-permute-start(bf16[4,16,896]{2,1,0:T(8,128)(2,1)} %get-tuple-element.198), channel_id=1, source_target_pairs={{0,0},{4,16},{8,4},{12,20},{16,8},{20,24},{24,12},{28,28},{1,1},{5... | collective-permute-start | bytes 344072 | tf_op jit(solution)/shard_map/ppermute | solution.py:794
  25.6 10.3 %collective-permute-start.4 = (bf16[4,16,896]{2,1,0:T(8,128)(2,1)}, bf16[4,16,896]{2,1,0:T(8,128)(2,1)}, u32[]{:S(2)}, u32[]{:S(2)}) collective-permute-start(bf16[4,16,896]{2,1,0:T(8,128)(2,1)} %get-tuple-element.197), channel_id=1, source_target_pairs={{0,16},{4,4},{8,20},{12,0},{16,24},{20,12},{24,28},{28,8},{1,17},{... | collective-permute-start | bytes 344072 | tf_op jit(solution)/shard_map/ppermute | solution.py:794
  59.9 36.9 %collective-permute-start.8 = (bf16[2,192,768]{2,1,0:T(8,128)(2,1)S(1)}, bf16[2,192,768]{2,1,0:T(8,128)(2,1)S(1)}, u32[]{:S(2)}, u32[]{:S(2)}) collective-permute-start(bf16[2,192,768]{2,1,0:T(8,128)(2,1)S(1)} %get-tuple-element.194), channel_id=1, source_target_pairs={{1,2},{2,3},{3,0},{5,6},{6,7},{7,4},{9,10},{10,11},{11,8},{13,14},... | collective-permute-start | bytes 1769480 | tf_op jit(solution)/shard_map/ppermute | solution.py:875
  61.2 35.6 %collective-permute-start.9 = (bf16[2,192,768]{2,1,0:T(8,128)(2,1)S(1)}, bf16[2,192,768]{2,1,0:T(8,128)(2,1)S(1)}, u32[]{:S(2)}, u32[]{:S(2)}) collective-permute-start(bf16[2,192,768]{2,1,0:T(8,128)(2,1)S(1)} %get-tuple-element.193), channel_id=1, source_target_pairs={{1,0},{2,1},{0,3},{5,4},{6,5},{4,7},{9,8},{10,9},{8,11},{13,12},{1... | collective-permute-start | bytes 1769480 | tf_op jit(solution)/shard_map/ppermute | solution.py:876
  141.5 19.4 %collective-permute-start.12 = (bf16[128,768]{1,0:T(8,128)(2,1)S(1)}, bf16[128,768]{1,0:T(8,128)(2,1)S(1)}, u32[]{:S(2)}, u32[]{:S(2)}) collective-permute-start(bf16[128,768]{1,0:T(8,128)(2,1)S(1)} %get-tuple-element.185), channel_id=1, source_target_pairs={{0,2},{1,3},{2,0},{3,1},{4,6},{5,7},{6,4},{7,5},{8,10},{9,11},{10,... | collective-permute-start | bytes 589832 | tf_op jit(solution)/shard_map/ppermute | solution.py:397
  143.1 17.8 %collective-permute-start.13 = (bf16[128,768]{1,0:T(8,128)(2,1)S(1)}, bf16[128,768]{1,0:T(8,128)(2,1)S(1)}, u32[]{:S(2)}, u32[]{:S(2)}) collective-permute-start(bf16[128,768]{1,0:T(8,128)(2,1)S(1)} %get-tuple-element.186), channel_id=1, source_target_pairs={{0,1},{1,2},{2,3},{3,0},{4,5},{5,6},{6,7},{7,4},{8,9},{9,10},{10,1... | collective-permute-start | bytes 589832 | tf_op jit(solution)/shard_map/ppermute | solution.py:397
  161.1 19.1 %collective-permute-start.15 = (bf16[128,768]{1,0:T(8,128)(2,1)S(1)}, bf16[128,768]{1,0:T(8,128)(2,1)S(1)}, u32[]{:S(2)}, u32[]{:S(2)}) collective-permute-start(bf16[128,768]{1,0:T(8,128)(2,1)S(1)} %get-tuple-element.164), channel_id=1, source_target_pairs={{0,2},{1,3},{2,0},{3,1},{4,6},{5,7},{6,4},{7,5},{8,10},{9,11},{10,... | collective-permute-start | bytes 589832 | tf_op jit(solution)/shard_map/ppermute | solution.py:397
  162.6 17.7 %collective-permute-start.16 = (bf16[128,768]{1,0:T(8,128)(2,1)S(1)}, bf16[128,768]{1,0:T(8,128)(2,1)S(1)}, u32[]{:S(2)}, u32[]{:S(2)}) collective-permute-start(bf16[128,768]{1,0:T(8,128)(2,1)S(1)} %get-tuple-element.164), channel_id=1, source_target_pairs={{0,1},{1,2},{2,3},{3,0},{4,5},{5,6},{6,7},{7,4},{8,9},{9,10},{10,1... | collective-permute-start | bytes 589832 | tf_op jit(solution)/shard_map/ppermute | solution.py:397
  166.4 14.0 %collective-permute-start.17 = (bf16[768,768]{1,0:T(8,128)(2,1)S(1)}, bf16[768,768]{1,0:T(8,128)(2,1)S(1)}, u32[]{:S(2)}, u32[]{:S(2)}) collective-permute-start(bf16[768,768]{1,0:T(8,128)(2,1)S(1)} %get-tuple-element.208), channel_id=1, source_target_pairs={{0,16},{16,0},{1,17},{17,1},{2,18},{18,2},{3,19},{19,3},{4,20},{20... | collective-permute-start | bytes 3538952 | tf_op jit(solution)/shard_map/ppermute | solution.py:393
  183.4 62.9 %collective-permute-start.18 = (bf16[128,768]{1,0:T(8,128)(2,1)}, bf16[128,768]{1,0:T(8,128)(2,1)S(1)}, u32[]{:S(2)}, u32[]{:S(2)}) collective-permute-start(bf16[128,768]{1,0:T(8,128)(2,1)} %get-tuple-element.118), channel_id=1, source_target_pairs={{0,3},{1,0},{2,1},{3,2},{4,7},{5,4},{6,5},{7,6},{8,11},{9,8},{10,9... | collective-permute-start | bytes 589832 | tf_op jit(solution)/shard_map/ppermute | solution.py:397
  183.4 62.9 %collective-permute-start.19 = (bf16[128,768]{1,0:T(8,128)(2,1)}, bf16[128,768]{1,0:T(8,128)(2,1)S(1)}, u32[]{:S(2)}, u32[]{:S(2)}) collective-permute-start(bf16[128,768]{1,0:T(8,128)(2,1)} %get-tuple-element.119), channel_id=1, source_target_pairs={{0,2},{1,3},{2,0},{3,1},{4,6},{5,7},{6,4},{7,5},{8,10},{9,11},{10,... | collective-permute-start | bytes 589832 | tf_op jit(solution)/shard_map/ppermute | solution.py:397
  184.4 61.9 %collective-permute-start.20 = (bf16[128,768]{1,0:T(8,128)(2,1)}, bf16[128,768]{1,0:T(8,128)(2,1)S(1)}, u32[]{:S(2)}, u32[]{:S(2)}) collective-permute-start(bf16[128,768]{1,0:T(8,128)(2,1)} %get-tuple-element.120), channel_id=1, source_target_pairs={{0,1},{1,2},{2,3},{3,0},{4,5},{5,6},{6,7},{7,4},{8,9},{9,10},{10,1... | collective-permute-start | bytes 589832 | tf_op jit(solution)/shard_map/ppermute | solution.py:397
  250.0 13.6 %collective-permute-start.26 = (bf16[4,576,768]{2,1,0:T(8,128)(2,1)}, bf16[4,576,768]{2,1,0:T(8,128)(2,1)}, u32[]{:S(2)}, u32[]{:S(2)}) collective-permute-start(bf16[4,576,768]{2,1,0:T(8,128)(2,1)} %get-tuple-element.139), channel_id=1, source_target_pairs={{0,16},{16,0},{1,17},{17,1},{2,18},{18,2},{3,19},{19,3},{4,20},{20... | collective-permute-start | bytes 10616840 | tf_op jit(solution)/shard_map/ppermute | solution.py:393
  250.1 13.5 %collective-permute-start.25 = (bf16[768,768]{1,0:T(8,128)(2,1)}, bf16[768,768]{1,0:T(8,128)(2,1)}, u32[]{:S(2)}, u32[]{:S(2)}) collective-permute-start(bf16[768,768]{1,0:T(8,128)(2,1)} %all-reduce.2.cloned.1.call-done), channel_id=1, source_target_pairs={{0,16},{16,0},{1,17},{17,1},{2,18},{18,2},{3,19},{19,3},{4,20},{20... | collective-permute-start | bytes 3538952 | tf_op jit(solution)/shard_map/ppermute | solution.py:393
  263.6 25.7 %collective-permute-start.34 = (bf16[128,768]{1,0:T(8,128)(2,1)S(1)}, bf16[128,768]{1,0:T(8,128)(2,1)S(1)}, u32[]{:S(2)}, u32[]{:S(2)}) collective-permute-start(bf16[128,768]{1,0:T(8,128)(2,1)S(1)} %add_convert_fusion.3), channel_id=1, source_target_pairs={{0,3},{1,0},{2,1},{3,2},{4,7},{5,4},{6,5},{7,6},{8,11},{9,8},{10,9... | collective-permute-start | bytes 589832 | tf_op jit(solution)/shard_map/ppermute | solution.py:397
  265.9 23.7 %collective-permute-start.35 = (bf16[128,768]{1,0:T(8,128)(2,1)S(1)}, bf16[128,768]{1,0:T(8,128)(2,1)S(1)}, u32[]{:S(2)}, u32[]{:S(2)}) collective-permute-start(bf16[128,768]{1,0:T(8,128)(2,1)S(1)} %add_convert_fusion.3), channel_id=1, source_target_pairs={{0,2},{1,3},{2,0},{3,1},{4,6},{5,7},{6,4},{7,5},{8,10},{9,11},{10,... | collective-permute-start | bytes 589832 | tf_op jit(solution)/shard_map/ppermute | solution.py:397
  266.1 27.3 %collective-permute-start.36 = (bf16[128,768]{1,0:T(8,128)(2,1)S(1)}, bf16[128,768]{1,0:T(8,128)(2,1)S(1)}, u32[]{:S(2)}, u32[]{:S(2)}) collective-permute-start(bf16[128,768]{1,0:T(8,128)(2,1)S(1)} %add_convert_fusion.3), channel_id=1, source_target_pairs={{0,1},{1,2},{2,3},{3,0},{4,5},{5,6},{6,7},{7,4},{8,9},{9,10},{10,1... | collective-permute-start | bytes 589832 | tf_op jit(solution)/shard_map/ppermute | solution.py:397
  268.0 11.7 %collective-permute-start.27 = (bf16[112,768]{1,0:T(8,128)(2,1)S(1)}, bf16[112,768]{1,0:T(8,128)(2,1)S(1)}, u32[]{:S(2)}, u32[]{:S(2)}) collective-permute-start(bf16[112,768]{1,0:T(8,128)(2,1)S(1)} %add_convert_fusion.4), channel_id=1, source_target_pairs={{0,12},{4,0},{8,4},{12,8},{1,13},{5,1},{9,5},{13,9},{2,14},{6,2},{... | collective-permute-start | bytes 516104 | tf_op jit(solution)/shard_map/ppermute | solution.py:459
  269.2 11.5 %collective-permute-start.28 = (bf16[112,768]{1,0:T(8,128)(2,1)S(1)}, bf16[112,768]{1,0:T(8,128)(2,1)S(1)}, u32[]{:S(2)}, u32[]{:S(2)}) collective-permute-start(bf16[112,768]{1,0:T(8,128)(2,1)S(1)} %add_convert_fusion.4), channel_id=1, source_target_pairs={{0,8},{4,12},{8,0},{12,4},{1,9},{5,13},{9,1},{13,5},{2,10},{6,14},... | collective-permute-start | bytes 516104 | tf_op jit(solution)/shard_map/ppermute | solution.py:459
  280.7 12.8 %collective-permute-start.30 = (bf16[4,16,768]{2,1,0:T(8,128)(2,1)S(1)}, bf16[4,16,768]{2,1,0:T(8,128)(2,1)S(1)}, u32[]{:S(2)}, u32[]{:S(2)}) collective-permute-start(bf16[4,16,768]{2,1,0:T(8,128)(2,1)S(1)} %get-tuple-element.202), channel_id=1, source_target_pairs={{0,0},{16,4},{4,8},{20,12},{8,16},{24,20},{12,24},{28,28},{1,1},{1... | collective-permute-start | bytes 294920 | tf_op jit(solution)/shard_map/ppermute | solution.py:1057
  (55 other events, 521.1 us)
Sparse Core Ops, SparseCore 0:
  182.0 52.6 all-reduce.1

commit v7 on v6

--- a/solution.py
+++ b/solution.py
@@ -799,7 +799,7 @@
             for step in steps
         ]
 
-    cap_parts = send_captions(cap_message, range(2))
+    cap_parts = send_captions(cap_message, range(txt_count))
 
     def item_spec(rows, width=D, first=0):
         return pl.BlockSpec((None, rows, width), lambda i, s: (first + i, 0, 0))
@@ -862,8 +862,7 @@
         (video_tokens, video_other, gain_tok_row),
         9,
     )
-    tok_norm, up1, down1, cap_message = lax.optimization_barrier((tok_norm, up1, down1, cap_message))
-    cap_parts = cap_parts + send_captions(cap_message, range(2, txt_count))
+    tok_norm, up1, down1, cap_parts = lax.optimization_barrier((tok_norm, up1, down1, cap_parts))
     cap = jnp.concatenate(cap_parts, axis=1)
     partner = jnp.where(z % 2 == 1, up1, down1)
     near = jnp.zeros(part_shape, BF16)

time: 312 us -> 309 us (level)
  transfers between devices with their start and end apart: 40 -> 40, of which waited for: 13 -> 11; matrix products, arithmetic and copies ran while one was open for 9% -> 8% of each run, Pallas kernels for 33% -> 34%
where the time goes in v7:
time: 309 us; the launch traced here: 308 us
  Pallas kernels  131 us (42%)
  starting transfers between devices  54.9 us (18%)
  waiting for transfers between devices  46 us (15%)
  local copies, waits for them, and re-layouts  27.8 us (9%)
  other arithmetic  20.3 us (7%)
  between operations  17 us (6%)
  matrix products  10.7 us (3%)
    pallas_call x4, Pallas kernels, call(): pl.pallas_call(kernel, name=name, grid_spec=pltpu.PrefetchScalarGridSpec(...  125 us
    ppermute x12, waiting for transfers between devices, head_shift(): lax.ppermute(values, 'head', [(i, (i - shift) % count) for i in range(cou...  25.6 us
    ppermute x12, starting transfers between devices, head_shift(): lax.ppermute(values, 'head', [(i, (i - shift) % count) for i in range(cou...  14.2 us
    dot_general x7, matrix products, dot(): return jnp.einsum(spec, a, b, preferred_element_type=F32)  10.7 us
    ppermute x4, starting transfers between devices, send_captions(): lax.ppermute(take_block(message, (place_index + step) % txt_count, own),...  10.1 us
    unnamed x81, local copies, waits for them, and re-layouts  9.36 us
    ppermute x3, waiting for transfers between devices, reduce_over_group(): total = total + lax.ppermute(chunk, 'txt', perm).astype(F32)  8.81 us
    ppermute x4, starting transfers between devices, local(): lax.ppermute(cap_back[:, step * cap_here:(step + 1) * cap_here], ('vid',...  8 us
  transfers between devices with their start and end apart: 40, of which 11 were waited for; matrix products, arithmetic and copies ran while one was open for 8% of the time, Pallas kernels for 34%

profile of v7, /device:TPU:0, one launch (start us, length us, event | category | flops | bytes accessed | tf_op | source)
XLA Modules:
  0.0 308.2 jit_solution(17933416504662579147)
XLA Ops:
  7.3 2.2 constant_dynamic-slice_fusion.7
  9.7 2.1 pad_maximum_fusion
  14.6 5.3 %collective-permute-start.1 = (bf16[2,192,768]{2,1,0:T(8,128)(2,1)}, bf16[2,192,768]{2,1,0:T(8,128)(2,1)}, u32[]{:S(2)}, u32[]{:S(2)}) collective-permute-start(bf16[2,192,768]{2,1,0:T(8,128)(2,1)} %constant_dynamic-slice_fusion.4), channel_id=1, source_target_pairs={{0,1},{1,2},{2,3},{4,5},{5,6},{6,7},{8,9},{9,10},{10,11},{12,13},{... | collective-permute-start | bytes 1769480 | tf_op jit(solution)/shard_map/ppermute | solution.py:761
  24.4 3.9 %collective-permute-start.4 = (bf16[4,16,896]{2,1,0:T(8,128)(2,1)}, bf16[4,16,896]{2,1,0:T(8,128)(2,1)S(1)}, u32[]{:S(2)}, u32[]{:S(2)}) collective-permute-start(bf16[4,16,896]{2,1,0:T(8,128)(2,1)} %get-tuple-element.203), channel_id=1, source_target_pairs={{0,16},{4,4},{8,20},{12,0},{16,24},{20,12},{24,28},{28,8},{1,17},{... | collective-permute-start | bytes 344072 | tf_op jit(solution)/shard_map/ppermute | solution.py:794
  35.2 4.6 %collective-permute-start.6 = (bf16[4,16,896]{2,1,0:T(8,128)(2,1)S(1)}, bf16[4,16,896]{2,1,0:T(8,128)(2,1)S(1)}, u32[]{:S(2)}, u32[]{:S(2)}) collective-permute-start(bf16[4,16,896]{2,1,0:T(8,128)(2,1)S(1)} %copy-done.33), channel_id=1, source_target_pairs={{0,20},{4,0},{8,16},{12,4},{16,28},{20,8},{24,24},{28,12},{1,21},{... | collective-permute-start | bytes 344072 | tf_op jit(solution)/shard_map/ppermute | solution.py:794
  39.9 10.7 %token_norm.1.tok_ref = bf16[4,1024,768]{2,1,0:T(8,128)(2,1)} custom-call(s32[8]{0:T(128)} %concatenate.28.s_ref, bf16[8,512,768]{2,1,0:T(8,128)(2,1)} %own_ref.3, bf16[4,640,768]{2,1,0:T(8,128)(2,1)} %collective-permute-done.other_ref, f32[1,768]{1,0:T(1,128)} %broadcast_in_dim.111.gain_ref), custom_call_target="tpu_custom_call" | custom-call | flops 9900000256 | bytes 9000000 | tf_op jit(solution)/shard_map/token_norm/pallas_call | solution.py:833
  52.0 2.1 fusion.28
  57.8 7.3 %collective-permute-start.9 = (bf16[2,192,768]{2,1,0:T(8,128)(2,1)S(1)}, bf16[2,192,768]{2,1,0:T(8,128)(2,1)S(1)}, u32[]{:S(2)}, u32[]{:S(2)}) collective-permute-start(bf16[2,192,768]{2,1,0:T(8,128)(2,1)S(1)} %get-tuple-element.199), channel_id=1, source_target_pairs={{1,0},{2,1},{0,3},{5,4},{6,5},{4,7},{9,8},{10,9},{8,11},{13,12},{1... | collective-permute-start | bytes 1769480 | tf_op jit(solution)/shard_map/ppermute | solution.py:875
  66.6 27.4 %attention_forward.2 = (bf16[4,128,768]{2,1,0:T(8,128)(2,1)}, bf16[4,1088,768]{2,1,0:T(8,128)(2,1)}, bf16[4,1088,768]{2,1,0:T(8,128)(2,1)}, f32[4,2,8,256]{3,2,1,0:T(8,128)}, f32[4,128,768]{2,1,0:T(8,128)}) custom-call(s32[8]{0:T(128)} %concatenate.28.s_ref, bf16[4,1024,768]{2,1,0:T(8,128)(2,1)} %token_norm.1.tok_ref, bf16[4,64,896]{2,1,0:T(8,128)(2,1)} %copy-done.30, ...), custom_call_target="tpu_custom_call" | custom-call | flops 25300000768 | bytes 23000000 | tf_op jit(solution)/shard_map/attention_forward/pallas_call | solution.py:833
  102.1 27.5 %attention_forward.3 = (bf16[4,128,768]{2,1,0:T(8,128)(2,1)}, bf16[4,1088,768]{2,1,0:T(8,128)(2,1)}, bf16[4,1088,768]{2,1,0:T(8,128)(2,1)}, f32[4,2,8,256]{3,2,1,0:T(8,128)}, f32[4,128,768]{2,1,0:T(8,128)}) custom-call(s32[8]{0:T(128)} %concatenate.27.s_ref, ...), custom_call_target="tpu_custom_call", output_to_operand_aliasing={{0}: (8, {}), {1}: (9, {}), {2}: (10, {}), {3}: (11, {}), {... | custom-call | flops 25300000768 | bytes 23000000 | tf_op jit(solution)/shard_map/attention_forward/pallas_call | solution.py:833
  129.7 2.3 fusion.32
  132.7 3.9 %multiply_convert_fusion = (bf16[4,128,768]{2,1,0:T(8,128)(2,1)S(1)}, f32[4,128,768]{2,1,0:T(8,128)S(1)}, f32[4,128,768]{2,1,0:T(8,128)S(1)}) fusion(bf16[768,768]{1,0:T(8,128)(2,1)S(1)} %copy-done, f32[4,128,768]{2,1,0:T(8,128)S(1)} %get-tuple-element.210.attn_ref, f32[768]{0:T(1024)S(1)} %copy-done.38, f32[4,128]{1,0:T(4,128)S(1)} %add_rsqrt_fusion, ...), kind=kOutput, calls=%fused_computation.11 | convolution fusion | flops 631111680 | bytes 6691840 | tf_op jit(solution)/shard_map/bld,df->blf/dot_general | solution.py:757
  146.3 11.8 %collective-permute-done.12 = bf16[128,768]{1,0:T(8,128)(2,1)S(1)} collective-permute-done((bf16[128,768]{1,0:T(8,128)(2,1)S(1)}, bf16[128,768]{1,0:T(8,128)(2,1)S(1)}, u32[]{:S(2)}, u32[]{:S(2)}) %collective-permute-start.12) | collective-permute-done | bytes 196640 | tf_op jit(solution)/shard_map/ppermute | solution.py:397
  165.4 12.1 %collective-permute-done.15 = bf16[128,768]{1,0:T(8,128)(2,1)S(1)} collective-permute-done((bf16[128,768]{1,0:T(8,128)(2,1)S(1)}, bf16[128,768]{1,0:T(8,128)(2,1)S(1)}, u32[]{:S(2)}, u32[]{:S(2)}) %collective-permute-start.15) | collective-permute-done | bytes 196640 | tf_op jit(solution)/shard_map/ppermute | solution.py:397
  183.7 59.9 %attention_backward.1 = (f32[8,512,768]{2,1,0:T(8,128)}, bf16[4,576,768]{2,1,0:T(8,128)(2,1)}, bf16[4,64,768]{2,1,0:T(8,128)(2,1)}, f32[8,64,768]{2,1,0:T(8,128)}, bf16[896,768]{1,0:T(8,128)(2,1)}) custom-call(s32[8]{0:T(128)} %concatenate.28.s_ref, bf16[4,128,768]{2,1,0:T(8,128)(2,1)} %get-tuple-element.127.q_ref, ...), custom_call_target="tpu_custom_call" | custom-call | flops 3300000000 | bytes 3000000 | tf_op jit(solution)/shard_map/attention_backward/pallas_call | solution.py:833
  244.9 2.3 collective-permute-done.21
  251.6 4.8 %collective-permute-done.22 = bf16[112,768]{1,0:T(8,128)(2,1)S(1)} collective-permute-done((bf16[112,768]{1,0:T(8,128)(2,1)S(1)}, bf16[112,768]{1,0:T(8,128)(2,1)S(1)}, u32[]{:S(2)}, u32[]{:S(2)}) %collective-permute-start.22) | collective-permute-done | bytes 172064 | tf_op jit(solution)/shard_map/ppermute | solution.py:449
  256.3 4.0 %collective-permute-done.23 = bf16[112,768]{1,0:T(8,128)(2,1)S(1)} collective-permute-done((bf16[112,768]{1,0:T(8,128)(2,1)S(1)}, bf16[112,768]{1,0:T(8,128)(2,1)S(1)}, u32[]{:S(2)}, u32[]{:S(2)}) %collective-permute-start.23) | collective-permute-done | bytes 172064 | tf_op jit(solution)/shard_map/ppermute | solution.py:449
  260.5 2.2 collective-permute-start.34
  266.7 3.8 %select_convert_fusion = (f32[768,768]{1,0:T(8,128)}, f32[768,768]{1,0:T(8,128)}) fusion(bf16[768,768]{1,0:T(8,128)(2,1)} %collective-permute-done.25, bf16[768,768]{1,0:T(8,128)(2,1)S(1)} %copy-done.26, pred[]{:T(512)S(6)} %eq.65), kind=kLoop, calls=%fused_computation.42 | loop fusion | flops 2359296 | bytes 7077889 | tf_op jit(solution)/shard_map/convert_element_type | solution.py:1091
  270.5 6.0 %place_rows.1 = (f32[8,512,768]{2,1,0:T(8,128)}, f32[8,64,768]{2,1,0:T(8,128)}) custom-call(s32[8]{0:T(128)} %concatenate.28.s_ref, f32[8,512,768]{2,1,0:T(8,128)} %get-tuple-element.148.video_in, f32[8,64,768]{2,1,0:T(8,128)} %get-tuple-element.149.lat_in, ...), custom_call_target="tpu_custom_call", output_to_operand_aliasing={{0}: (1, {}), {1}: (2, {})} | custom-call | flops 6000000000 | bytes 10000000 | tf_op jit(solution)/shard_map/place_rows/pallas_call | solution.py:1013
  278.2 4.8 %collective-permute-done.29 = bf16[112,768]{1,0:T(8,128)(2,1)S(1)} collective-permute-done((bf16[112,768]{1,0:T(8,128)(2,1)S(1)}, bf16[112,768]{1,0:T(8,128)(2,1)S(1)}, u32[]{:S(2)}, u32[]{:S(2)}) %collective-permute-start.29) | collective-permute-done | bytes 172064 | tf_op jit(solution)/shard_map/ppermute | solution.py:459
  283.1 3.4 %collective-permute-start.31 = (bf16[4,16,768]{2,1,0:T(8,128)(2,1)S(1)}, bf16[4,16,768]{2,1,0:T(8,128)(2,1)S(1)}, u32[]{:S(2)}, u32[]{:S(2)}) collective-permute-start(bf16[4,16,768]{2,1,0:T(8,128)(2,1)S(1)} %get-tuple-element.207), channel_id=1, source_target_pairs={{16,0},{4,4},{20,8},{0,12},{24,16},{12,20},{28,24},{8,28},{17,1},{... | collective-permute-start | bytes 294920 | tf_op jit(solution)/shard_map/ppermute | solution.py:1056
  286.6 3.9 %collective-permute-start.33 = (bf16[4,16,768]{2,1,0:T(8,128)(2,1)S(1)}, bf16[4,16,768]{2,1,0:T(8,128)(2,1)S(1)}, u32[]{:S(2)}, u32[]{:S(2)}) collective-permute-start(bf16[4,16,768]{2,1,0:T(8,128)(2,1)S(1)} %get-tuple-element.205), channel_id=1, source_target_pairs={{20,0},{0,4},{16,8},{4,12},{28,16},{8,20},{24,24},{12,28},{21,1},{... | collective-permute-start | bytes 294920 | tf_op jit(solution)/shard_map/ppermute | solution.py:1056
  (234 shorter events, 72.9 us)
Async XLA Ops:
  7.2 236.4 %all-reduce.2.cloned.1.call-start = ((), (), s32[]{:S(2)}) async-start(), calls=%async_computation | async-start | bytes 2359296 | tf_op jit(solution)/shard_map/psum | solution.py:952
  11.8 23.4 %collective-permute-start = (bf16[4,640,768]{2,1,0:T(8,128)(2,1)}, bf16[4,640,768]{2,1,0:T(8,128)(2,1)}, u32[]{:S(2)}, u32[]{:S(2)}) collective-permute-start(bf16[4,640,768]{2,1,0:T(8,128)(2,1)} %pad_maximum_fusion), channel_id=1, source_target_pairs={{0,16},{16,0},{1,17},{17,1},{2,18},{18,2},{3,19},{19,3},{4,20},{20... | collective-permute-start | bytes 11796488 | tf_op jit(solution)/shard_map/ppermute | solution.py:393
  14.6 36.0 %collective-permute-start.1 = (bf16[2,192,768]{2,1,0:T(8,128)(2,1)}, bf16[2,192,768]{2,1,0:T(8,128)(2,1)}, u32[]{:S(2)}, u32[]{:S(2)}) collective-permute-start(bf16[2,192,768]{2,1,0:T(8,128)(2,1)} %constant_dynamic-slice_fusion.4), channel_id=1, source_target_pairs={{0,1},{1,2},{2,3},{4,5},{5,6},{6,7},{8,9},{9,10},{10,11},{12,13},{... | collective-permute-start | bytes 1769480 | tf_op jit(solution)/shard_map/ppermute | solution.py:761
  19.9 30.7 %collective-permute-start.2 = (bf16[2,192,768]{2,1,0:T(8,128)(2,1)}, bf16[2,192,768]{2,1,0:T(8,128)(2,1)}, u32[]{:S(2)}, u32[]{:S(2)}) collective-permute-start(bf16[2,192,768]{2,1,0:T(8,128)(2,1)} %constant_dynamic-slice_fusion.4), channel_id=1, source_target_pairs={{1,0},{2,1},{3,2},{5,4},{6,5},{7,6},{9,8},{10,9},{11,10},{13,12},{... | collective-permute-start | bytes 1769480 | tf_op jit(solution)/shard_map/ppermute | solution.py:762
  24.4 26.2 %collective-permute-start.4 = (bf16[4,16,896]{2,1,0:T(8,128)(2,1)}, bf16[4,16,896]{2,1,0:T(8,128)(2,1)S(1)}, u32[]{:S(2)}, u32[]{:S(2)}) collective-permute-start(bf16[4,16,896]{2,1,0:T(8,128)(2,1)} %get-tuple-element.203), channel_id=1, source_target_pairs={{0,16},{4,4},{8,20},{12,0},{16,24},{20,12},{24,28},{28,8},{1,17},{... | collective-permute-start | bytes 344072 | tf_op jit(solution)/shard_map/ppermute | solution.py:794
  35.2 15.4 %collective-permute-start.5 = (bf16[4,16,896]{2,1,0:T(8,128)(2,1)S(1)}, bf16[4,16,896]{2,1,0:T(8,128)(2,1)S(1)}, u32[]{:S(2)}, u32[]{:S(2)}) collective-permute-start(bf16[4,16,896]{2,1,0:T(8,128)(2,1)S(1)} %copy-done.34), channel_id=1, source_target_pairs={{0,4},{4,20},{8,0},{12,16},{16,12},{20,28},{24,8},{28,24},{1,5},{5... | collective-permute-start | bytes 344072 | tf_op jit(solution)/shard_map/ppermute | solution.py:794
  35.2 15.4 %collective-permute-start.6 = (bf16[4,16,896]{2,1,0:T(8,128)(2,1)S(1)}, bf16[4,16,896]{2,1,0:T(8,128)(2,1)S(1)}, u32[]{:S(2)}, u32[]{:S(2)}) collective-permute-start(bf16[4,16,896]{2,1,0:T(8,128)(2,1)S(1)} %copy-done.33), channel_id=1, source_target_pairs={{0,20},{4,0},{8,16},{12,4},{16,28},{20,8},{24,24},{28,12},{1,21},{... | collective-permute-start | bytes 344072 | tf_op jit(solution)/shard_map/ppermute | solution.py:794
  56.5 37.5 %collective-permute-start.8 = (bf16[2,192,768]{2,1,0:T(8,128)(2,1)S(1)}, bf16[2,192,768]{2,1,0:T(8,128)(2,1)S(1)}, u32[]{:S(2)}, u32[]{:S(2)}) collective-permute-start(bf16[2,192,768]{2,1,0:T(8,128)(2,1)S(1)} %get-tuple-element.200), channel_id=1, source_target_pairs={{1,2},{2,3},{3,0},{5,6},{6,7},{7,4},{9,10},{10,11},{11,8},{13,14},... | collective-permute-start | bytes 1769480 | tf_op jit(solution)/shard_map/ppermute | solution.py:874
  57.8 36.3 %collective-permute-start.9 = (bf16[2,192,768]{2,1,0:T(8,128)(2,1)S(1)}, bf16[2,192,768]{2,1,0:T(8,128)(2,1)S(1)}, u32[]{:S(2)}, u32[]{:S(2)}) collective-permute-start(bf16[2,192,768]{2,1,0:T(8,128)(2,1)S(1)} %get-tuple-element.199), channel_id=1, source_target_pairs={{1,0},{2,1},{0,3},{5,4},{6,5},{4,7},{9,8},{10,9},{8,11},{13,12},{1... | collective-permute-start | bytes 1769480 | tf_op jit(solution)/shard_map/ppermute | solution.py:875
  138.7 19.4 %collective-permute-start.12 = (bf16[128,768]{1,0:T(8,128)(2,1)S(1)}, bf16[128,768]{1,0:T(8,128)(2,1)S(1)}, u32[]{:S(2)}, u32[]{:S(2)}) collective-permute-start(bf16[128,768]{1,0:T(8,128)(2,1)S(1)} %get-tuple-element.191), channel_id=1, source_target_pairs={{0,2},{1,3},{2,0},{3,1},{4,6},{5,7},{6,4},{7,5},{8,10},{9,11},{10,... | collective-permute-start | bytes 589832 | tf_op jit(solution)/shard_map/ppermute | solution.py:397
  140.4 17.8 %collective-permute-start.13 = (bf16[128,768]{1,0:T(8,128)(2,1)S(1)}, bf16[128,768]{1,0:T(8,128)(2,1)S(1)}, u32[]{:S(2)}, u32[]{:S(2)}) collective-permute-start(bf16[128,768]{1,0:T(8,128)(2,1)S(1)} %get-tuple-element.192), channel_id=1, source_target_pairs={{0,1},{1,2},{2,3},{3,0},{4,5},{5,6},{6,7},{7,4},{8,9},{9,10},{10,1... | collective-permute-start | bytes 589832 | tf_op jit(solution)/shard_map/ppermute | solution.py:397
  158.3 19.2 %collective-permute-start.15 = (bf16[128,768]{1,0:T(8,128)(2,1)S(1)}, bf16[128,768]{1,0:T(8,128)(2,1)S(1)}, u32[]{:S(2)}, u32[]{:S(2)}) collective-permute-start(bf16[128,768]{1,0:T(8,128)(2,1)S(1)} %get-tuple-element.170), channel_id=1, source_target_pairs={{0,2},{1,3},{2,0},{3,1},{4,6},{5,7},{6,4},{7,5},{8,10},{9,11},{10,... | collective-permute-start | bytes 589832 | tf_op jit(solution)/shard_map/ppermute | solution.py:397
  159.9 17.7 %collective-permute-start.16 = (bf16[128,768]{1,0:T(8,128)(2,1)S(1)}, bf16[128,768]{1,0:T(8,128)(2,1)S(1)}, u32[]{:S(2)}, u32[]{:S(2)}) collective-permute-start(bf16[128,768]{1,0:T(8,128)(2,1)S(1)} %get-tuple-element.170), channel_id=1, source_target_pairs={{0,1},{1,2},{2,3},{3,0},{4,5},{5,6},{6,7},{7,4},{8,9},{9,10},{10,1... | collective-permute-start | bytes 589832 | tf_op jit(solution)/shard_map/ppermute | solution.py:397
  163.6 14.0 %collective-permute-start.17 = (bf16[768,768]{1,0:T(8,128)(2,1)S(1)}, bf16[768,768]{1,0:T(8,128)(2,1)S(1)}, u32[]{:S(2)}, u32[]{:S(2)}) collective-permute-start(bf16[768,768]{1,0:T(8,128)(2,1)S(1)} %get-tuple-element.214), channel_id=1, source_target_pairs={{0,16},{16,0},{1,17},{17,1},{2,18},{18,2},{3,19},{19,3},{4,20},{20... | collective-permute-start | bytes 3538952 | tf_op jit(solution)/shard_map/ppermute | solution.py:393
  180.7 62.9 %collective-permute-start.18 = (bf16[128,768]{1,0:T(8,128)(2,1)}, bf16[128,768]{1,0:T(8,128)(2,1)S(1)}, u32[]{:S(2)}, u32[]{:S(2)}) collective-permute-start(bf16[128,768]{1,0:T(8,128)(2,1)} %get-tuple-element.124), channel_id=1, source_target_pairs={{0,3},{1,0},{2,1},{3,2},{4,7},{5,4},{6,5},{7,6},{8,11},{9,8},{10,9... | collective-permute-start | bytes 589832 | tf_op jit(solution)/shard_map/ppermute | solution.py:397
  180.7 62.9 %collective-permute-start.19 = (bf16[128,768]{1,0:T(8,128)(2,1)}, bf16[128,768]{1,0:T(8,128)(2,1)S(1)}, u32[]{:S(2)}, u32[]{:S(2)}) collective-permute-start(bf16[128,768]{1,0:T(8,128)(2,1)} %get-tuple-element.125), channel_id=1, source_target_pairs={{0,2},{1,3},{2,0},{3,1},{4,6},{5,7},{6,4},{7,5},{8,10},{9,11},{10,... | collective-permute-start | bytes 589832 | tf_op jit(solution)/shard_map/ppermute | solution.py:397
  181.6 61.9 %collective-permute-start.20 = (bf16[128,768]{1,0:T(8,128)(2,1)}, bf16[128,768]{1,0:T(8,128)(2,1)S(1)}, u32[]{:S(2)}, u32[]{:S(2)}) collective-permute-start(bf16[128,768]{1,0:T(8,128)(2,1)} %get-tuple-element.126), channel_id=1, source_target_pairs={{0,1},{1,2},{2,3},{3,0},{4,5},{5,6},{6,7},{7,4},{8,9},{9,10},{10,1... | collective-permute-start | bytes 589832 | tf_op jit(solution)/shard_map/ppermute | solution.py:397
  247.2 13.3 %collective-permute-start.26 = (bf16[4,576,768]{2,1,0:T(8,128)(2,1)}, bf16[4,576,768]{2,1,0:T(8,128)(2,1)}, u32[]{:S(2)}, u32[]{:S(2)}) collective-permute-start(bf16[4,576,768]{2,1,0:T(8,128)(2,1)} %get-tuple-element.145), channel_id=1, source_target_pairs={{0,16},{16,0},{1,17},{17,1},{2,18},{18,2},{3,19},{19,3},{4,20},{20... | collective-permute-start | bytes 10616840 | tf_op jit(solution)/shard_map/ppermute | solution.py:393
  247.3 13.1 %collective-permute-start.25 = (bf16[768,768]{1,0:T(8,128)(2,1)}, bf16[768,768]{1,0:T(8,128)(2,1)}, u32[]{:S(2)}, u32[]{:S(2)}) collective-permute-start(bf16[768,768]{1,0:T(8,128)(2,1)} %all-reduce.2.cloned.1.call-done), channel_id=1, source_target_pairs={{0,16},{16,0},{1,17},{17,1},{2,18},{18,2},{3,19},{19,3},{4,20},{20... | collective-permute-start | bytes 3538952 | tf_op jit(solution)/shard_map/ppermute | solution.py:393
  260.5 26.0 %collective-permute-start.34 = (bf16[128,768]{1,0:T(8,128)(2,1)S(1)}, bf16[128,768]{1,0:T(8,128)(2,1)S(1)}, u32[]{:S(2)}, u32[]{:S(2)}) collective-permute-start(bf16[128,768]{1,0:T(8,128)(2,1)S(1)} %add_convert_fusion.3), channel_id=1, source_target_pairs={{0,3},{1,0},{2,1},{3,2},{4,7},{5,4},{6,5},{7,6},{8,11},{9,8},{10,9... | collective-permute-start | bytes 589832 | tf_op jit(solution)/shard_map/ppermute | solution.py:397
  262.7 23.9 %collective-permute-start.35 = (bf16[128,768]{1,0:T(8,128)(2,1)S(1)}, bf16[128,768]{1,0:T(8,128)(2,1)S(1)}, u32[]{:S(2)}, u32[]{:S(2)}) collective-permute-start(bf16[128,768]{1,0:T(8,128)(2,1)S(1)} %add_convert_fusion.3), channel_id=1, source_target_pairs={{0,2},{1,3},{2,0},{3,1},{4,6},{5,7},{6,4},{7,5},{8,10},{9,11},{10,... | collective-permute-start | bytes 589832 | tf_op jit(solution)/shard_map/ppermute | solution.py:397
  262.7 27.8 %collective-permute-start.36 = (bf16[128,768]{1,0:T(8,128)(2,1)S(1)}, bf16[128,768]{1,0:T(8,128)(2,1)S(1)}, u32[]{:S(2)}, u32[]{:S(2)}) collective-permute-start(bf16[128,768]{1,0:T(8,128)(2,1)S(1)} %add_convert_fusion.3), channel_id=1, source_target_pairs={{0,1},{1,2},{2,3},{3,0},{4,5},{5,6},{6,7},{7,4},{8,9},{9,10},{10,1... | collective-permute-start | bytes 589832 | tf_op jit(solution)/shard_map/ppermute | solution.py:397
  265.2 12.3 %collective-permute-start.28 = (bf16[112,768]{1,0:T(8,128)(2,1)S(1)}, bf16[112,768]{1,0:T(8,128)(2,1)S(1)}, u32[]{:S(2)}, u32[]{:S(2)}) collective-permute-start(bf16[112,768]{1,0:T(8,128)(2,1)S(1)} %add_convert_fusion.4), channel_id=1, source_target_pairs={{0,8},{4,12},{8,0},{12,4},{1,9},{5,13},{9,1},{13,5},{2,10},{6,14},... | collective-permute-start | bytes 516104 | tf_op jit(solution)/shard_map/ppermute | solution.py:459
  277.5 13.0 %collective-permute-start.30 = (bf16[4,16,768]{2,1,0:T(8,128)(2,1)S(1)}, bf16[4,16,768]{2,1,0:T(8,128)(2,1)S(1)}, u32[]{:S(2)}, u32[]{:S(2)}) collective-permute-start(bf16[4,16,768]{2,1,0:T(8,128)(2,1)S(1)} %get-tuple-element.208), channel_id=1, source_target_pairs={{0,0},{16,4},{4,8},{20,12},{8,16},{24,20},{12,24},{28,28},{1,1},{1... | collective-permute-start | bytes 294920 | tf_op jit(solution)/shard_map/ppermute | solution.py:1056
  (55 other events, 513.5 us)
Sparse Core Ops, SparseCore 0:
  179.3 51.9 all-reduce.1

commit v8 on v7

--- a/solution.py
+++ b/solution.py
@@ -1057,9 +1057,7 @@
         )
     late = gather_places(late_total, place_index, txt_count)
     video_grad, latent_grad = place(video_grad, latent_grad, other_here)
-    late, video_grad, latent_grad, cap_parts, growth = lax.optimization_barrier(
-        (late, video_grad, latent_grad, cap_parts, growth)
-    )
+    late, video_grad, latent_grad = lax.optimization_barrier((late, video_grad, latent_grad))
     late = gather_cores(late, core).astype(F32)
     caption_grad = jnp.zeros((txt_count, own, cap_here, D), F32)
     for step, part in enumerate(cap_parts):

time: 309 us -> 316 us (1.023)
    ppermute x12, waiting for transfers between devices: 25.6 us -> 33.7 us  [head_shift(): lax.ppermute(values, 'head', [(i, (i - shift) % count) for i in range(cou...]
    ppermute x3, waiting for transfers between devices: 4.82 us -> 0.01 us  [gather_places(): lax.ppermute(total, 'txt', perm)]
  transfers between devices with their start and end apart: 40 -> 40, of which waited for: 11 -> 10; matrix products, arithmetic and copies ran while one was open for 8% -> 8% of each run, Pallas kernels for 34% -> 33%
where the time goes in v8:
time: 316 us; the launch traced here: 314 us
  Pallas kernels  131 us (41%)
  starting transfers between devices  57.9 us (18%)
  waiting for transfers between devices  48.3 us (15%)
  local copies, waits for them, and re-layouts  27.8 us (9%)
  other arithmetic  21.4 us (7%)
  between operations  17 us (5%)
  matrix products  10.7 us (3%)
    pallas_call x4, Pallas kernels, call(): pl.pallas_call(kernel, name=name, grid_spec=pltpu.PrefetchScalarGridSpec(...  125 us
    ppermute x12, waiting for transfers between devices, head_shift(): lax.ppermute(values, 'head', [(i, (i - shift) % count) for i in range(cou...  33.7 us
    ppermute x12, starting transfers between devices, head_shift(): lax.ppermute(values, 'head', [(i, (i - shift) % count) for i in range(cou...  14.3 us
    dot_general x7, matrix products, dot(): return jnp.einsum(spec, a, b, preferred_element_type=F32)  10.7 us
    ppermute x4, starting transfers between devices, send_captions(): lax.ppermute(take_block(message, (place_index + step) % txt_count, own),...  10.1 us
    ppermute x4, starting transfers between devices, local(): lax.ppermute(cap_back[:, step * cap_here:(step + 1) * cap_here], ('vid',...  9.9 us
    unnamed x81, local copies, waits for them, and re-layouts  9.37 us
    ppermute x3, waiting for transfers between devices, reduce_over_group(): total = total + lax.ppermute(chunk, 'txt', perm).astype(F32)  8.81 us
  transfers between devices with their start and end apart: 40, of which 10 were waited for; matrix products, arithmetic and copies ran while one was open for 8% of the time, Pallas kernels for 33%

profile of v8, /device:TPU:0, one launch (start us, length us, event | category | flops | bytes accessed | tf_op | source)
XLA Modules:
  0.0 314.4 jit_solution(17324138960041467417)
XLA Ops:
  7.3 2.2 constant_dynamic-slice_fusion.7
  9.7 2.1 pad_maximum_fusion
  14.6 5.3 %collective-permute-start.1 = (bf16[2,192,768]{2,1,0:T(8,128)(2,1)}, bf16[2,192,768]{2,1,0:T(8,128)(2,1)}, u32[]{:S(2)}, u32[]{:S(2)}) collective-permute-start(bf16[2,192,768]{2,1,0:T(8,128)(2,1)} %constant_dynamic-slice_fusion.4), channel_id=1, source_target_pairs={{0,1},{1,2},{2,3},{4,5},{5,6},{6,7},{8,9},{9,10},{10,11},{12,13},{... | collective-permute-start | bytes 1769480 | tf_op jit(solution)/shard_map/ppermute | solution.py:761
  24.4 3.9 %collective-permute-start.4 = (bf16[4,16,896]{2,1,0:T(8,128)(2,1)}, bf16[4,16,896]{2,1,0:T(8,128)(2,1)S(1)}, u32[]{:S(2)}, u32[]{:S(2)}) collective-permute-start(bf16[4,16,896]{2,1,0:T(8,128)(2,1)} %get-tuple-element.193), channel_id=1, source_target_pairs={{0,16},{4,4},{8,20},{12,0},{16,24},{20,12},{24,28},{28,8},{1,17},{... | collective-permute-start | bytes 344072 | tf_op jit(solution)/shard_map/ppermute | solution.py:794
  35.2 4.6 %collective-permute-start.6 = (bf16[4,16,896]{2,1,0:T(8,128)(2,1)S(1)}, bf16[4,16,896]{2,1,0:T(8,128)(2,1)S(1)}, u32[]{:S(2)}, u32[]{:S(2)}) collective-permute-start(bf16[4,16,896]{2,1,0:T(8,128)(2,1)S(1)} %copy-done.33), channel_id=1, source_target_pairs={{0,20},{4,0},{8,16},{12,4},{16,28},{20,8},{24,24},{28,12},{1,21},{... | collective-permute-start | bytes 344072 | tf_op jit(solution)/shard_map/ppermute | solution.py:794
  39.9 10.7 %token_norm.1.tok_ref = bf16[4,1024,768]{2,1,0:T(8,128)(2,1)} custom-call(s32[8]{0:T(128)} %concatenate.28.s_ref, bf16[8,512,768]{2,1,0:T(8,128)(2,1)} %own_ref.3, bf16[4,640,768]{2,1,0:T(8,128)(2,1)} %collective-permute-done.other_ref, f32[1,768]{1,0:T(1,128)} %broadcast_in_dim.111.gain_ref), custom_call_target="tpu_custom_call" | custom-call | flops 9900000256 | bytes 9000000 | tf_op jit(solution)/shard_map/token_norm/pallas_call | solution.py:833
  52.0 2.1 fusion.28
  57.8 7.3 %collective-permute-start.9 = (bf16[2,192,768]{2,1,0:T(8,128)(2,1)S(1)}, bf16[2,192,768]{2,1,0:T(8,128)(2,1)S(1)}, u32[]{:S(2)}, u32[]{:S(2)}) collective-permute-start(bf16[2,192,768]{2,1,0:T(8,128)(2,1)S(1)} %get-tuple-element.189), channel_id=1, source_target_pairs={{1,0},{2,1},{0,3},{5,4},{6,5},{4,7},{9,8},{10,9},{8,11},{13,12},{1... | collective-permute-start | bytes 1769480 | tf_op jit(solution)/shard_map/ppermute | solution.py:875
  66.6 27.4 %attention_forward.2 = (bf16[4,128,768]{2,1,0:T(8,128)(2,1)}, bf16[4,1088,768]{2,1,0:T(8,128)(2,1)}, bf16[4,1088,768]{2,1,0:T(8,128)(2,1)}, f32[4,2,8,256]{3,2,1,0:T(8,128)}, f32[4,128,768]{2,1,0:T(8,128)}) custom-call(s32[8]{0:T(128)} %concatenate.28.s_ref, bf16[4,1024,768]{2,1,0:T(8,128)(2,1)} %token_norm.1.tok_ref, bf16[4,64,896]{2,1,0:T(8,128)(2,1)} %copy-done.30, ...), custom_call_target="tpu_custom_call" | custom-call | flops 25300000768 | bytes 23000000 | tf_op jit(solution)/shard_map/attention_forward/pallas_call | solution.py:833
  102.1 27.5 %attention_forward.3 = (bf16[4,128,768]{2,1,0:T(8,128)(2,1)}, bf16[4,1088,768]{2,1,0:T(8,128)(2,1)}, bf16[4,1088,768]{2,1,0:T(8,128)(2,1)}, f32[4,2,8,256]{3,2,1,0:T(8,128)}, f32[4,128,768]{2,1,0:T(8,128)}) custom-call(s32[8]{0:T(128)} %concatenate.27.s_ref, ...), custom_call_target="tpu_custom_call", output_to_operand_aliasing={{0}: (8, {}), {1}: (9, {}), {2}: (10, {}), {3}: (11, {}), {... | custom-call | flops 25300000768 | bytes 23000000 | tf_op jit(solution)/shard_map/attention_forward/pallas_call | solution.py:833
  129.7 2.3 fusion.32
  132.7 3.9 %multiply_convert_fusion = (bf16[4,128,768]{2,1,0:T(8,128)(2,1)S(1)}, f32[4,128,768]{2,1,0:T(8,128)S(1)}, f32[4,128,768]{2,1,0:T(8,128)S(1)}) fusion(bf16[768,768]{1,0:T(8,128)(2,1)S(1)} %copy-done, f32[4,128,768]{2,1,0:T(8,128)S(1)} %get-tuple-element.200.attn_ref, f32[768]{0:T(1024)S(1)} %copy-done.38, f32[4,128]{1,0:T(4,128)S(1)} %add_rsqrt_fusion, ...), kind=kOutput, calls=%fused_computation.11 | convolution fusion | flops 631111680 | bytes 6691840 | tf_op jit(solution)/shard_map/bld,df->blf/dot_general | solution.py:757
  146.3 11.8 %collective-permute-done.12 = bf16[128,768]{1,0:T(8,128)(2,1)S(1)} collective-permute-done((bf16[128,768]{1,0:T(8,128)(2,1)S(1)}, bf16[128,768]{1,0:T(8,128)(2,1)S(1)}, u32[]{:S(2)}, u32[]{:S(2)}) %collective-permute-start.12) | collective-permute-done | bytes 196640 | tf_op jit(solution)/shard_map/ppermute | solution.py:397
  165.4 12.1 %collective-permute-done.15 = bf16[128,768]{1,0:T(8,128)(2,1)S(1)} collective-permute-done((bf16[128,768]{1,0:T(8,128)(2,1)S(1)}, bf16[128,768]{1,0:T(8,128)(2,1)S(1)}, u32[]{:S(2)}, u32[]{:S(2)}) %collective-permute-start.15) | collective-permute-done | bytes 196640 | tf_op jit(solution)/shard_map/ppermute | solution.py:397
  183.7 59.9 %attention_backward.1 = (f32[8,512,768]{2,1,0:T(8,128)}, bf16[4,576,768]{2,1,0:T(8,128)(2,1)}, bf16[4,64,768]{2,1,0:T(8,128)(2,1)}, f32[8,64,768]{2,1,0:T(8,128)}, bf16[896,768]{1,0:T(8,128)(2,1)}) custom-call(s32[8]{0:T(128)} %concatenate.28.s_ref, bf16[4,128,768]{2,1,0:T(8,128)(2,1)} %get-tuple-element.122.q_ref, ...), custom_call_target="tpu_custom_call" | custom-call | flops 3300000000 | bytes 3000000 | tf_op jit(solution)/shard_map/attention_backward/pallas_call | solution.py:833
  244.9 2.3 collective-permute-done.21
  251.6 4.8 %collective-permute-done.22 = bf16[112,768]{1,0:T(8,128)(2,1)S(1)} collective-permute-done((bf16[112,768]{1,0:T(8,128)(2,1)S(1)}, bf16[112,768]{1,0:T(8,128)(2,1)S(1)}, u32[]{:S(2)}, u32[]{:S(2)}) %collective-permute-start.22) | collective-permute-done | bytes 172064 | tf_op jit(solution)/shard_map/ppermute | solution.py:449
  256.3 4.0 %collective-permute-done.23 = bf16[112,768]{1,0:T(8,128)(2,1)S(1)} collective-permute-done((bf16[112,768]{1,0:T(8,128)(2,1)S(1)}, bf16[112,768]{1,0:T(8,128)(2,1)S(1)}, u32[]{:S(2)}, u32[]{:S(2)}) %collective-permute-start.23) | collective-permute-done | bytes 172064 | tf_op jit(solution)/shard_map/ppermute | solution.py:449
  263.5 3.8 %select_convert_fusion = (f32[768,768]{1,0:T(8,128)}, f32[768,768]{1,0:T(8,128)}) fusion(bf16[768,768]{1,0:T(8,128)(2,1)} %collective-permute-done.25, bf16[768,768]{1,0:T(8,128)(2,1)S(1)} %copy-done.26, pred[]{:T(512)S(6)} %eq.65), kind=kLoop, calls=%fused_computation.42 | loop fusion | flops 2359296 | bytes 7077889 | tf_op jit(solution)/shard_map/convert_element_type | solution.py:1089
  270.6 6.0 %place_rows.1 = (f32[8,512,768]{2,1,0:T(8,128)}, f32[8,64,768]{2,1,0:T(8,128)}) custom-call(s32[8]{0:T(128)} %concatenate.28.s_ref, f32[8,512,768]{2,1,0:T(8,128)} %get-tuple-element.144.video_in, f32[8,64,768]{2,1,0:T(8,128)} %get-tuple-element.145.lat_in, ...), custom_call_target="tpu_custom_call", output_to_operand_aliasing={{0}: (1, {}), {1}: (2, {})} | custom-call | flops 6000000000 | bytes 10000000 | tf_op jit(solution)/shard_map/place_rows/pallas_call | solution.py:1013
  276.6 4.6 %collective-permute-start.35 = (bf16[4,16,768]{2,1,0:T(8,128)(2,1)S(1)}, bf16[4,16,768]{2,1,0:T(8,128)(2,1)S(1)}, u32[]{:S(2)}, u32[]{:S(2)}) collective-permute-start(bf16[4,16,768]{2,1,0:T(8,128)(2,1)S(1)} %get-tuple-element.197), channel_id=1, source_target_pairs={{16,0},{4,4},{20,8},{0,12},{24,16},{12,20},{28,24},{8,28},{17,1},{... | collective-permute-start | bytes 294920 | tf_op jit(solution)/shard_map/ppermute | solution.py:1056
  283.6 2.1 collective-permute-start.29
  287.6 2.2 collective-permute-start.37
  291.3 8.1 %collective-permute-done.28 = bf16[128,768]{1,0:T(8,128)(2,1)S(1)} collective-permute-done((bf16[128,768]{1,0:T(8,128)(2,1)S(1)}, bf16[128,768]{1,0:T(8,128)(2,1)S(1)}, u32[]{:S(2)}, u32[]{:S(2)}) %collective-permute-start.28) | collective-permute-done | bytes 196640 | tf_op jit(solution)/shard_map/ppermute | solution.py:397
  (234 shorter events, 76.5 us)
Async XLA Ops:
  7.2 236.4 %all-reduce.2.cloned.1.call-start = ((), (), s32[]{:S(2)}) async-start(), calls=%async_computation | async-start | bytes 2359296 | tf_op jit(solution)/shard_map/psum | solution.py:952
  11.8 23.4 %collective-permute-start = (bf16[4,640,768]{2,1,0:T(8,128)(2,1)}, bf16[4,640,768]{2,1,0:T(8,128)(2,1)}, u32[]{:S(2)}, u32[]{:S(2)}) collective-permute-start(bf16[4,640,768]{2,1,0:T(8,128)(2,1)} %pad_maximum_fusion), channel_id=1, source_target_pairs={{0,16},{16,0},{1,17},{17,1},{2,18},{18,2},{3,19},{19,3},{4,20},{20... | collective-permute-start | bytes 11796488 | tf_op jit(solution)/shard_map/ppermute | solution.py:393
  14.6 36.0 %collective-permute-start.1 = (bf16[2,192,768]{2,1,0:T(8,128)(2,1)}, bf16[2,192,768]{2,1,0:T(8,128)(2,1)}, u32[]{:S(2)}, u32[]{:S(2)}) collective-permute-start(bf16[2,192,768]{2,1,0:T(8,128)(2,1)} %constant_dynamic-slice_fusion.4), channel_id=1, source_target_pairs={{0,1},{1,2},{2,3},{4,5},{5,6},{6,7},{8,9},{9,10},{10,11},{12,13},{... | collective-permute-start | bytes 1769480 | tf_op jit(solution)/shard_map/ppermute | solution.py:761
  19.9 30.7 %collective-permute-start.2 = (bf16[2,192,768]{2,1,0:T(8,128)(2,1)}, bf16[2,192,768]{2,1,0:T(8,128)(2,1)}, u32[]{:S(2)}, u32[]{:S(2)}) collective-permute-start(bf16[2,192,768]{2,1,0:T(8,128)(2,1)} %constant_dynamic-slice_fusion.4), channel_id=1, source_target_pairs={{1,0},{2,1},{3,2},{5,4},{6,5},{7,6},{9,8},{10,9},{11,10},{13,12},{... | collective-permute-start | bytes 1769480 | tf_op jit(solution)/shard_map/ppermute | solution.py:762
  24.4 26.2 %collective-permute-start.4 = (bf16[4,16,896]{2,1,0:T(8,128)(2,1)}, bf16[4,16,896]{2,1,0:T(8,128)(2,1)S(1)}, u32[]{:S(2)}, u32[]{:S(2)}) collective-permute-start(bf16[4,16,896]{2,1,0:T(8,128)(2,1)} %get-tuple-element.193), channel_id=1, source_target_pairs={{0,16},{4,4},{8,20},{12,0},{16,24},{20,12},{24,28},{28,8},{1,17},{... | collective-permute-start | bytes 344072 | tf_op jit(solution)/shard_map/ppermute | solution.py:794
  35.2 15.4 %collective-permute-start.5 = (bf16[4,16,896]{2,1,0:T(8,128)(2,1)S(1)}, bf16[4,16,896]{2,1,0:T(8,128)(2,1)S(1)}, u32[]{:S(2)}, u32[]{:S(2)}) collective-permute-start(bf16[4,16,896]{2,1,0:T(8,128)(2,1)S(1)} %copy-done.34), channel_id=1, source_target_pairs={{0,4},{4,20},{8,0},{12,16},{16,12},{20,28},{24,8},{28,24},{1,5},{5... | collective-permute-start | bytes 344072 | tf_op jit(solution)/shard_map/ppermute | solution.py:794
  35.2 15.4 %collective-permute-start.6 = (bf16[4,16,896]{2,1,0:T(8,128)(2,1)S(1)}, bf16[4,16,896]{2,1,0:T(8,128)(2,1)S(1)}, u32[]{:S(2)}, u32[]{:S(2)}) collective-permute-start(bf16[4,16,896]{2,1,0:T(8,128)(2,1)S(1)} %copy-done.33), channel_id=1, source_target_pairs={{0,20},{4,0},{8,16},{12,4},{16,28},{20,8},{24,24},{28,12},{1,21},{... | collective-permute-start | bytes 344072 | tf_op jit(solution)/shard_map/ppermute | solution.py:794
  56.5 37.5 %collective-permute-start.8 = (bf16[2,192,768]{2,1,0:T(8,128)(2,1)S(1)}, bf16[2,192,768]{2,1,0:T(8,128)(2,1)S(1)}, u32[]{:S(2)}, u32[]{:S(2)}) collective-permute-start(bf16[2,192,768]{2,1,0:T(8,128)(2,1)S(1)} %get-tuple-element.190), channel_id=1, source_target_pairs={{1,2},{2,3},{3,0},{5,6},{6,7},{7,4},{9,10},{10,11},{11,8},{13,14},... | collective-permute-start | bytes 1769480 | tf_op jit(solution)/shard_map/ppermute | solution.py:874
  57.8 36.3 %collective-permute-start.9 = (bf16[2,192,768]{2,1,0:T(8,128)(2,1)S(1)}, bf16[2,192,768]{2,1,0:T(8,128)(2,1)S(1)}, u32[]{:S(2)}, u32[]{:S(2)}) collective-permute-start(bf16[2,192,768]{2,1,0:T(8,128)(2,1)S(1)} %get-tuple-element.189), channel_id=1, source_target_pairs={{1,0},{2,1},{0,3},{5,4},{6,5},{4,7},{9,8},{10,9},{8,11},{13,12},{1... | collective-permute-start | bytes 1769480 | tf_op jit(solution)/shard_map/ppermute | solution.py:875
  138.7 19.4 %collective-permute-start.12 = (bf16[128,768]{1,0:T(8,128)(2,1)S(1)}, bf16[128,768]{1,0:T(8,128)(2,1)S(1)}, u32[]{:S(2)}, u32[]{:S(2)}) collective-permute-start(bf16[128,768]{1,0:T(8,128)(2,1)S(1)} %get-tuple-element.181), channel_id=1, source_target_pairs={{0,2},{1,3},{2,0},{3,1},{4,6},{5,7},{6,4},{7,5},{8,10},{9,11},{10,... | collective-permute-start | bytes 589832 | tf_op jit(solution)/shard_map/ppermute | solution.py:397
  140.4 17.8 %collective-permute-start.13 = (bf16[128,768]{1,0:T(8,128)(2,1)S(1)}, bf16[128,768]{1,0:T(8,128)(2,1)S(1)}, u32[]{:S(2)}, u32[]{:S(2)}) collective-permute-start(bf16[128,768]{1,0:T(8,128)(2,1)S(1)} %get-tuple-element.182), channel_id=1, source_target_pairs={{0,1},{1,2},{2,3},{3,0},{4,5},{5,6},{6,7},{7,4},{8,9},{9,10},{10,1... | collective-permute-start | bytes 589832 | tf_op jit(solution)/shard_map/ppermute | solution.py:397
  158.3 19.2 %collective-permute-start.15 = (bf16[128,768]{1,0:T(8,128)(2,1)S(1)}, bf16[128,768]{1,0:T(8,128)(2,1)S(1)}, u32[]{:S(2)}, u32[]{:S(2)}) collective-permute-start(bf16[128,768]{1,0:T(8,128)(2,1)S(1)} %get-tuple-element.160), channel_id=1, source_target_pairs={{0,2},{1,3},{2,0},{3,1},{4,6},{5,7},{6,4},{7,5},{8,10},{9,11},{10,... | collective-permute-start | bytes 589832 | tf_op jit(solution)/shard_map/ppermute | solution.py:397
  159.9 17.7 %collective-permute-start.16 = (bf16[128,768]{1,0:T(8,128)(2,1)S(1)}, bf16[128,768]{1,0:T(8,128)(2,1)S(1)}, u32[]{:S(2)}, u32[]{:S(2)}) collective-permute-start(bf16[128,768]{1,0:T(8,128)(2,1)S(1)} %get-tuple-element.160), channel_id=1, source_target_pairs={{0,1},{1,2},{2,3},{3,0},{4,5},{5,6},{6,7},{7,4},{8,9},{9,10},{10,1... | collective-permute-start | bytes 589832 | tf_op jit(solution)/shard_map/ppermute | solution.py:397
  163.6 14.0 %collective-permute-start.17 = (bf16[768,768]{1,0:T(8,128)(2,1)S(1)}, bf16[768,768]{1,0:T(8,128)(2,1)S(1)}, u32[]{:S(2)}, u32[]{:S(2)}) collective-permute-start(bf16[768,768]{1,0:T(8,128)(2,1)S(1)} %get-tuple-element.204), channel_id=1, source_target_pairs={{0,16},{16,0},{1,17},{17,1},{2,18},{18,2},{3,19},{19,3},{4,20},{20... | collective-permute-start | bytes 3538952 | tf_op jit(solution)/shard_map/ppermute | solution.py:393
  180.7 62.9 %collective-permute-start.18 = (bf16[128,768]{1,0:T(8,128)(2,1)}, bf16[128,768]{1,0:T(8,128)(2,1)S(1)}, u32[]{:S(2)}, u32[]{:S(2)}) collective-permute-start(bf16[128,768]{1,0:T(8,128)(2,1)} %get-tuple-element.119), channel_id=1, source_target_pairs={{0,3},{1,0},{2,1},{3,2},{4,7},{5,4},{6,5},{7,6},{8,11},{9,8},{10,9... | collective-permute-start | bytes 589832 | tf_op jit(solution)/shard_map/ppermute | solution.py:397
  180.7 62.9 %collective-permute-start.19 = (bf16[128,768]{1,0:T(8,128)(2,1)}, bf16[128,768]{1,0:T(8,128)(2,1)S(1)}, u32[]{:S(2)}, u32[]{:S(2)}) collective-permute-start(bf16[128,768]{1,0:T(8,128)(2,1)} %get-tuple-element.120), channel_id=1, source_target_pairs={{0,2},{1,3},{2,0},{3,1},{4,6},{5,7},{6,4},{7,5},{8,10},{9,11},{10,... | collective-permute-start | bytes 589832 | tf_op jit(solution)/shard_map/ppermute | solution.py:397
  181.6 61.9 %collective-permute-start.20 = (bf16[128,768]{1,0:T(8,128)(2,1)}, bf16[128,768]{1,0:T(8,128)(2,1)S(1)}, u32[]{:S(2)}, u32[]{:S(2)}) collective-permute-start(bf16[128,768]{1,0:T(8,128)(2,1)} %get-tuple-element.121), channel_id=1, source_target_pairs={{0,1},{1,2},{2,3},{3,0},{4,5},{5,6},{6,7},{7,4},{8,9},{9,10},{10,1... | collective-permute-start | bytes 589832 | tf_op jit(solution)/shard_map/ppermute | solution.py:397
  260.5 23.1 %collective-permute-start.31 = (bf16[112,768]{1,0:T(8,128)(2,1)S(1)}, bf16[112,768]{1,0:T(8,128)(2,1)S(1)}, u32[]{:S(2)}, u32[]{:S(2)}) collective-permute-start(bf16[112,768]{1,0:T(8,128)(2,1)S(1)} %add_convert_fusion.4), channel_id=1, source_target_pairs={{0,12},{4,0},{8,4},{12,8},{1,13},{5,1},{9,5},{13,9},{2,14},{6,2},{... | collective-permute-start | bytes 516104 | tf_op jit(solution)/shard_map/ppermute | solution.py:459
  261.2 24.5 %collective-permute-start.32 = (bf16[112,768]{1,0:T(8,128)(2,1)S(1)}, bf16[112,768]{1,0:T(8,128)(2,1)S(1)}, u32[]{:S(2)}, u32[]{:S(2)}) collective-permute-start(bf16[112,768]{1,0:T(8,128)(2,1)S(1)} %add_convert_fusion.4), channel_id=1, source_target_pairs={{0,8},{4,12},{8,0},{12,4},{1,9},{5,13},{9,1},{13,5},{2,10},{6,14},... | collective-permute-start | bytes 516104 | tf_op jit(solution)/shard_map/ppermute | solution.py:459
  262.6 25.0 %collective-permute-start.33 = (bf16[112,768]{1,0:T(8,128)(2,1)S(1)}, bf16[112,768]{1,0:T(8,128)(2,1)S(1)}, u32[]{:S(2)}, u32[]{:S(2)}) collective-permute-start(bf16[112,768]{1,0:T(8,128)(2,1)S(1)} %add_convert_fusion.4), channel_id=1, source_target_pairs={{0,4},{4,8},{8,12},{12,0},{1,5},{5,9},{9,13},{13,1},{2,6},{6,10},{... | collective-permute-start | bytes 516104 | tf_op jit(solution)/shard_map/ppermute | solution.py:459
  268.6 21.2 %collective-permute-start.27 = (bf16[128,768]{1,0:T(8,128)(2,1)S(1)}, bf16[128,768]{1,0:T(8,128)(2,1)S(1)}, u32[]{:S(2)}, u32[]{:S(2)}) collective-permute-start(bf16[128,768]{1,0:T(8,128)(2,1)S(1)} %add_convert_fusion.3), channel_id=1, source_target_pairs={{0,3},{1,0},{2,1},{3,2},{4,7},{5,4},{6,5},{7,6},{8,11},{9,8},{10,9... | collective-permute-start | bytes 589832 | tf_op jit(solution)/shard_map/ppermute | solution.py:397
  283.5 16.0 %collective-permute-start.28 = (bf16[128,768]{1,0:T(8,128)(2,1)S(1)}, bf16[128,768]{1,0:T(8,128)(2,1)S(1)}, u32[]{:S(2)}, u32[]{:S(2)}) collective-permute-start(bf16[128,768]{1,0:T(8,128)(2,1)S(1)} %add_convert_fusion.3), channel_id=1, source_target_pairs={{0,2},{1,3},{2,0},{3,1},{4,6},{5,7},{6,4},{7,5},{8,10},{9,11},{10,... | collective-permute-start | bytes 589832 | tf_op jit(solution)/shard_map/ppermute | solution.py:397
  283.6 15.8 %collective-permute-start.29 = (bf16[128,768]{1,0:T(8,128)(2,1)S(1)}, bf16[128,768]{1,0:T(8,128)(2,1)S(1)}, u32[]{:S(2)}, u32[]{:S(2)}) collective-permute-start(bf16[128,768]{1,0:T(8,128)(2,1)S(1)} %add_convert_fusion.3), channel_id=1, source_target_pairs={{0,1},{1,2},{2,3},{3,0},{4,5},{5,6},{6,7},{7,4},{8,9},{9,10},{10,1... | collective-permute-start | bytes 589832 | tf_op jit(solution)/shard_map/ppermute | solution.py:397
  285.7 14.2 %collective-permute-start.36 = (bf16[4,16,768]{2,1,0:T(8,128)(2,1)S(1)}, bf16[4,16,768]{2,1,0:T(8,128)(2,1)S(1)}, u32[]{:S(2)}, u32[]{:S(2)}) collective-permute-start(bf16[4,16,768]{2,1,0:T(8,128)(2,1)S(1)} %get-tuple-element.196), channel_id=1, source_target_pairs={{4,0},{20,4},{0,8},{16,12},{12,16},{28,20},{8,24},{24,28},{5,1},{2... | collective-permute-start | bytes 294920 | tf_op jit(solution)/shard_map/ppermute | solution.py:1056
  (55 other events, 535.7 us)
Sparse Core Ops, SparseCore 0:
  179.3 51.9 all-reduce.1
